TPU v7x, 32 devices: a whole 2x2x4 slice. The times are simulated.
32 devices in a mesh: dp: 2 (over core), row: 4 (over z), col: 4 (over y, x).
Axes of the slice: x: 2, y: 2, z: 4, core: 2. Of those that a mesh axis runs over, the one named last changes fastest.
Arguments:
- inputs: bfloat16 [16, 1024, 1024], P(('dp', 'row'), None, 'col'), may hold values from -6 to 6
- out_grad: bfloat16 [16, 1024, 1024], P(('dp', 'row'), None, 'col'), may hold values from -6 to 6
- seq_lengths: int32 [16], P(('dp', 'row')), may hold values from 1 to 1024, 12288 in all
- first_gain: bfloat16 [1024], replicated, may hold values from 0.099609375 to 1.8984375
- query_proj: bfloat16 [1024, 1024], P('row', 'col'), may hold values from -0.1875 to 0.1875
- key_proj: bfloat16 [1024, 1024], P('row', 'col'), may hold values from -0.1875 to 0.1875
- value_proj: bfloat16 [1024, 2048], P('row', 'col'), may hold values from -0.1875 to 0.1875
- decay_proj: bfloat16 [1024, 8], P('row', 'col'), may hold values from -0.1875 to 0.1875
- beta_proj: bfloat16 [1024, 8], P('row', 'col'), may hold values from -0.1875 to 0.1875
- gate_proj: bfloat16 [1024, 2048], P('row', 'col'), may hold values from -0.1875 to 0.1875
- query_conv: bfloat16 [4, 1024], P(None, 'col'), may hold values from -3 to 3
- key_conv: bfloat16 [4, 1024], P(None, 'col'), may hold values from -3 to 3
- value_conv: bfloat16 [4, 2048], P(None, 'col'), may hold values from -3 to 3
- decay_log: float32 [8], P('col'), may hold values from 0 to 2.77
- step_bias: float32 [8], P('col'), may hold values from -6.9 to -2.3
- output_gain: bfloat16 [256], replicated, may hold values from 0.099609375 to 1.8984375
- output_proj: bfloat16 [2048, 1024], P('col', 'row'), may hold values from -0.25 to 0.25
- second_gain: bfloat16 [1024], replicated, may hold values from 0.099609375 to 1.8984375
- hidden_gate: bfloat16 [1024, 2816], P('row', 'col'), may hold values from -0.1875 to 0.1875
- hidden_up: bfloat16 [1024, 2816], P('row', 'col'), may hold values from -0.1875 to 0.1875
- hidden_down: bfloat16 [2816, 1024], P('col', 'row'), may hold values from -0.109375 to 0.109375
Outputs:
- result: bfloat16 [16, 1024, 1024], P(('dp', 'row'), None, 'col')
- input_grad: float32 [16, 1024, 1024], P(('dp', 'row'), None, 'col')
- first_gain_grad: float32 [1024], P('col')
- query_proj_grad: float32 [1024, 1024], P('row', 'col')
- key_proj_grad: float32 [1024, 1024], P('row', 'col')
- value_proj_grad: float32 [1024, 2048], P('row', 'col')
- decay_proj_grad: float32 [1024, 8], P('row', 'col')
- beta_proj_grad: float32 [1024, 8], P('row', 'col')
- gate_proj_grad: float32 [1024, 2048], P('row', 'col')
- query_conv_grad: float32 [4, 1024], P(None, 'col')
- key_conv_grad: float32 [4, 1024], P(None, 'col')
- value_conv_grad: float32 [4, 2048], P(None, 'col')
- decay_log_grad: float32 [8], P('col')
- step_bias_grad: float32 [8], P('col')
- output_gain_grad: float32 [256], replicated
- output_proj_grad: float32 [2048, 1024], P('col', 'row')
- second_gain_grad: float32 [1024], P('col')
- hidden_gate_grad: float32 [1024, 2816], P('row', 'col')
- hidden_up_grad: float32 [1024, 2816], P('row', 'col')
- hidden_down_grad: float32 [2816, 1024], P('col', 'row')
Inputs may be any that keep to these rules, and one draw needn't show every extreme that they name: `seq_lengths`: the valid tokens of a sequence come first, the rest is padding; the longest sequence has exactly 1024.
All inputs are finite; a program needn't handle non-finite values. No bound on the sum of `seq_lengths` on one device may be relied on, other than what follows from the above.
Results may differ from a plain program's by a relative error of at most 0.014.
Values may be sent and summed in bfloat16 or wider, within the bound.
No kernel may reach another device: no remote copies, remote signals or barrier semaphores. Data moves between devices by JAX's collectives and lax.ppermute only.
A program may use at most 320 MiB of HBM per device.

v0:
```python
import jax
import jax.numpy as jnp
from jax import lax
from jax.sharding import PartitionSpec as P

D = 1024
DK = 128
DV = 256
CONV = 4
SPAN = 64


HIGHEST = lax.Precision.HIGHEST
NORM_EPS = 1e-05
UNIT_EPS = 1e-06


def causal_conv(values, kernel):
    length = values.shape[1]
    padded = jnp.pad(values, ((0, 0), (CONV - 1, 0), (0, 0)))
    summed = padded[:, 0:length] * kernel[0]
    for offset in range(1, CONV):
        summed = summed + padded[:, offset : offset + length] * kernel[offset]
    return jax.nn.silu(summed)


def unit_rows(values):
    return values * lax.rsqrt(jnp.sum(values * values, axis=-1, keepdims=True) + UNIT_EPS)


def delta_rule(queries, key_vecs, val_vecs, log_decay, beta_vals):
    seq_count, length, head_count = log_decay.shape
    blocks = length // SPAN

    def split_blocks(values):
        shaped = values.reshape((seq_count, blocks, SPAN, head_count) + values.shape[3:])
        return jnp.swapaxes(shaped, 2, 3)

    query_blk = split_blocks(queries)
    key_blk = split_blocks(key_vecs)
    value_blk = split_blocks(val_vecs)
    beta_blk = split_blocks(beta_vals)
    cumulative = jnp.cumsum(split_blocks(log_decay), axis=-1)
    log_gap = cumulative[..., :, None] - cumulative[..., None, :]
    row_ids = lax.broadcasted_iota(jnp.int32, (SPAN, SPAN), 0)
    col_ids = lax.broadcasted_iota(jnp.int32, (SPAN, SPAN), 1)
    lower_strict = row_ids > col_ids
    lower_incl = row_ids >= col_ids
    strict_fac = jnp.where(lower_strict, jnp.exp(jnp.where(lower_strict, log_gap, 0.0)), 0.0)
    incl_fac = jnp.where(lower_incl, jnp.exp(jnp.where(lower_incl, log_gap, 0.0)), 0.0)
    key_gram = jnp.einsum("sbhik,sbhjk->sbhij", key_blk, key_blk, precision=HIGHEST)
    coupling = beta_blk[..., None] * key_gram * strict_fac
    system = coupling + jnp.eye(SPAN, dtype=coupling.dtype)
    decayed = jnp.exp(cumulative)[..., None]
    right_side = jnp.concatenate(
        [beta_blk[..., None] * value_blk, beta_blk[..., None] * decayed * key_blk], axis=-1
    )
    solved = jax.scipy.linalg.solve_triangular(system, right_side, lower=True, unit_diagonal=True)
    value_dim = value_blk.shape[-1]
    new_vals = solved[..., :value_dim]
    key_part = solved[..., value_dim:]
    scores = jnp.einsum("sbhik,sbhjk->sbhij", query_blk, key_blk, precision=HIGHEST) * incl_fac
    query_dec = query_blk * decayed
    key_dec = key_blk * jnp.exp(cumulative[..., -1:] - cumulative)[..., None]
    block_decay = jnp.exp(cumulative[..., -1])[..., None, None]
    stacked = tuple(
        (
            jnp.moveaxis(piece, 1, 0)
            for piece in (new_vals, key_part, query_dec, scores, key_dec, block_decay)
        )
    )

    def advance(carry_state, pieces):
        new_part, key_piece, query_piece, score_piece, keydec_piece, decay_piece = pieces
        updates = new_part - jnp.einsum(
            "shck,shkv->shcv", key_piece, carry_state, precision=HIGHEST
        )
        output = jnp.einsum("shck,shkv->shcv", query_piece, carry_state, precision=HIGHEST)
        output = output + jnp.einsum("shij,shjv->shiv", score_piece, updates, precision=HIGHEST)
        carry_state = decay_piece * carry_state + jnp.einsum(
            "shck,shcv->shkv", keydec_piece, updates, precision=HIGHEST
        )
        return (carry_state, output)

    initial = jnp.zeros((seq_count, head_count, key_blk.shape[-1], value_dim), queries.dtype)
    unused_state, outputs = lax.scan(advance, initial, stacked)
    return jnp.transpose(outputs, (1, 0, 3, 2, 4)).reshape(seq_count, length, head_count, value_dim)


def mixer(
    query_in,
    key_in,
    value_in,
    decay_in,
    beta_in,
    gate_in,
    query_conv,
    key_conv,
    value_conv,
    decay_log,
    step_bias,
    output_gain,
):
    seq_count, length = (query_in.shape[0], query_in.shape[1])
    head_count = decay_log.shape[0]
    queries = unit_rows(
        causal_conv(query_in, query_conv).reshape(seq_count, length, head_count, DK)
    ) * DK ** (-0.5)
    key_vecs = unit_rows(causal_conv(key_in, key_conv).reshape(seq_count, length, head_count, DK))
    val_vecs = causal_conv(value_in, value_conv).reshape(seq_count, length, head_count, DV)
    beta_vals = jax.nn.sigmoid(beta_in)
    log_decay = -jnp.exp(decay_log) * jax.nn.softplus(decay_in + step_bias)
    mixer_out = delta_rule(queries, key_vecs, val_vecs, log_decay, beta_vals)
    normed = mixer_out * lax.rsqrt(
        jnp.mean(mixer_out * mixer_out, axis=-1, keepdims=True) + NORM_EPS
    )
    normed = normed * output_gain * jax.nn.silu(gate_in.reshape(seq_count, length, head_count, DV))
    return normed.reshape(seq_count, length, head_count * DV)


def gather_features(values):
    return lax.all_gather(values, "col", axis=1, tiled=True)


def sum_features(values):
    return lax.psum_scatter(values, "col", scatter_dimension=1, tiled=True)


def contract_rows(left, right):
    return lax.dot_general(
        left, right, (((0,), (0,)), ((), ())), preferred_element_type=jnp.float32
    )


def contract_cols(left, right):
    return lax.dot_general(
        left, right, (((1,), (1,)), ((), ())), preferred_element_type=jnp.float32
    )


def out_weight_grad(left, right):
    return lax.psum_scatter(
        contract_rows(left, right).astype(jnp.bfloat16), "row", scatter_dimension=1, tiled=True
    ).astype(jnp.float32)


def in_weight_grad(normed, grads):
    return lax.psum_scatter(
        contract_rows(normed, grads).astype(jnp.bfloat16), "row", scatter_dimension=0, tiled=True
    ).astype(jnp.float32)


def split_columns(values, widths):
    pieces = []
    offset = 0
    for column_width in widths:
        pieces.append(values[:, offset : offset + column_width])
        offset = offset + column_width
    return pieces


def on_device(
    inputs,
    out_grad,
    seq_lengths,
    first_gain,
    query_proj,
    key_proj,
    value_proj,
    decay_proj,
    beta_proj,
    gate_proj,
    query_conv,
    key_conv,
    value_conv,
    decay_log,
    step_bias,
    output_gain,
    output_proj,
    second_gain,
    hidden_gate,
    hidden_up,
    hidden_down,
):
    seq_count, length, col_width = inputs.shape
    tokens = seq_count * length
    col_index = lax.axis_index("col")
    gathered = (
        lax.all_gather(query_proj, "row", axis=0, tiled=True),
        lax.all_gather(key_proj, "row", axis=0, tiled=True),
        lax.all_gather(value_proj, "row", axis=0, tiled=True),
        lax.all_gather(decay_proj, "row", axis=0, tiled=True),
        lax.all_gather(beta_proj, "row", axis=0, tiled=True),
        lax.all_gather(gate_proj, "row", axis=0, tiled=True),
        lax.all_gather(hidden_gate, "row", axis=0, tiled=True),
        lax.all_gather(hidden_up, "row", axis=0, tiled=True),
        lax.all_gather(output_proj, "row", axis=1, tiled=True),
        lax.all_gather(hidden_down, "row", axis=1, tiled=True),
    )
    widths = [piece.shape[1] for piece in gathered[0:6]]
    input_weights = jnp.concatenate(gathered[0:6], axis=1)
    feed_weights = jnp.concatenate(gathered[6:8], axis=1)
    out_rows = gathered[8]
    down_rows = gathered[9]
    positions = lax.broadcasted_iota(jnp.int32, (seq_count, length), 1)
    valid_mask = (positions < seq_lengths[:, None]).astype(jnp.float32).reshape(tokens, 1)
    local_low = inputs.reshape(tokens, col_width)
    local_rows = local_low.astype(jnp.float32)
    full_rows = gather_features(local_low).astype(jnp.float32)
    first_scale = lax.rsqrt(jnp.mean(full_rows * full_rows, axis=1, keepdims=True) + NORM_EPS)
    first_full = first_gain.astype(jnp.float32)
    first_local = lax.dynamic_slice_in_dim(first_full, col_index * col_width, col_width)
    normed_first = (full_rows * first_scale * first_full * valid_mask).astype(jnp.bfloat16)
    projected = jnp.dot(normed_first, input_weights, preferred_element_type=jnp.float32)
    pieces = split_columns(projected, widths)
    mixer_args = tuple((piece.reshape(seq_count, length, piece.shape[1]) for piece in pieces)) + (
        query_conv.astype(jnp.float32),
        key_conv.astype(jnp.float32),
        value_conv.astype(jnp.float32),
        decay_log,
        step_bias,
        output_gain.astype(jnp.float32),
    )
    mixer_out, mixer_back = jax.vjp(mixer, *mixer_args)
    mixed_low = mixer_out.reshape(tokens, -1).astype(jnp.bfloat16)
    attention = sum_features(jnp.dot(mixed_low, out_rows, preferred_element_type=jnp.float32))
    hidden_res = local_rows + attention
    second_full = second_gain.astype(jnp.float32)
    second_local = lax.dynamic_slice_in_dim(second_full, col_index * col_width, col_width)
    full_res = lax.all_gather(hidden_res, "col", axis=1, tiled=True)
    second_scale = lax.rsqrt(jnp.mean(full_res * full_res, axis=1, keepdims=True) + NORM_EPS)
    normed_second = (full_res * second_scale * second_full * valid_mask).astype(jnp.bfloat16)
    gate_up = jnp.dot(normed_second, feed_weights, preferred_element_type=jnp.float32)
    ff_half = gate_up.shape[1] // 2
    gate_act = gate_up[:, :ff_half]
    up_act = gate_up[:, ff_half:]
    sigmoid_gate = jax.nn.sigmoid(gate_act)
    silu_gate = gate_act * sigmoid_gate
    hidden_act = (silu_gate * up_act).astype(jnp.bfloat16)
    feed_out = sum_features(jnp.dot(hidden_act, down_rows, preferred_element_type=jnp.float32))
    result = (
        ((hidden_res + feed_out) * valid_mask)
        .astype(jnp.bfloat16)
        .reshape(seq_count, length, col_width)
    )
    grad_out = out_grad.reshape(tokens, col_width).astype(jnp.float32) * valid_mask
    feed_grad_full = gather_features(grad_out.astype(jnp.bfloat16))
    down_grad = out_weight_grad(hidden_act, feed_grad_full)
    inner_grad = contract_cols(feed_grad_full, down_rows)
    gate_grad = (
        inner_grad * up_act * sigmoid_gate * (1.0 + gate_act * (1.0 - sigmoid_gate))
    ).astype(jnp.bfloat16)
    up_grad = (inner_grad * silu_gate).astype(jnp.bfloat16)
    gate_up_grad = jnp.concatenate([gate_grad, up_grad], axis=1)
    feed_weight_grad = in_weight_grad(normed_second, gate_up_grad)
    second_grad = sum_features(contract_cols(gate_up_grad, feed_weights)) * valid_mask
    second_hat = hidden_res * second_scale
    second_scaled = second_grad * second_local
    second_gain_grad = jnp.sum(second_grad * second_hat, axis=0)
    second_dot = lax.psum(jnp.sum(second_scaled * second_hat, axis=1, keepdims=True), "col")
    hidden_grad = grad_out + second_scale * (second_scaled - second_hat * second_dot / D)
    attn_grad_full = gather_features(hidden_grad.astype(jnp.bfloat16))
    out_proj_grad = out_weight_grad(mixed_low, attn_grad_full)
    mixed_grad = contract_cols(attn_grad_full, out_rows).reshape(seq_count, length, -1)
    mixer_grads = mixer_back(mixed_grad)
    proj_grad = jnp.concatenate(
        [grad_piece.reshape(tokens, -1) for grad_piece in mixer_grads[0:6]], axis=1
    ).astype(jnp.bfloat16)
    input_weight_grad = in_weight_grad(normed_first, proj_grad)
    first_grad = sum_features(contract_cols(proj_grad, input_weights)) * valid_mask
    first_hat = local_rows * first_scale
    first_scaled = first_grad * first_local
    first_gain_grad = jnp.sum(first_grad * first_hat, axis=0)
    first_dot, gain_out_grad = lax.psum(
        (jnp.sum(first_scaled * first_hat, axis=1, keepdims=True), mixer_grads[11]), "col"
    )
    input_grad = hidden_grad + first_scale * (first_scaled - first_hat * first_dot / D)
    input_weight_grad, out_proj_grad, feed_weight_grad, down_grad = (
        lax.psum(input_weight_grad.astype(jnp.bfloat16), "dp").astype(jnp.float32),
        lax.psum(out_proj_grad.astype(jnp.bfloat16), "dp").astype(jnp.float32),
        lax.psum(feed_weight_grad.astype(jnp.bfloat16), "dp").astype(jnp.float32),
        lax.psum(down_grad.astype(jnp.bfloat16), "dp").astype(jnp.float32),
    )
    small_sums = lax.psum(
        (
            first_gain_grad,
            second_gain_grad,
            mixer_grads[6],
            mixer_grads[7],
            mixer_grads[8],
            mixer_grads[9],
            mixer_grads[10],
            gain_out_grad,
        ),
        ("dp", "row"),
    )
    proj_grads = split_columns(input_weight_grad, widths)
    return (
        result,
        input_grad.reshape(seq_count, length, col_width),
        small_sums[0],
        proj_grads[0],
        proj_grads[1],
        proj_grads[2],
        proj_grads[3],
        proj_grads[4],
        proj_grads[5],
        small_sums[2],
        small_sums[3],
        small_sums[4],
        small_sums[5],
        small_sums[6],
        small_sums[7],
        out_proj_grad,
        small_sums[1],
        feed_weight_grad[:, :ff_half],
        feed_weight_grad[:, ff_half:],
        down_grad,
    )


def solution(mesh):
    in_specs = (
        P(("dp", "row"), None, "col"),
        P(("dp", "row"), None, "col"),
        P(("dp", "row")),
        P(),
        P("row", "col"),
        P("row", "col"),
        P("row", "col"),
        P("row", "col"),
        P("row", "col"),
        P("row", "col"),
        P(None, "col"),
        P(None, "col"),
        P(None, "col"),
        P("col"),
        P("col"),
        P(),
        P("col", "row"),
        P(),
        P("row", "col"),
        P("row", "col"),
        P("col", "row"),
    )
    out_specs = (
        P(("dp", "row"), None, "col"),
        P(("dp", "row"), None, "col"),
        P("col"),
        P("row", "col"),
        P("row", "col"),
        P("row", "col"),
        P("row", "col"),
        P("row", "col"),
        P("row", "col"),
        P(None, "col"),
        P(None, "col"),
        P(None, "col"),
        P("col"),
        P("col"),
        P(),
        P("col", "row"),
        P("col"),
        P("row", "col"),
        P("row", "col"),
        P("col", "row"),
    )
    return jax.shard_map(
        on_device, mesh=mesh, in_specs=in_specs, out_specs=out_specs, check_vma=False
    )
```

profile of v0, /device:TPU:1, one launch (start us, length us, event | category | flops | bytes accessed | tf_op | source)
XLA Modules:
  0.0 2144.8 jit_solution(803768090531166199)
XLA Ops:
  10.9 17.8 all_gather.43
  28.7 20.1 all_gather.44
  49.0 11.6 all_gather.46
  60.8 13.9 all_gather.47
  75.1 10.4 all-gather.15.cloned.1.call-done
  92.2 47.8 %all-gather.11.cloned.1.call-done = bf16[2048,1024]{1,0:T(8,128)(2,1)} async-done(((bf16[2048,256]{1,0:T(8,128)(2,1)}), bf16[2048,1024]{1,0:T(8,128)(2,1)}) %all-gather.11.cloned.1.call-update) | async-done | bytes 4194320 | tf_op jit(solution)/shard_map/all_gather | solution.py:122
  192.6 316.0 %custom-call.10 = f32[2,16,2,1,64,64]{4,5,3,2,1,0:T(8,128)} custom-call(f32[2,16,2,1,64,64]{5,4,3,2,1,0:T(8,128)} %fusion.109), custom_call_target="InvertDiagBlocksLowerTriangular" | custom-call | tf_op jit(solution)/shard_map/jvp(jit(_solve_triangular))/vmap(vmap(vmap()))/triangular_solve | solution.py:58
  516.2 10.2 fusion.90
  591.3 131.3 %while.44 = (s32[]{:T(128)}, f32[2,2,128,256]{3,2,1,0:T(8,128)S(1)}, f32[16,2,2,64,256]{4,2,3,0,1:T(2,128)}, f32[16,2,2,128,256]{4,3,2,1,0:T(8,128)}, f32[16,2,2...) while((s32[]{:T(128)}, ...), condition=%wide.region_5.6_spmd.clone, body=%wide.region_4.5_spmd.clone.sunk | while | flops 353239040 | bytes 6295230 | solution.py:86
  755.4 85.1 %reduce-scatter.9.cloned.1.call-done = f32[2048,256]{1,0:T(8,128)} async-done(((f32[2048,1024]{1,0:T(8,128)}), f32[2048,256]{1,0:T(8,128)}) %reduce-scatter.9.cloned.1.call-update) | async-done | bytes 2097168 | tf_op jit(solution)/shard_map/reduce_scatter | solution.py:126
  846.3 30.0 %all-gather.21.cloned.1.call-done = bf16[1024,704]{0,1:T(8,128)(2,1)} async-done(((bf16[256,704]{0,1:T(8,128)(2,1)}), bf16[1024,704]{0,1:T(8,128)(2,1)}) %all-gather.21.cloned.1.call-update) | async-done | bytes 1441808 | tf_op jit(solution)/shard_map/all_gather | solution.py:195
  878.9 32.9 %all-gather.23.cloned.1.call-done = bf16[1024,704]{0,1:T(8,128)(2,1)} async-done(((bf16[256,704]{0,1:T(8,128)(2,1)}), bf16[1024,704]{0,1:T(8,128)(2,1)}) %all-gather.23.cloned.1.call-update) | async-done | bytes 1441808 | tf_op jit(solution)/shard_map/all_gather | solution.py:196
  914.4 86.5 %all-gather.19.cloned.1.call-done = f32[2048,1024]{1,0:T(8,128)} async-done(((f32[2048,256]{1,0:T(8,128)}), f32[2048,1024]{1,0:T(8,128)}) %all-gather.19.cloned.1.call-update) | async-done | bytes 8388624 | tf_op jit(solution)/shard_map/all_gather | solution.py:230
  1006.6 11.6 fusion.217
  1018.2 18.5 all-gather.25.cloned.1.call-done
  1036.7 54.6 %all-gather.27.cloned.1.call-done = bf16[2048,1024]{1,0:T(8,128)(2,1)} async-done(((bf16[2048,256]{1,0:T(8,128)(2,1)}), bf16[2048,1024]{1,0:T(8,128)(2,1)}) %all-gather.27.cloned.1.call-update) | async-done | bytes 4194320 | tf_op jit(solution)/shard_map/all_gather | solution.py:122
  1091.3 11.3 multiply_convert_fusion.2
  1123.1 77.5 %reduce-scatter.13.cloned.1.call-done = f32[2048,256]{1,0:T(8,128)} async-done(((f32[2048,1024]{1,0:T(8,128)}), f32[2048,256]{1,0:T(8,128)}) %reduce-scatter.13.cloned.1.call-update) | async-done | bytes 2097168 | tf_op jit(solution)/shard_map/reduce_scatter | solution.py:126
  1210.4 79.5 %reduce-scatter.11.cloned.1.call-done = f32[2048,256]{1,0:T(8,128)} async-done(((f32[2048,1024]{1,0:T(8,128)}), f32[2048,256]{1,0:T(8,128)}) %reduce-scatter.11.cloned.1.call-update) | async-done | bytes 2097168 | tf_op jit(solution)/shard_map/reduce_scatter | solution.py:126
  1310.2 14.0 convolution_convert_fusion
  1324.2 22.6 %all-gather.29.cloned.1.call-done = bf16[2048,1024]{1,0:T(8,128)(2,1)} async-done(((bf16[2048,256]{1,0:T(8,128)(2,1)}), bf16[2048,1024]{1,0:T(8,128)(2,1)}) %all-gather.29.cloned.1.call-update) | async-done | bytes 4194320 | tf_op jit(solution)/shard_map/all_gather | solution.py:122
  1382.2 13.5 fusion.86
  1411.5 282.5 %while.45 = (s32[]{:T(128)}, f32[2,2,128,256]{3,2,1,0:T(8,128)S(1)}, f32[16,2,2,64,256]{4,3,2,1,0:T(8,128)}, f32[16,2,2,64,128]{4,3,2,1,0:T(8,128)S(1)}, f32[16,...) while((s32[]{:T(128)}, ...), condition=%wide.region_16.17_spmd.clone, body=%wide.region_14.16_spmd.clone.sunk | while | flops 706019328 | bytes 9969441 | solution.py:86
  1702.7 12.2 fusion.72
  1771.2 11.1 multiply_reduce_fusion.3
  1877.5 27.9 %concatenate.20 = bf16[2048,1540]{0,1:T(8,128)(2,1)} concatenate(bf16[2048,256]{0,1:T(8,128)(2,1)} %copy.480, bf16[2048,256]{0,1:T(8,128)(2,1)S(1)} %copy.481, bf16[2048,512]{0,1:T(8,128)(2,1)} %copy.482, bf16[2048,2]{0,1:T(2,128)(2,1)S(1)} %fusion.200, bf16[2048,2]{0,1:T(2,128)(2,1)S(1)} %fusion.193, bf16[2048,512]{0,1:T(8,128)(2,1)S(1)} %copy-done.30), dimensions={1} | concatenate | bytes 12615680 | tf_op jit(solution)/shard_map/concatenate | solution.py:266
  1905.4 11.8 convolution_convert_fusion.1
  1917.4 60.6 %reduce-scatter.17.cloned.1.call-done = bf16[256,1540]{0,1:T(8,128)(2,1)} async-done(((bf16[1024,1540]{0,1:T(8,128)(2,1)}), bf16[256,1540]{0,1:T(8,128)(2,1)}) %reduce-scatter.17.cloned.1.call-update) | async-done | bytes 788496 | tf_op jit(solution)/shard_map/reduce_scatter | solution.py:148
  1978.1 12.0 fusion.236
  1991.1 11.4 all-reduce.36.cloned.1.call-done
  2012.2 80.9 %reduce-scatter.15.cloned.1.call-done = f32[2048,256]{1,0:T(8,128)} async-done(((f32[2048,1024]{1,0:T(8,128)}), f32[2048,256]{1,0:T(8,128)}) %reduce-scatter.15.cloned.1.call-update) | async-done | bytes 2097168 | tf_op jit(solution)/shard_map/reduce_scatter | solution.py:126
  2102.7 32.2 %all-reduce.31 = (f32[256]{0:T(256)}, f32[4,256]{1,0:T(4,128)}, f32[4,256]{1,0:T(4,128)}, f32[4,512]{1,0:T(4,128)}, f32[2]{0:T(128)}, /*index=5*/f32[2]{0:T(128)}, f32[256]{0:T(256)}, f32[256]{0:T(256)}) all-reduce(f32[256]{0:T(256)S(1)} %get-tuple-element.741, ...), channel_id=1, replica_groups=mesh['dp'=2,'row'=4,'col'=4] {'dp','row'}, use_global_device_ids=true, to_apply=%region_32.33 | all-reduce | flops 4868 | bytes 38944 | tf_op jit(solution)/shard_map/psum | solution.py:284
  (806 shorter events, 881.7 us)
Async XLA Ops:
  7.3 67.8 %all-gather.13.cloned.1.call-start = ((), (), s32[]{:S(2)}) async-start(), calls=%async_computation.9 | async-start | bytes 1310720 | tf_op jit(solution)/shard_map/all_gather | solution.py:191
  8.0 77.5 %all-gather.15.cloned.1.call-start = ((), (), s32[]{:S(2)}) async-start(), calls=%async_computation.10 | async-start | bytes 1310720 | tf_op jit(solution)/shard_map/all_gather | solution.py:194
  8.8 131.2 %all-gather.11.cloned.1.call-start = ((), (), s32[]{:S(2)}) async-start(), calls=%async_computation.8 | async-start | bytes 5242880 | tf_op jit(solution)/shard_map/all_gather | solution.py:122
  9.5 736.9 %all-gather.17.cloned.1.call-start = ((), (), s32[]{:S(2)}) async-start(), calls=%async_computation.11 | async-start | bytes 1310720 | tf_op jit(solution)/shard_map/all_gather | solution.py:197
  10.1 830.5 %reduce-scatter.9.cloned.1.call-start = ((), (), s32[]{:S(2)}) async-start(), calls=%async_computation.12 | async-start | bytes 10485760 | tf_op jit(solution)/shard_map/reduce_scatter | solution.py:126
  10.2 571.7 %copy-start.68 = (pred[64,64]{1,0:T(8,128)(4,1)}, pred[64,64]{1,0:T(8,128)(4,1)S(1)}, u32[]{:S(2)}) copy-start(pred[64,64]{1,0:T(8,128)(4,1)S(1)} %iota_compare_fusion) | copy-start | bytes 12292
  10.9 1299.2 %copy-start.59 = (f32[1,8,2,128]{3,1,2,0:T(8,128)}, f32[1,8,2,128]{3,1,2,0:T(8,128)S(1)}, u32[]{:S(2)}) copy-start(f32[1,8,2,128]{3,1,2,0:T(8,128)S(1)} %copy.661) | copy-start | bytes 24580
  74.9 441.3 %copy-start.80 = (f32[1,512]{1,0:T(1,128)}, f32[1,512]{1,0:T(1,128)S(1)}, u32[]{:S(2)}) copy-start(f32[1,512]{1,0:T(1,128)S(1)} %get-tuple-element.878) | copy-start | bytes 6148
  74.9 441.3 %copy-start.82 = (f32[1,512]{1,0:T(1,128)}, f32[1,512]{1,0:T(1,128)S(1)}, u32[]{:S(2)}) copy-start(f32[1,512]{1,0:T(1,128)S(1)} %get-tuple-element.879) | copy-start | bytes 6148
  74.9 441.3 %copy-start.84 = (f32[1,512]{1,0:T(1,128)}, f32[1,512]{1,0:T(1,128)S(1)}, u32[]{:S(2)}) copy-start(f32[1,512]{1,0:T(1,128)S(1)} %get-tuple-element.880) | copy-start | bytes 6148
  74.9 441.3 %copy-start.86 = (f32[1,512]{1,0:T(1,128)}, f32[1,512]{1,0:T(1,128)S(1)}, u32[]{:S(2)}) copy-start(f32[1,512]{1,0:T(1,128)S(1)} %get-tuple-element.881) | copy-start | bytes 6148
  75.0 475.2 %copy-start.89 = (f32[1,256]{1,0:T(1,128)}, f32[1,256]{1,0:T(1,128)S(1)}, u32[]{:S(2)}) copy-start(f32[1,256]{1,0:T(1,128)S(1)} %get-tuple-element.882) | copy-start | bytes 3076
  75.0 475.2 %copy-start.91 = (f32[1,256]{1,0:T(1,128)}, f32[1,256]{1,0:T(1,128)S(1)}, u32[]{:S(2)}) copy-start(f32[1,256]{1,0:T(1,128)S(1)} %get-tuple-element.883) | copy-start | bytes 3076
  75.0 475.2 %copy-start.93 = (f32[1,256]{1,0:T(1,128)}, f32[1,256]{1,0:T(1,128)S(1)}, u32[]{:S(2)}) copy-start(f32[1,256]{1,0:T(1,128)S(1)} %get-tuple-element.884) | copy-start | bytes 3076
  75.0 475.2 %copy-start.95 = (f32[1,256]{1,0:T(1,128)}, f32[1,256]{1,0:T(1,128)S(1)}, u32[]{:S(2)}) copy-start(f32[1,256]{1,0:T(1,128)S(1)} %get-tuple-element.885) | copy-start | bytes 3076
  171.2 410.7 %copy-start = (f32[2,16,64,2,128]{4,3,2,1,0:T(2,128)}, f32[2,16,64,2,128]{4,3,2,1,0:T(2,128)S(1)}, u32[]{:S(2)}) copy-start(f32[2,16,64,2,128]{4,3,2,1,0:T(2,128)S(1)} %reshape.417) | copy-start | bytes 6291460
  182.5 399.4 %copy-start.43 = (f32[2,16,64,2]{2,3,1,0:T(2,128)}, f32[2,16,64,2]{2,3,1,0:T(2,128)S(1)}, u32[]{:S(2)}) copy-start(f32[2,16,64,2]{2,3,1,0:T(2,128)S(1)} %copy.377) | copy-start | bytes 49156
  184.2 391.3 %copy-start.37 = (f32[2,16,2,64]{3,1,2,0:T(8,128)}, f32[2,16,2,64]{3,1,2,0:T(8,128)S(1)}, u32[]{:S(2)}) copy-start(f32[2,16,2,64]{3,1,2,0:T(8,128)S(1)} %reduce_window_sum.24) | copy-start | bytes 49156
  754.0 122.3 %all-gather.21.cloned.1.call-start = ((), (), s32[]{:S(2)}) async-start(), calls=%async_computation.14 | async-start | bytes 1802240 | tf_op jit(solution)/shard_map/all_gather | solution.py:195
  754.6 157.2 %all-gather.23.cloned.1.call-start = ((), (), s32[]{:S(2)}) async-start(), calls=%async_computation.15 | async-start | bytes 1802240 | tf_op jit(solution)/shard_map/all_gather | solution.py:196
  755.4 245.5 %all-gather.19.cloned.1.call-start = ((), (), s32[]{:S(2)}) async-start(), calls=%async_computation.13 | async-start | bytes 10485760 | tf_op jit(solution)/shard_map/all_gather | solution.py:230
  843.7 193.0 %all-gather.25.cloned.1.call-start = ((), (), s32[]{:S(2)}) async-start(), calls=%async_computation.16 | async-start | bytes 1802240 | tf_op jit(solution)/shard_map/all_gather | solution.py:198
  844.5 246.9 %all-gather.27.cloned.1.call-start = ((), (), s32[]{:S(2)}) async-start(), calls=%async_computation.18 | async-start | bytes 5242880 | tf_op jit(solution)/shard_map/all_gather | solution.py:122
  846.2 354.4 %reduce-scatter.13.cloned.1.call-start = ((), (), s32[]{:S(2)}) async-start(), calls=%async_computation.19 | async-start | bytes 10485760 | tf_op jit(solution)/shard_map/reduce_scatter | solution.py:126
  1114.1 175.9 %reduce-scatter.11.cloned.1.call-start = ((), (), s32[]{:S(2)}) async-start(), calls=%async_computation.17 | async-start | bytes 10485760 | tf_op jit(solution)/shard_map/reduce_scatter | solution.py:126
  1123.0 223.8 %all-gather.29.cloned.1.call-start = ((), (), s32[]{:S(2)}) async-start(), calls=%async_computation.20 | async-start | bytes 5242880 | tf_op jit(solution)/shard_map/all_gather | solution.py:122
  1294.1 623.3 %reduce-scatter.23.cloned.1.call-start = ((), (), s32[]{:S(2)}) async-start(), calls=%async_computation.25 | async-start | bytes 1802240 | tf_op jit(solution)/shard_map/reduce_scatter | solution.py:142
  1301.6 615.7 %reduce-scatter.21.cloned.1.call-start = ((), (), s32[]{:S(2)}) async-start(), calls=%async_computation.24 | async-start | bytes 3604480 | tf_op jit(solution)/shard_map/reduce_scatter | solution.py:148
  1324.2 593.2 %reduce-scatter.19.cloned.1.call-start = ((), (), s32[]{:S(2)}) async-start(), calls=%async_computation.23 | async-start | bytes 1310720 | tf_op jit(solution)/shard_map/reduce_scatter | solution.py:142
  1877.4 100.6 %reduce-scatter.17.cloned.1.call-start = ((), (), s32[]{:S(2)}) async-start(), calls=%async_computation.22 | async-start | bytes 3952640 | tf_op jit(solution)/shard_map/reduce_scatter | solution.py:148
  1917.3 85.2 %all-reduce.36.cloned.1.call-start = ((), (), s32[]{:S(2)}) async-start(), calls=%async_computation.26 | async-start | bytes 4268032 | tf_op jit(solution)/shard_map/psum | solution.py:279
  1978.0 115.0 %reduce-scatter.15.cloned.1.call-start = ((), (), s32[]{:S(2)}) async-start(), calls=%async_computation.21 | async-start | bytes 10485760 | tf_op jit(solution)/shard_map/reduce_scatter | solution.py:126
  (116 other events, 2756.3 us)
Sparse Core Ops, SparseCore 0:
  9.7 41.9 all-gather.12
  53.2 32.2 all-gather.14
  87.4 52.5 all-gather.10
  141.4 28.8 all-gather.16
  754.2 86.3 reduce-scatter.8
  842.0 34.2 all-gather.20
  877.9 33.7 all-gather.22
  913.7 87.0 all-gather.18
  1002.5 34.2 all-gather.24
  1039.1 52.1 all-gather.26
  1114.2 86.3 reduce-scatter.12
  1203.5 86.3 reduce-scatter.10
  1294.2 52.5 all-gather.28
  1349.1 33.0 reduce-scatter.22
  1384.5 55.0 reduce-scatter.20
  1877.5 27.0 reduce-scatter.18
  1917.4 60.5 reduce-scatter.16
  1980.4 22.0 all-reduce.35
  2005.9 87.1 reduce-scatter.14
where the time goes:
time: 2160 us; the launch traced here: 2140 us
  waiting for transfers between devices  703 us (33%)
  matrix products  523 us (24%)
  other arithmetic  512 us (24%)
  local copies, waits for them, and re-layouts  279 us (13%)
  blocking collectives  110 us (5%)
    reduce_scatter x4, waiting for transfers between devices, sum_features(): return lax.psum_scatter(values, 'col', scatter_dimension=1, tiled=True)  323 us
    another operation x3, other arithmetic, delta_rule(): jax.scipy.linalg.solve_triangular(system, right_side, lower=True, unit_di...  318 us
    all_gather x3, waiting for transfers between devices, gather_features(): return lax.all_gather(values, 'col', axis=1, tiled=True)  125 us
    dot_general x48, matrix products, advance(): jnp.einsum('shck,shkv->shcv', key_piece, carry_state, precision=HIGHEST)  86.5 us
    all_gather x1, waiting for transfers between devices, on_device(): full_res = lax.all_gather(hidden_res, 'col', axis=1, tiled=True)  86.5 us
    dot_general x48, matrix products, advance(): jnp.einsum('shij,shjv->shiv', score_piece, updates, precision=HIGHEST)  84.7 us
    dot_general x48, matrix products, advance(): jnp.einsum('shck,shkv->shcv', query_piece, carry_state, precision=HIGHEST)  83.7 us
    dot_general x48, matrix products, advance(): jnp.einsum('shck,shcv->shkv', keydec_piece, updates, precision=HIGHEST)  83.3 us
  transfers between devices with their start and end apart: 19, of which 14 were waited for; matrix products, arithmetic and copies ran while one was open for 58% of the time, Pallas kernels for 0%

commit v1 on v0

v1 whole, which is shorter than its diff:
```python
import functools
import jax
import jax.numpy as jnp
from jax import lax
from jax.experimental import pallas as pl
from jax.experimental.pallas import tpu as pltpu
from jax.sharding import PartitionSpec as P

DK = 128
DV = 256
CONV = 4
NORM_EPS = 1e-05
UNIT_EPS = 1e-06
BLK = 128
SUB = 32
F32 = jnp.float32
BF16 = jnp.bfloat16


def mm(a, b):
    return lax.dot_general(a, b, (((1,), (0,)), ((), ())), preferred_element_type=F32)


def mm_nt(a, b):
    return lax.dot_general(a, b, (((1,), (1,)), ((), ())), preferred_element_type=F32)


def halves(a):
    hi = a.astype(BF16)
    return hi, (a - hi.astype(F32)).astype(BF16)


def mm3(a, b):
    ah, al = halves(a)
    bh, bl = halves(b)
    return mm(ah, bh) + (mm(ah, bl) + mm(al, bh))


def sigm(v):
    return 1.0 / (1.0 + jnp.exp(-v))


def iota2(shape, axis):
    return lax.broadcasted_iota(jnp.int32, shape, axis)


def unit_lower_inverse(mats):
    groups = BLK // SUB
    lane = iota2((SUB, BLK), 1)
    sub = iota2((SUB, BLK), 0)
    lane_group = lane // SUB
    solved = []
    for b in range(groups):
        rows = slice(b * SUB, (b + 1) * SUB)
        packed = jnp.zeros((SUB, BLK), F32)
        for p, mat in enumerate(mats):
            piece = mat[rows]
            shift = (SUB * (p - b)) % BLK
            if shift:
                piece = pltpu.roll(piece, shift, 1)
            packed = jnp.where(lane_group == p, piece, packed)
        acc = jnp.where(lane - lane_group * SUB == sub, 1.0, 0.0).astype(F32)
        tiles = [acc[8 * t : 8 * t + 8] for t in range(SUB // 8)]
        coefs = [packed[8 * t : 8 * t + 8] for t in range(SUB // 8)]
        base = (iota2((8, BLK), 1) // SUB) * SUB
        for j in range(SUB - 1):
            row = jnp.broadcast_to(tiles[j // 8][j % 8 : j % 8 + 1], (8, BLK))
            for t in range((j + 1) // 8, SUB // 8):
                col = jnp.take_along_axis(coefs[t], base + j, axis=1)
                tiles[t] = tiles[t] - col * row
        solved.append(jnp.concatenate(tiles, axis=0))
    out = []
    row_i = iota2((BLK, BLK), 0)
    col_i = iota2((BLK, BLK), 1)
    for p, mat in enumerate(mats):
        blocks = []
        for b in range(groups):
            piece = solved[b]
            shift = (SUB * (b - p)) % BLK
            if shift:
                piece = pltpu.roll(piece, shift, 1)
            blocks.append(jnp.where(lane_group == b, piece, 0.0))
        inv = jnp.concatenate(blocks, axis=0)
        zero32 = jnp.zeros((SUB, BLK), F32)
        off = jnp.where((row_i // 64 == col_i // 64) & (row_i // SUB > col_i // SUB), mat, 0.0)
        lhs = jnp.concatenate([off[32:64], off[96:128]], axis=0)
        part = mm3(lhs, inv)
        placed = jnp.concatenate([zero32, part[:32], zero32, part[32:]], axis=0)
        lhs = jnp.concatenate([inv[32:64], inv[96:128]], axis=0)
        part = mm3(lhs, placed)
        inv = inv - jnp.concatenate([zero32, part[:32], zero32, part[32:]], axis=0)
        off = jnp.where(col_i[64:] < 64, mat[64:], 0.0)
        part = mm3(off, inv)
        zero64 = jnp.zeros((64, BLK), F32)
        part = mm3(inv[64:], jnp.concatenate([zero64, part], axis=0))
        inv = jnp.concatenate([inv[:64], inv[64:] - part], axis=0)
        out.append(inv)
    return out


def decay_terms(ab, neg_rate, bias, heads):
    pre = ab + bias
    soft = jnp.maximum(pre, 0.0) + jnp.log(1.0 + jnp.exp(-jnp.abs(pre)))
    log_decay = neg_rate * soft
    beta = sigm(ab)
    row_i = iota2((BLK, BLK), 0)
    col_i = iota2((BLK, BLK), 1)
    tri = jnp.where(row_i >= col_i, 1.0, 0.0).astype(BF16)
    hi = log_decay.astype(BF16)
    rest = log_decay - hi.astype(F32)
    mid = rest.astype(BF16)
    low = (rest - mid.astype(F32)).astype(BF16)
    cum = mm(tri, hi) + (mm(tri, mid) + mm(tri, low))
    return log_decay, beta, cum


def conv_taps(xs_ref, s, kernel):
    pre = xs_ref[s, 5 : 5 + BLK, :] * kernel[0:1]
    for i in range(1, CONV):
        pre = pre + xs_ref[s, 5 + i : 5 + i + BLK, :] * kernel[i : i + 1]
    return pre


def fwd_kernel(heads, nseq, proj_ref, conv_ref, rate_ref, gain_ref,
               mixed_ref, o_ref, u_ref, s_ref, t_ref, xs_ref, state_ref):
    qkv = heads * (2 * DK + DV)
    gate_at = qkv
    ab_at = qkv + heads * DV
    step = pl.program_id(1)

    @pl.when(step == 0)
    def _():
        xs_ref[:, 0:8, :] = jnp.zeros((nseq, 8, qkv), F32)
        state_ref[...] = jnp.zeros_like(state_ref)

    row_i = iota2((BLK, BLK), 0)
    col_i = iota2((BLK, BLK), 1)
    kernel = conv_ref[...]
    neg_rate = rate_ref[0:1]
    bias = rate_ref[1:2]
    gain = gain_ref[...]
    items = []
    for s in range(nseq):
        xs_ref[s, 8 : 8 + BLK, :] = proj_ref[s, :, 0:qkv]
        pre = conv_taps(xs_ref, s, kernel)
        xs_ref[s, 0:8, :] = xs_ref[s, BLK : BLK + 8, :]
        act = pre * sigm(pre)
        ab = proj_ref[s, :, ab_at : ab_at + 128]
        _, beta_all, cum_all = decay_terms(ab, neg_rate, bias, heads)
        cum_t = cum_all.T
        for h in range(heads):
            q = act[:, h * DK : (h + 1) * DK]
            k = act[:, (heads + h) * DK : (heads + h + 1) * DK]
            v = act[:, 2 * heads * DK + h * DV : 2 * heads * DK + (h + 1) * DV]
            qn = q * (lax.rsqrt(jnp.sum(q * q, axis=1, keepdims=True) + UNIT_EPS) * DK ** -0.5)
            kn = k * lax.rsqrt(jnp.sum(k * k, axis=1, keepdims=True) + UNIT_EPS)
            cum = cum_all[:, h : h + 1]
            cum_row = cum_t[h : h + 1, :]
            beta = beta_all[:, heads + h : heads + h + 1]
            ratio = jnp.exp(jnp.where(row_i >= col_i, cum - cum_row, -1e30))
            kb = kn.astype(BF16)
            kq = jnp.concatenate([kb, qn.astype(BF16)], axis=0)
            gram = mm_nt(kq, kb)
            a = jnp.where(row_i > col_i, gram[:BLK] * ratio * beta, 0.0)
            p = gram[BLK:] * ratio
            last = cum[BLK - 1 : BLK]
            kd = kn * jnp.exp(last - cum)
            items.append((s, h, kq, a, p, kd, v, beta, jnp.exp(cum), jnp.exp(last)))
    invs = []
    for at in range(0, len(items), 4):
        invs = invs + unit_lower_inverse([item[3] for item in items[at : at + 4]])
    for item, inv in zip(items, invs):
        s, h, kq, a, p, kd, v, beta, ecum, elast = item
        state = state_ref[s, h]
        low_state = state.astype(BF16)
        ks_qs = mm(kq, low_state)
        x = beta * (v - ecum * ks_qs[:BLK])
        inv_low = inv.astype(BF16)
        u = mm(inv_low, x.astype(BF16)).astype(BF16)
        pk = jnp.concatenate([p, kd.T], axis=0).astype(BF16)
        pu = mm(pk, u)
        o = ecum * ks_qs[BLK:] + pu[:BLK]
        state_ref[s, h] = elast * state + pu[BLK:]
        s_ref[s, 0, h] = low_state
        t_ref[s, 0, h] = inv_low
        cols = slice(h * DV, (h + 1) * DV)
        u_ref[s, :, cols] = u
        o_ref[s, :, cols] = o
        g = proj_ref[s, :, gate_at + h * DV : gate_at + (h + 1) * DV]
        norm = o * lax.rsqrt(jnp.mean(o * o, axis=1, keepdims=True) + NORM_EPS)
        mixed_ref[s, :, cols] = (norm * gain * (g * sigm(g))).astype(BF16)


def rate_rows(decay_log, step_bias):
    heads = decay_log.shape[0]
    pad = 128 - heads
    return jnp.stack([jnp.pad(-jnp.exp(decay_log), (0, pad)), jnp.pad(step_bias, (0, pad))])


def mixer_fwd(proj, conv, rates, gain, heads, nseq):
    seqs, length, width = proj.shape
    blocks = length // BLK
    qkv = heads * (2 * DK + DV)
    vals = heads * DV
    tok = lambda i, c: (i, c, 0)
    return pl.pallas_call(
        functools.partial(fwd_kernel, heads, nseq),
        out_shape=(
            jax.ShapeDtypeStruct((seqs, length, vals), BF16),
            jax.ShapeDtypeStruct((seqs, length, vals), F32),
            jax.ShapeDtypeStruct((seqs, length, vals), BF16),
            jax.ShapeDtypeStruct((seqs, blocks, heads, DK, DV), BF16),
            jax.ShapeDtypeStruct((seqs, blocks, heads, BLK, BLK), BF16),
        ),
        grid=(seqs // nseq, blocks),
        in_specs=[
            pl.BlockSpec((nseq, BLK, width), tok),
            pl.BlockSpec((CONV, qkv), lambda i, c: (0, 0)),
            pl.BlockSpec((2, 128), lambda i, c: (0, 0)),
            pl.BlockSpec((1, DV), lambda i, c: (0, 0)),
        ],
        out_specs=(
            pl.BlockSpec((nseq, BLK, vals), tok),
            pl.BlockSpec((nseq, BLK, vals), tok),
            pl.BlockSpec((nseq, BLK, vals), tok),
            pl.BlockSpec((nseq, 1, heads, DK, DV), lambda i, c: (i, c, 0, 0, 0)),
            pl.BlockSpec((nseq, 1, heads, BLK, BLK), lambda i, c: (i, c, 0, 0, 0)),
        ),
        scratch_shapes=[
            pltpu.VMEM((nseq, 8 + BLK, qkv), F32),
            pltpu.VMEM((nseq, heads, DK, DV), F32),
        ],
        compiler_params=pltpu.CompilerParams(dimension_semantics=("arbitrary", "arbitrary")),
        name="mixer_fwd",
    )(proj, conv, rates, gain)


def colsum(v):
    return jnp.sum(v.reshape(v.shape[0] // 8, 8, v.shape[1]), axis=0)


def bwd_kernel(heads, nseq, proj_ref, prev_ref, dmix_ref, o_ref, u_ref, s_ref, t_ref,
               conv_ref, rate_ref, gain_ref,
               dproj_ref, dots_ref, dconv_ref, drate_ref, dgain_ref, xs_ref, ds_ref, dstate_ref):
    qkv = heads * (2 * DK + DV)
    gate_at = qkv
    ab_at = qkv + heads * DV
    step = pl.program_id(1)
    first = pl.num_programs(1) - 1

    @pl.when(step == 0)
    def _():
        ds_ref[:, BLK : BLK + 8, :] = jnp.zeros((nseq, 8, qkv), F32)
        dstate_ref[...] = jnp.zeros_like(dstate_ref)

    @pl.when((step == 0) & (pl.program_id(0) == 0))
    def _():
        dconv_ref[...] = jnp.zeros_like(dconv_ref)
        drate_ref[...] = jnp.zeros_like(drate_ref)
        dgain_ref[...] = jnp.zeros_like(dgain_ref)

    row_i = iota2((BLK, BLK), 0)
    col_i = iota2((BLK, BLK), 1)
    lower = row_i >= col_i
    strict = row_i > col_i
    kernel = conv_ref[...]
    neg_rate = rate_ref[0:1]
    bias = rate_ref[1:2]
    gain = gain_ref[...]
    has_prev = jnp.where(step == first, 0.0, 1.0).astype(F32)
    lane1 = iota2((1, 128), 1)
    for s in range(nseq):
        xs_ref[s, 0:8, :] = prev_ref[s, :, 0:qkv] * has_prev
        xs_ref[s, 8 : 8 + BLK, :] = proj_ref[s, :, 0:qkv]
        pre = conv_taps(xs_ref, s, kernel)
        sig = sigm(pre)
        act = pre * sig
        dsilu = sig * (1.0 + pre * (1.0 - sig))
        ab = proj_ref[s, :, ab_at : ab_at + 128]
        log_decay, beta_all, cum_all = decay_terms(ab, neg_rate, bias, heads)
        cum_t = cum_all.T
        dots = jnp.zeros((BLK, 1), F32)
        dcum_all = jnp.zeros((BLK, 128), F32)
        dbeta_all = jnp.zeros((BLK, 128), F32)
        dact = [None] * (3 * heads)
        for h in range(heads):
            q = act[:, h * DK : (h + 1) * DK]
            k = act[:, (heads + h) * DK : (heads + h + 1) * DK]
            v = act[:, 2 * heads * DK + h * DV : 2 * heads * DK + (h + 1) * DV]
            rq = lax.rsqrt(jnp.sum(q * q, axis=1, keepdims=True) + UNIT_EPS)
            rk = lax.rsqrt(jnp.sum(k * k, axis=1, keepdims=True) + UNIT_EPS)
            qh = q * rq
            qn = qh * DK ** -0.5
            kn = k * rk
            cum = cum_all[:, h : h + 1]
            cum_row = cum_t[h : h + 1, :]
            beta = beta_all[:, heads + h : heads + h + 1]
            ecum = jnp.exp(cum)
            last = cum[BLK - 1 : BLK]
            elast = jnp.exp(last)
            ratio = jnp.exp(jnp.where(lower, cum - cum_row, -1e30))
            ktail = jnp.exp(last - cum)
            kb = kn.astype(BF16)
            qb = qn.astype(BF16)
            gram = mm_nt(jnp.concatenate([kb, qb], axis=0), kb)
            sfac = jnp.where(strict, ratio * beta, 0.0)
            kgr = gram[:BLK]
            p = gram[BLK:] * ratio
            cols = slice(h * DV, (h + 1) * DV)
            o = o_ref[s, :, cols]
            g = proj_ref[s, :, gate_at + h * DV : gate_at + (h + 1) * DV]
            dm = dmix_ref[s, :, cols].astype(F32)
            ro = lax.rsqrt(jnp.mean(o * o, axis=1, keepdims=True) + NORM_EPS)
            n = o * ro
            gs = sigm(g)
            gsil = g * gs
            dmn = dm * n
            dgain_ref[...] += colsum(dmn * gsil)
            dgate = dmn * gain * (gs * (1.0 + g * (1.0 - gs)))
            dproj_ref[s, :, gate_at + h * DV : gate_at + (h + 1) * DV] = dgate.astype(BF16)
            dots = dots + jnp.sum(dgate * g, axis=1, keepdims=True)
            dn = dm * gain * gsil
            do = ro * (dn - n * jnp.mean(dn * n, axis=1, keepdims=True))
            dob = do.astype(BF16)
            dstate = dstate_ref[s, h]
            dstb = dstate.astype(BF16)
            u = u_ref[s, :, cols]
            sb = s_ref[s, 0, h]
            tinv = t_ref[s, 0, h]
            kd = kn * ktail
            du = mm(jnp.concatenate([p.T, kd], axis=1).astype(BF16), jnp.concatenate([dob, dstb], axis=0))
            dx = mm(tinv.astype(F32).T.astype(BF16), du.astype(BF16))
            dxb = dx.astype(BF16)
            ddx = jnp.concatenate([dob, dxb], axis=0)
            both = mm_nt(ddx, jnp.concatenate([sb, u], axis=0))
            be = beta * ecum
            z = both[BLK:, :DK]
            dqi = ecum * both[:BLK, :DK]
            dki = -be * z
            dks = -be * dx
            lhs = jnp.concatenate([qn.T, kn.T], axis=1).astype(BF16)
            rhs = jnp.concatenate([(ecum * do).astype(BF16), dks.astype(BF16)], axis=0)
            dstate_ref[s, h] = elast * dstate + mm(lhs, rhs)
            dkd = mm_nt(u, dstb)
            dp = both[:BLK, DK:]
            da = -both[BLK:, DK:]
            dqk = dp * ratio
            dkg = da * sfac
            dlog = dp * p + dkg * kgr
            pair = jnp.concatenate([dqk, dkg + dkg.T], axis=0).astype(BF16)
            prod = mm(pair, kb)
            dqn = dqi + prod[:BLK]
            dkn = dki + prod[BLK:] + mm(dqk.T.astype(BF16), qb) + dkd * ktail
            kz = jnp.sum(kn * z, axis=1, keepdims=True)
            dkdk = jnp.sum(dkd * kd, axis=1, keepdims=True)
            row_sum = jnp.sum(dlog, axis=1, keepdims=True)
            col_sum = jnp.sum(dlog.T, axis=1, keepdims=True)
            dcum = row_sum - col_sum + jnp.sum(qn * dqi, axis=1, keepdims=True) - be * kz - dkdk
            tail = jnp.sum(dkdk, axis=0, keepdims=True) + elast * jnp.sum(
                jnp.sum(sb.astype(F32) * dstate, axis=1, keepdims=True), axis=0, keepdims=True)
            dcum = dcum + jnp.where(row_i[:, 0:1] == BLK - 1, tail, 0.0)
            kgl = jnp.sum(da * jnp.where(strict, ratio * kgr, 0.0), axis=1, keepdims=True)
            dbeta = jnp.sum(dx * v, axis=1, keepdims=True) - ecum * kz + kgl
            dcum_all = jnp.where(lane1 == h, dcum, dcum_all)
            dbeta_all = jnp.where(lane1 == heads + h, dbeta, dbeta_all)
            dact[h] = (DK ** -0.5 * rq) * (dqn - qh * jnp.sum(dqn * qh, axis=1, keepdims=True))
            dact[heads + h] = rk * (dkn - kn * jnp.sum(dkn * kn, axis=1, keepdims=True))
            dact[2 * heads + h] = beta * dx
        tri = jnp.where(col_i >= row_i, 1.0, 0.0).astype(BF16)
        hi, lo = halves(dcum_all)
        dlog_decay = mm(tri, hi) + mm(tri, lo)
        dpre_a = dlog_decay * neg_rate * sigm(ab + bias)
        dpre_b = dbeta_all * beta_all * (1.0 - beta_all)
        dproj_ref[s, :, ab_at : ab_at + 128] = (dpre_a + dpre_b).astype(BF16)
        dots = dots + jnp.sum((dpre_a + dpre_b) * ab, axis=1, keepdims=True)
        drate_ref[0:8, :] += colsum(dlog_decay * log_decay)
        drate_ref[8:16, :] += colsum(dpre_a)
        dpre = jnp.concatenate(dact, axis=1) * dsilu
        ds_ref[s, 0:BLK, :] = dpre
        dx_in = ds_ref[s, 3 : 3 + BLK, :] * kernel[0:1]
        for i in range(1, CONV):
            dx_in = dx_in + ds_ref[s, 3 - i : 3 - i + BLK, :] * kernel[i : i + 1]
        dproj_ref[s, :, 0:qkv] = dx_in.astype(BF16)
        dots = dots + jnp.sum(dx_in * xs_ref[s, 8 : 8 + BLK, :], axis=1, keepdims=True)
        dots_ref[s, 0] = jnp.broadcast_to(dots, (BLK, 128)).T[0:8]
        for i in range(CONV):
            dconv_ref[8 * i : 8 * i + 8, :] += colsum(dpre * xs_ref[s, 5 + i : 5 + i + BLK, :])
        ds_ref[s, BLK : BLK + 8, :] = ds_ref[s, 0:8, :]


def mixer_bwd(proj, dmixed, saved, conv, rates, gain, heads, nseq):
    o, u, states, invs = saved
    seqs, length, width = proj.shape
    blocks = length // BLK
    qkv = heads * (2 * DK + DV)
    vals = heads * DV
    tok = lambda i, c: (i, blocks - 1 - c, 0)
    whole = lambda i, c: (0, 0)
    dproj, dots, dconv, drate, dgain = pl.pallas_call(
        functools.partial(bwd_kernel, heads, nseq),
        out_shape=(
            jax.ShapeDtypeStruct((seqs, length, width), BF16),
            jax.ShapeDtypeStruct((seqs, blocks, 8, 128), F32),
            jax.ShapeDtypeStruct((8 * CONV, qkv), F32),
            jax.ShapeDtypeStruct((16, 128), F32),
            jax.ShapeDtypeStruct((8, DV), F32),
        ),
        grid=(seqs // nseq, blocks),
        in_specs=[
            pl.BlockSpec((nseq, BLK, width), tok),
            pl.BlockSpec((nseq, 8, qkv), lambda i, c: (i, jnp.maximum((blocks - 1 - c) * (BLK // 8) - 1, 0), 0)),
            pl.BlockSpec((nseq, BLK, vals), tok),
            pl.BlockSpec((nseq, BLK, vals), tok),
            pl.BlockSpec((nseq, BLK, vals), tok),
            pl.BlockSpec((nseq, 1, heads, DK, DV), lambda i, c: (i, blocks - 1 - c, 0, 0, 0)),
            pl.BlockSpec((nseq, 1, heads, BLK, BLK), lambda i, c: (i, blocks - 1 - c, 0, 0, 0)),
            pl.BlockSpec((CONV, qkv), whole),
            pl.BlockSpec((2, 128), whole),
            pl.BlockSpec((1, DV), whole),
        ],
        out_specs=(
            pl.BlockSpec((nseq, BLK, width), tok),
            pl.BlockSpec((nseq, 1, 8, 128), lambda i, c: (i, blocks - 1 - c, 0, 0)),
            pl.BlockSpec((8 * CONV, qkv), whole),
            pl.BlockSpec((16, 128), whole),
            pl.BlockSpec((8, DV), whole),
        ),
        scratch_shapes=[
            pltpu.VMEM((nseq, 8 + BLK, qkv), F32),
            pltpu.VMEM((nseq, BLK + 8, qkv), F32),
            pltpu.VMEM((nseq, heads, DK, DV), F32),
        ],
        compiler_params=pltpu.CompilerParams(dimension_semantics=("arbitrary", "arbitrary")),
        name="mixer_bwd",
    )(proj, proj, dmixed, o, u, states, invs, conv, rates, gain)
    dconv = jnp.sum(dconv.reshape(CONV, 8, qkv), axis=1)
    drate = jnp.sum(drate.reshape(2, 8, 128), axis=1)[:, :heads]
    dgain = jnp.sum(dgain, axis=0)
    return dproj, dots[:, :, 0, :], dconv, drate[0], drate[1], dgain


D = 1024
PARTS = 1


def contract_rows(left, right):
    return lax.dot_general(left, right, (((0,), (0,)), ((), ())), preferred_element_type=F32)


def xor_perm(size, bit):
    return [(i, i ^ bit) for i in range(size)]


def send_col(values, bit):
    return lax.ppermute(values, "col", xor_perm(4, bit))


def gather_features(values):
    half = values.shape[0] // 2
    from_x = send_col(values, 1)
    from_y = send_col(values, 2)
    far_top = send_col(from_y[:half], 1)
    far_low = send_col(from_x[half:], 2)
    return jnp.concatenate(
        [values, from_x, from_y, jnp.concatenate([far_top, far_low], axis=0)], axis=1
    )


def sum_features(partial):
    width = partial.shape[1] // 4
    half = partial.shape[0] // 2
    own, part_x, part_y, far = [partial[:, width * i : width * i + width] for i in range(4)]
    far = far.astype(BF16)
    via_x = send_col(far[:half], 1).astype(F32)
    via_y = send_col(far[half:], 2).astype(F32)
    to_y = jnp.concatenate([part_y[:half] + via_x, part_y[half:]], axis=0).astype(BF16)
    to_x = jnp.concatenate([part_x[:half], part_x[half:] + via_y], axis=0).astype(BF16)
    return own + send_col(to_x, 1).astype(F32) + send_col(to_y, 2).astype(F32)


def sum_scalars(values):
    total = values
    for bit in range(1, 4):
        total = total + send_col(values, bit)
    return total


def col_order(values, col):
    rows = values.shape[0] // 4
    return jnp.concatenate(
        [lax.dynamic_slice_in_dim(values, (col ^ b) * rows, rows, 0) for b in range(4)], axis=0
    )


def swap_cores(mine, dp):
    other = lax.ppermute(mine, "dp", [(0, 1), (1, 0)])
    return jnp.where(
        dp == 0, jnp.concatenate([mine, other], axis=0), jnp.concatenate([other, mine], axis=0)
    )


def gather_weight(block, dp, col):
    rows = block.shape[0] // 2
    half = lax.dynamic_slice_in_dim(block, dp * rows, rows, 0)
    return col_order(lax.all_gather(half, ("row", "dp"), axis=0, tiled=True), col)


def scatter_weight(grad, dp, col):
    mine = lax.psum_scatter(
        col_order(grad.astype(BF16), col), ("row", "dp"), scatter_dimension=0, tiled=True
    )
    return swap_cores(mine, dp).astype(F32)


def on_device(
    inputs,
    out_grad,
    seq_lengths,
    first_gain,
    query_proj,
    key_proj,
    value_proj,
    decay_proj,
    beta_proj,
    gate_proj,
    query_conv,
    key_conv,
    value_conv,
    decay_log,
    step_bias,
    output_gain,
    output_proj,
    second_gain,
    hidden_gate,
    hidden_up,
    hidden_down,
):
    seq_count, length, col_width = inputs.shape
    heads = decay_log.shape[0]
    parts = PARTS
    per_part = seq_count // parts
    tokens = per_part * length
    col = lax.axis_index("col")
    dp = lax.axis_index("dp")
    row_block = query_proj.shape[0]
    vals = heads * DV
    qkv = heads * (2 * DK + DV)
    ff_half = hidden_gate.shape[1]

    in_block = jnp.concatenate(
        [query_proj, key_proj, value_proj, gate_proj, decay_proj, beta_proj,
         jnp.zeros((row_block, 128 - 2 * heads), BF16)], axis=1)
    in_weights = gather_weight(in_block, dp, col)
    out_weights = gather_weight(output_proj.T, dp, col)
    ff_weights = gather_weight(
        jnp.concatenate([hidden_gate, hidden_up, hidden_down.T], axis=1), dp, col)
    up_weights = ff_weights[:, : 2 * ff_half]
    down_weights = ff_weights[:, 2 * ff_half :]

    conv = jnp.concatenate([query_conv, key_conv, value_conv], axis=1).astype(F32)
    rates = rate_rows(decay_log, step_bias)
    gain_row = output_gain.astype(F32)[None]
    first_order = col_order(first_gain.astype(F32), col)[None]
    second_order = col_order(second_gain.astype(F32), col)[None]
    first_local = first_order[:, :col_width]
    second_local = second_order[:, :col_width]
    positions = lax.broadcasted_iota(jnp.int32, (seq_count, length), 1)
    valid_all = (positions < seq_lengths[:, None]).astype(F32)

    state = []
    for part in range(parts):
        seqs = slice(part * per_part, (part + 1) * per_part)
        valid = valid_all[seqs].reshape(tokens, 1)
        local_low = inputs[seqs].reshape(tokens, col_width)
        full = gather_features(local_low).astype(F32)
        scale = lax.rsqrt(jnp.mean(full * full, axis=1, keepdims=True) + NORM_EPS)
        normed = (full * scale * first_order * valid).astype(BF16)
        grad_out = out_grad[seqs].reshape(tokens, col_width).astype(F32) * valid
        state.append(dict(valid=valid, local=local_low.astype(F32), scale=scale, normed=normed,
                          grad_out=grad_out))
    for st in state:
        proj = jnp.dot(st["normed"], in_weights, preferred_element_type=F32)
        st["proj"] = proj.reshape(per_part, length, -1)
        mixed, *st["saved"] = mixer_fwd(st["proj"], conv, rates, gain_row, heads, per_part)
        st["mixed"] = mixed.reshape(tokens, vals)
        attention = sum_features(mm_nt(st["mixed"], out_weights))
        st["hidden"] = st["local"] + attention
        st["grad_full"] = gather_features(st["grad_out"].astype(BF16))
    results = []
    ff_grad = 0.0
    second_gain_grad = 0.0
    for st in state:
        full = gather_features(st["hidden"].astype(BF16)).astype(F32)
        scale = lax.rsqrt(jnp.mean(full * full, axis=1, keepdims=True) + NORM_EPS)
        normed = (full * scale * second_order * st["valid"]).astype(BF16)
        gate_up = jnp.dot(normed, up_weights, preferred_element_type=F32)
        gate_act = gate_up[:, :ff_half]
        up_act = gate_up[:, ff_half:]
        sig = jax.nn.sigmoid(gate_act)
        silu = gate_act * sig
        act = (silu * up_act).astype(BF16)
        inner_grad = jnp.dot(st["grad_full"], down_weights, preferred_element_type=F32)
        gate_grad = (inner_grad * up_act * sig * (1.0 + gate_act * (1.0 - sig))).astype(BF16)
        up_grad = (inner_grad * silu).astype(BF16)
        both = jnp.concatenate([gate_grad, up_grad], axis=1)
        dots = sum_scalars(jnp.sum(
            gate_grad.astype(F32) * gate_act + up_grad.astype(F32) * up_act, axis=1))[:, None]
        second_grad = sum_features(mm_nt(both, up_weights)) * st["valid"]
        hat = st["hidden"] * scale
        second_gain_grad = second_gain_grad + jnp.sum(second_grad * hat, axis=0)
        st["hidden_grad"] = st["grad_out"] + scale * (
            second_grad * second_local - hat * (dots * (1.0 / D)))
        st["attn_grad"] = gather_features(st["hidden_grad"].astype(BF16))
        feed = sum_features(mm_nt(act, down_weights))
        results.append(((st["hidden"] + feed) * st["valid"]).astype(BF16))
        ff_grad = ff_grad + jnp.concatenate(
            [contract_rows(normed, both), contract_rows(st["grad_full"], act)], axis=1)
    ff_grad = scatter_weight(ff_grad, dp, col)
    out_weight_grad = 0.0
    in_weight_grad = 0.0
    first_gain_grad = 0.0
    input_grads = []
    small = 0.0
    for st in state:
        mixed_grad = jnp.dot(st["attn_grad"], out_weights, preferred_element_type=F32)
        out_weight_grad = out_weight_grad + contract_rows(st["attn_grad"], st["mixed"])
        dproj, dots, *grads = mixer_bwd(
            st["proj"], mixed_grad.reshape(per_part, length, vals), st["saved"], conv, rates,
            gain_row, heads, per_part)
        small = small + jnp.concatenate([grad.reshape(-1) for grad in grads])
        dproj = dproj.reshape(tokens, -1)
        dots = sum_scalars(dots)
        in_weight_grad = in_weight_grad + contract_rows(st["normed"], dproj)
        st["dots"] = dots.reshape(tokens, 1)
        first_grad = sum_features(mm_nt(dproj, in_weights)) * st["valid"]
        hat = st["local"] * st["scale"]
        first_gain_grad = first_gain_grad + jnp.sum(first_grad * hat, axis=0)
        input_grads.append(st["hidden_grad"] + st["scale"] * (
            first_grad * first_local - hat * (st["dots"] * (1.0 / D))))
    out_weight_grad = scatter_weight(out_weight_grad, dp, col)
    in_weight_grad = scatter_weight(in_weight_grad, dp, col)
    conv_size = CONV * qkv
    small_sums = lax.psum(
        jnp.concatenate([small[: conv_size + 2 * heads], second_gain_grad, first_gain_grad]),
        ("dp", "row"))
    conv_grad = small_sums[:conv_size].reshape(CONV, qkv)
    gain_out_grad = lax.psum(small[conv_size + 2 * heads :], ("dp", "row", "col"))
    at = conv_size + 2 * heads
    gate_at = qkv + vals
    qk = heads * DK
    return (
        jnp.concatenate(results, axis=0).reshape(seq_count, length, col_width),
        jnp.concatenate(input_grads, axis=0).reshape(seq_count, length, col_width),
        small_sums[at + col_width : at + 2 * col_width],
        in_weight_grad[:, :qk],
        in_weight_grad[:, qk : 2 * qk],
        in_weight_grad[:, 2 * qk : qkv],
        in_weight_grad[:, gate_at : gate_at + heads],
        in_weight_grad[:, gate_at + heads : gate_at + 2 * heads],
        in_weight_grad[:, qkv:gate_at],
        conv_grad[:, :qk],
        conv_grad[:, qk : 2 * qk],
        conv_grad[:, 2 * qk :],
        small_sums[conv_size : conv_size + heads],
        small_sums[conv_size + heads : at],
        gain_out_grad,
        out_weight_grad.T,
        small_sums[at : at + col_width],
        ff_grad[:, :ff_half],
        ff_grad[:, ff_half : 2 * ff_half],
        ff_grad[:, 2 * ff_half :].T,
    )


def solution(mesh):
    in_specs = (
        P(("dp", "row"), None, "col"),
        P(("dp", "row"), None, "col"),
        P(("dp", "row")),
        P(),
        P("row", "col"),
        P("row", "col"),
        P("row", "col"),
        P("row", "col"),
        P("row", "col"),
        P("row", "col"),
        P(None, "col"),
        P(None, "col"),
        P(None, "col"),
        P("col"),
        P("col"),
        P(),
        P("col", "row"),
        P(),
        P("row", "col"),
        P("row", "col"),
        P("col", "row"),
    )
    out_specs = (
        P(("dp", "row"), None, "col"),
        P(("dp", "row"), None, "col"),
        P("col"),
        P("row", "col"),
        P("row", "col"),
        P("row", "col"),
        P("row", "col"),
        P("row", "col"),
        P("row", "col"),
        P(None, "col"),
        P(None, "col"),
        P(None, "col"),
        P("col"),
        P("col"),
        P(),
        P("col", "row"),
        P("col"),
        P("row", "col"),
        P("row", "col"),
        P("col", "row"),
    )
    return jax.shard_map(
        on_device, mesh=mesh, in_specs=in_specs, out_specs=out_specs, check_vma=False
    )
```

time: 2160 us -> 693 us (0.32)
  waiting for transfers between devices: 703 us -> 226 us
  other arithmetic: 512 us -> 69.8 us
  matrix products: 523 us -> 122 us
  local copies, waits for them, and re-layouts: 279 us -> 39.6 us
  Pallas kernels: 0 us -> 110 us
  blocking collectives: 110 us -> 75 us
  starting transfers between devices: 0.93 us -> 29.3 us
    reduce_scatter x8 -> x3, waiting for transfers between devices: 384 us -> 0.02 us  [scatter_weight(): lax.psum_scatter(col_order(grad.astype(BF16), col), ('row', 'dp'), scatte...]
    dot_general x207 -> x8, matrix products: 460 us -> 82.4 us  [the longest x4 30.6 us: mm_nt(): lax.dot_general(a, b, (((1,), (1,)), ((), ())), preferred_element_type=F32)]
    another operation x12 -> x5, other arithmetic: 339 us -> 4.82 us  [the longest x3 318 us: delta_rule(): jax.scipy.linalg.solve_triangular(system, right_side, lower=True, unit_di...]
    all_gather x10 -> x3, waiting for transfers between devices: 303 us -> 13 us  [gather_weight(): lax.all_gather(half, ('row', 'dp'), axis=0, tiled=True)]
    ppermute x0 -> x41, waiting for transfers between devices: none -> 213 us  [the longest x38 212 us: send_col(): return lax.ppermute(values, 'col', xor_perm(4, bit))]
    pallas_call x0 -> x2, Pallas kernels: none -> 110 us  [the longest x1 67.1 us: mixer_bwd(): pl.pallas_call(functools.partial(bwd_kernel, heads, nseq), out_shape=(jax...]
    all_gather x4 -> x0, blocking collectives: 63.4 us -> none  [the longest x1 20.1 us: on_device(): lax.all_gather(key_proj, 'row', axis=0, tiled=True)]
    reduce_sum x35 -> x6, other arithmetic: 93.3 us -> 32.6 us  [the longest x2 24.6 us: on_device(): scale = lax.rsqrt(jnp.mean(full * full, axis=1, keepdims=True) + NORM_EPS)]
  transfers between devices with their start and end apart: 19 -> 47, of which waited for: 14 -> 23; matrix products, arithmetic and copies ran while one was open for 58% -> 27% of each run, Pallas kernels for 0% -> 16%
where the time goes in v1:
time: 693 us; the launch traced here: 687 us
  waiting for transfers between devices  226 us (33%)
  matrix products  122 us (18%)
  Pallas kernels  110 us (16%)
  blocking collectives  75 us (11%)
  other arithmetic  69.8 us (10%)
  local copies, waits for them, and re-layouts  39.6 us (6%)
  starting transfers between devices  29.3 us (4%)
  between operations  15.4 us (2%)
    ppermute x38, waiting for transfers between devices, send_col(): return lax.ppermute(values, 'col', xor_perm(4, bit))  212 us
    pallas_call x1, Pallas kernels, mixer_bwd(): pl.pallas_call(functools.partial(bwd_kernel, heads, nseq), out_shape=(jax...  67.1 us
    psum x1, blocking collectives, on_device(): lax.psum(small[conv_size + 2 * heads:], ('dp', 'row', 'col'))  45.8 us
    pallas_call x1, Pallas kernels, mixer_fwd(): pl.pallas_call(functools.partial(fwd_kernel, heads, nseq), out_shape=(jax...  42.8 us
    dot_general x4, matrix products, contract_rows(): lax.dot_general(left, right, (((0,), (0,)), ((), ())), preferred_element_...  39.5 us
    dot_general x4, matrix products, mm_nt(): lax.dot_general(a, b, (((1,), (1,)), ((), ())), preferred_element_type=F32)  30.6 us
    psum x1, blocking collectives, on_device(): lax.psum(jnp.concatenate([small[:conv_size + 2 * heads], second_gain_grad...  29.1 us
    ppermute x38, starting transfers between devices, send_col(): return lax.ppermute(values, 'col', xor_perm(4, bit))  27.9 us
  transfers between devices with their start and end apart: 47, of which 23 were waited for; matrix products, arithmetic and copies ran while one was open for 27% of the time, Pallas kernels for 16%

profile of v1, /device:TPU:1, one launch (start us, length us, event | category | flops | bytes accessed | tf_op | source)
XLA Modules:
  0.0 686.6 jit_solution(7652138042535111656)
XLA Ops:
  18.8 19.2 %collective-permute-done.1 = bf16[2048,256]{1,0:T(8,128)(2,1)S(1)} collective-permute-done((bf16[2048,256]{1,0:T(8,128)(2,1)}, bf16[2048,256]{1,0:T(8,128)(2,1)S(1)}, u32[]{:S(2)}, u32[]{:S(2)}) %collective-permute-start.1) | collective-permute-done | bytes 1048608 | tf_op jit(solution)/shard_map/ppermute | solution.py:455
  41.9 8.5 %collective-permute-done.2 = bf16[1024,256]{1,0:T(8,128)(2,1)S(1)} collective-permute-done((bf16[1024,256]{1,0:T(8,128)(2,1)S(1)}, bf16[1024,256]{1,0:T(8,128)(2,1)S(1)}, u32[]{:S(2)}, u32[]{:S(2)}) %collective-permute-start.2) | collective-permute-done | bytes 524320 | tf_op jit(solution)/shard_map/ppermute | solution.py:455
  51.2 11.8 %fusion = f32[2048]{0:T(1024)S(1)} fusion(bf16[1024,256]{1,0:T(8,128)(2,1)S(1)} %collective-permute-done.3, bf16[1024,256]{1,0:T(8,128)(2,1)S(1)} %collective-permute-done.2, bf16[2048,256]{1,0:T(8,128)(2,1)S(1)} %collective-permute-done.1, bf16[2048,256]{1,0:T(8,128)(2,1)S(1)} %collective-permute-done, bf16[2048,256]{1,0:T(8,128)(2,1)S(1)} %bitcast.62), kind=kLoop, calls=%fused_computation.4 | loop fusion | flops 25163776 | bytes 4202496 | tf_op jit(solution)/shard_map/reduce_sum | solution.py:576
  65.2 12.9 %all-gather.4.cloned.1.call-done = bf16[1024,1664]{1,0:T(8,128)(2,1)} async-done(((bf16[128,1664]{1,0:T(8,128)(2,1)}), bf16[1024,1664]{1,0:T(8,128)(2,1)}) %all-gather.4.cloned.1.call-update) | async-done | bytes 3407888 | tf_op jit(solution)/shard_map/all_gather | solution.py:505
  80.4 13.2 %fusion.45 = f32[2048,1664]{1,0:T(8,128)} fusion(bf16[256,1664]{1,0:T(8,128)(2,1)S(1)} %get-tuple-element.146, bf16[256,1664]{1,0:T(8,128)(2,1)S(1)} %get-tuple-element.147, bf16[256,1664]{1,0:T(8,128)(2,1)S(1)} %get-tuple-element.148, bf16[256,1664]{1,0:T(8,128)(2,1)S(1)} %get-tuple-element.145, f32[2048]{0:T(1024)S(1)} %bitcast.71, ...), kind=kOutput, calls=%fused_computation.108 | convolution fusion | flops 7022313472 | bytes 21254144 | tf_op jit(solution)/shard_map/dot_general | solution.py:582
  93.6 42.8 %mixer_fwd.1 = (bf16[2,1024,512]{2,1,0:T(8,128)(2,1)}, f32[2,1024,512]{2,1,0:T(8,128)}, bf16[2,1024,512]{2,1,0:T(8,128)(2,1)}, bf16[2,8,2,128,256]{4,3,2,1,0:T(8,128)(2,1)}, bf16[2,8,2,128,128]{4,3,2,1,0:T(8,128)(2,1)}) custom-call(f32[2,1024,1664]{2,1,0:T(8,128)} %bitcast.57, f32[4,1024]{1,0:T(4,128)} %maximum_convert_fusion.conv_ref, ...), custom_call_target="tpu_custom_call" | custom-call | tf_op jit(solution)/shard_map/mixer_fwd/pallas_call | solution.py:206
  143.1 10.9 %collective-permute-done.4 = bf16[1024,256]{1,0:T(8,128)(2,1)S(1)} collective-permute-done((bf16[1024,256]{1,0:T(8,128)(2,1)S(1)}, bf16[1024,256]{1,0:T(8,128)(2,1)S(1)}, u32[]{:S(2)}, u32[]{:S(2)}) %collective-permute-start.4) | collective-permute-done | bytes 524320 | tf_op jit(solution)/shard_map/ppermute | solution.py:455
  158.8 19.7 %collective-permute-done.5 = bf16[2048,256]{1,0:T(8,128)(2,1)S(1)} collective-permute-done((bf16[2048,256]{1,0:T(8,128)(2,1)S(1)}, bf16[2048,256]{1,0:T(8,128)(2,1)S(1)}, u32[]{:S(2)}, u32[]{:S(2)}) %collective-permute-start.5) | collective-permute-done | bytes 1048608 | tf_op jit(solution)/shard_map/ppermute | solution.py:455
  182.0 20.0 %collective-permute-done.17 = bf16[2048,256]{1,0:T(8,128)(2,1)S(1)} collective-permute-done((bf16[2048,256]{1,0:T(8,128)(2,1)S(1)}, bf16[2048,256]{1,0:T(8,128)(2,1)S(1)}, u32[]{:S(2)}, u32[]{:S(2)}) %collective-permute-start.17) | collective-permute-done | bytes 1048608 | tf_op jit(solution)/shard_map/ppermute | solution.py:455
  207.3 17.2 %collective-permute-done.9 = bf16[2048,256]{1,0:T(8,128)(2,1)} collective-permute-done((bf16[2048,256]{1,0:T(8,128)(2,1)}, bf16[2048,256]{1,0:T(8,128)(2,1)}, u32[]{:S(2)}, u32[]{:S(2)}) %collective-permute-start.9) | collective-permute-done | bytes 1048608 | tf_op jit(solution)/shard_map/ppermute | solution.py:455
  228.1 17.8 %collective-permute-done.10 = bf16[1024,256]{1,0:T(8,128)(2,1)S(1)} collective-permute-done((bf16[1024,256]{1,0:T(8,128)(2,1)S(1)}, bf16[1024,256]{1,0:T(8,128)(2,1)S(1)}, u32[]{:S(2)}, u32[]{:S(2)}) %collective-permute-start.10) | collective-permute-done | bytes 524320 | tf_op jit(solution)/shard_map/ppermute | solution.py:455
  246.9 12.8 %fusion.4 = f32[2048]{0:T(1024)S(1)} fusion(bf16[1024,256]{1,0:T(8,128)(2,1)S(1)} %collective-permute-done.11, bf16[1024,256]{1,0:T(8,128)(2,1)S(1)} %collective-permute-done.10, bf16[2048,256]{1,0:T(8,128)(2,1)} %collective-permute-done.9, bf16[2048,256]{1,0:T(8,128)(2,1)} %collective-permute-done.8, bf16[2048,256]{1,0:T(8,128)(2,1)} %convert_element_type.156), kind=kLoop, calls=%fused_computation.8 | loop fusion | flops 25163776 | bytes 4202496 | tf_op jit(solution)/shard_map/reduce_sum | solution.py:594
  259.8 19.3 %fusion.11 = f32[2048,1408]{0,1:T(8,128)} fusion(bf16[1024,2112]{0,1:T(8,128)(2,1)S(1)} %pad_maximum_fusion.2, f32[1024]{0:T(1024)S(1)} %pad_maximum_fusion.23, f32[2048]{0:T(1024)S(1)} %add_rsqrt_fusion, f32[2048]{0:T(1024)S(1)} %bitcast.73, bf16[1024,256]{1,0:T(8,128)(2,1)S(1)} %collective-permute-done.11, ...), kind=kOutput, calls=%fused_computation.41 | convolution fusion | flops 5934940160 | bytes 18632704 | tf_op jit(solution)/shard_map/dot_general | solution.py:596
  279.2 12.6 %add_reduce_fusion = (f32[2048]{0:T(1024)S(1)}, bf16[2048,704]{0,1:T(8,128)(2,1)}, bf16[2048,704]{0,1:T(8,128)(2,1)}, bf16[2048,704]{0,1:T(8,128)(2,1)}) fusion(f32[2048,1408]{0,1:T(8,128)} %fusion.11, bf16[256,2112]{0,1:T(8,128)(2,1)S(1)} %get-tuple-element.122, bf16[256,2112]{0,1:T(8,128)(2,1)S(1)} %get-tuple-element.123, ...), kind=kOutput, calls=%fused_computation.17 | convolution fusion | flops 3009804288 | bytes 28712960 | tf_op jit(solution)/shard_map/dot_general | solution.py:602
  291.8 6.7 convolution_convert_fusion.2
  301.1 11.3 %convolution_convert_fusion = bf16[1024,1408]{1,0:T(8,128)(2,1)S(1)} fusion(bf16[2048,704]{0,1:T(8,128)(2,1)} %get-tuple-element.106, bf16[2048,704]{0,1:T(8,128)(2,1)} %get-tuple-element.105, f32[1024]{0:T(1024)S(1)} %pad_maximum_fusion.23, f32[2048]{0:T(1024)S(1)} %add_rsqrt_fusion, f32[2048]{0:T(1024)S(1)} %bitcast.74, bf16[1024,256]{1,0:T(8,128)(2,1)} %copy-done.42, ...), kind=kOutput, calls=%fused_computation.33 | convolution fusion | flops 5947916288 | bytes 12865536 | tf_op jit(solution)/shard_map/dot_general | solution.py:447
  312.9 8.2 %pad_maximum_fusion.1 = bf16[1024,2112]{1,0:T(8,128)(2,1)} fusion(bf16[256,2112]{1,0:T(8,128)(2,1)S(1)} %get-tuple-element.120, bf16[256,2112]{1,0:T(8,128)(2,1)S(1)} %get-tuple-element.119, bf16[256,2112]{1,0:T(8,128)(2,1)S(1)} %get-tuple-element.118, bf16[256,2112]{1,0:T(8,128)(2,1)S(1)} %get-tuple-element.117), kind=kLoop, calls=%fused_computation.27 | loop fusion | flops 17301504 | bytes 8650752 | tf_op jit(solution)/shard_map/concatenate | solution.py:490
  321.1 9.9 %fusion.78 = (bf16[2048,1024]{1,0:T(8,128)(2,1)S(1)}, f32[2048,1024]{1,0:T(8,128)S(1)}) fusion(bf16[1024,2112]{0,1:T(8,128)(2,1)} %copy-done.13, bf16[2048,704]{0,1:T(8,128)(2,1)} %get-tuple-element.106, bf16[2048,704]{0,1:T(8,128)(2,1)} %get-tuple-element.105), kind=kOutput, calls=%fused_computation.178 | convolution fusion | flops 5919211520 | bytes 21233664 | tf_op jit(solution)/shard_map/dot_general | solution.py:25
  331.9 10.2 %collective-permute-done.20 = bf16[1024,256]{1,0:T(8,128)(2,1)S(1)} collective-permute-done((bf16[1024,256]{1,0:T(8,128)(2,1)S(1)}, bf16[1024,256]{1,0:T(8,128)(2,1)S(1)}, u32[]{:S(2)}, u32[]{:S(2)}) %collective-permute-start.20) | collective-permute-done | bytes 524320 | tf_op jit(solution)/shard_map/ppermute | solution.py:455
  347.0 17.2 %collective-permute-done.24 = f32[2048]{0:T(1024)S(1)} collective-permute-done((f32[2048]{0:T(1024)S(1)}, f32[2048]{0:T(1024)S(1)}, u32[]{:S(2)}, u32[]{:S(2)}) %collective-permute-start.24) | collective-permute-done | bytes 8224 | tf_op jit(solution)/shard_map/ppermute | solution.py:455
  369.3 19.0 %collective-permute-done.28 = bf16[2048,256]{1,0:T(8,128)(2,1)S(1)} collective-permute-done((bf16[2048,256]{1,0:T(8,128)(2,1)S(1)}, bf16[2048,256]{1,0:T(8,128)(2,1)S(1)}, u32[]{:S(2)}, u32[]{:S(2)}) %collective-permute-start.28) | collective-permute-done | bytes 1048608 | tf_op jit(solution)/shard_map/ppermute | solution.py:455
  389.6 6.7 fusion.80
  399.7 9.2 %convolution_convert_fusion.3 = bf16[1024,512]{1,0:T(8,128)(2,1)S(1)} fusion(bf16[2048,512]{1,0:T(8,128)(2,1)S(1)} %bitcast.67, bf16[1024,256]{1,0:T(8,128)(2,1)S(1)} %collective-permute-done.30, bf16[1024,256]{1,0:T(8,128)(2,1)S(1)} %collective-permute-done.29, bf16[2048,256]{1,0:T(8,128)(2,1)S(1)} %collective-permute-done.28, ...), kind=kOutput, calls=%fused_computation.67 | convolution fusion | flops 2168979456 | bytes 7340032 | tf_op jit(solution)/shard_map/dot_general | solution.py:447
  410.4 6.7 fusion.48
  417.1 67.1 %mixer_bwd.1 = (bf16[2,1024,1664]{2,1,0:T(8,128)(2,1)}, f32[2,8,8,128]{3,2,1,0:T(8,128)}, f32[32,1024]{1,0:T(8,128)}, f32[16,128]{1,0:T(8,128)}, f32[8,256]{1,0:T(8,128)}) custom-call(f32[2,1024,1664]{2,1,0:T(8,128)} %bitcast.58, f32[2,1024,1664]{2,1,0:T(8,128)} %bitcast.59, f32[2,1024,512]{2,1,0:T(8,128)} %bitcast.65, ...), custom_call_target="tpu_custom_call" | custom-call | tf_op jit(solution)/shard_map/mixer_bwd/pallas_call | solution.py:399
  484.2 12.3 %convolution_convert_fusion.1 = bf16[1024,1664]{1,0:T(8,128)(2,1)S(1)} fusion(bf16[2048,1664]{1,0:T(8,128)(2,1)} %bitcast.90, f32[2048]{0:T(1024)S(1)} %bitcast.76, f32[1024]{0:T(1024)S(1)} %pad_maximum_fusion.22, f32[2048]{0:T(1024)S(1)} %add_rsqrt_fusion.1, bf16[1024,256]{1,0:T(8,128)(2,1)} %copy-done.39, bf16[1024,256]{1,0:T(8,128)(2,1)} %copy-done.37, ...), kind=kOutput, calls=%fused_computation.34 | convolution fusion | flops 7010385920 | bytes 14438400 | tf_op jit(solution)/shard_map/dot_general | solution.py:447
  496.8 6.6 pad_maximum_fusion.6
  508.3 10.1 %fusion.79 = (bf16[2048,1024]{1,0:T(8,128)(2,1)S(1)}, f32[2048,1024]{1,0:T(8,128)S(1)}) fusion(bf16[2048,1664]{1,0:T(8,128)(2,1)} %bitcast.91, bf16[256,1664]{1,0:T(8,128)(2,1)S(1)} %copy-done.32, bf16[256,1664]{1,0:T(8,128)(2,1)S(1)} %copy-done.34, bf16[256,1664]{1,0:T(8,128)(2,1)S(1)} %copy-done.36, bf16[256,1664]{1,0:T(8,128)(2,1)S(1)} %copy-done.30), kind=kOutput, calls=%fused_computation.179 | convolution fusion | flops 6995050496 | bytes 22806528 | tf_op jit(solution)/shard_map/dot_general | solution.py:25
  533.7 39.5 %collective-permute-done.35 = f32[2,8,128]{2,1,0:T(8,128)S(1)} collective-permute-done((f32[2,8,128]{2,1,0:T(8,128)S(1)}, f32[2,8,128]{2,1,0:T(8,128)S(1)}, u32[]{:S(2)}, u32[]{:S(2)}) %collective-permute-start.35) | collective-permute-done | bytes 8224 | tf_op jit(solution)/shard_map/ppermute | solution.py:455
  576.4 45.8 %psum.15 = f32[256]{0:T(256)} all-reduce(f32[256]{0:T(256)S(1)} %reduce_sum.79), channel_id=1, replica_groups=mesh['dp'=2,'row'=4,'col'=4] {'dp','row','col'}, use_global_device_ids=true, to_apply=%region_10.11 | all-reduce | flops 256 | bytes 2048 | tf_op jit(solution)/shard_map/psum | solution.py:647
  622.3 7.9 %fusion.18 = (f32[256]{0:T(256)S(1)}, f32[256]{0:T(256)S(1)}, f32[2048,256]{1,0:T(8,128)}, bf16[2048,256]{1,0:T(8,128)(2,1)}) fusion(f32[2048]{0:T(1024)S(1)} %add_rsqrt_fusion.1, f32[2048]{0:T(1024)S(1)} %bitcast.77, bf16[2048,256]{1,0:T(8,128)(2,1)} %collective-permute-done.34, bf16[2048,256]{1,0:T(8,128)(2,1)} %collective-permute-done.32, ...), kind=kLoop, calls=%fused_computation.48 | loop fusion | flops 15203840 | bytes 21007360 | tf_op jit(solution)/shard_map/reduce_sum | solution.py:637
  630.3 29.1 %psum.14 = f32[4612]{0:T(1024)S(1)} all-reduce(f32[4612]{0:T(1024)S(1)} %concatenate.142), channel_id=1, replica_groups=mesh['dp'=2,'row'=4,'col'=4] {'dp','row'}, use_global_device_ids=true, to_apply=%region_7.8 | all-reduce | flops 4612 | bytes 36896 | tf_op jit(solution)/shard_map/psum | solution.py:643
  (303 shorter events, 109.0 us)
Async XLA Ops:
  7.3 55.7 %all-gather.6.cloned.1.call-start = ((), (), s32[]{:S(2)}) async-start(), calls=%async_computation.4 | async-start | bytes 1179648 | tf_op jit(solution)/shard_map/all_gather | solution.py:505
  8.8 69.3 %all-gather.4.cloned.1.call-start = ((), (), s32[]{:S(2)}) async-start(), calls=%async_computation.3 | async-start | bytes 3833856 | tf_op jit(solution)/shard_map/all_gather | solution.py:505
  12.7 192.0 %all-gather.8.cloned.1.call-start = ((), (), s32[]{:S(2)}) async-start(), calls=%async_computation.5 | async-start | bytes 4866048 | tf_op jit(solution)/shard_map/all_gather | solution.py:505
  12.8 25.2 %collective-permute-start.1 = (bf16[2048,256]{1,0:T(8,128)(2,1)}, bf16[2048,256]{1,0:T(8,128)(2,1)S(1)}, u32[]{:S(2)}, u32[]{:S(2)}) collective-permute-start(bf16[2048,256]{1,0:T(8,128)(2,1)} %bitcast.60), channel_id=1, source_target_pairs={{0,2},{1,3},{2,0},{3,1},{4,6},{5,7},{6,4},{7,5},{8,10},{9,11},{10,... | collective-permute-start | bytes 3145736 | tf_op jit(solution)/shard_map/ppermute | solution.py:455
  14.9 24.3 %collective-permute-start = (bf16[2048,256]{1,0:T(8,128)(2,1)}, bf16[2048,256]{1,0:T(8,128)(2,1)S(1)}, u32[]{:S(2)}, u32[]{:S(2)}) collective-permute-start(bf16[2048,256]{1,0:T(8,128)(2,1)} %bitcast.61), channel_id=1, source_target_pairs={{0,1},{1,0},{2,3},{3,2},{4,5},{5,4},{6,7},{7,6},{8,9},{9,8},{10,11... | collective-permute-start | bytes 3145736 | tf_op jit(solution)/shard_map/ppermute | solution.py:455
  18.1 642.6 %reduce-scatter.8.cloned.1.call-start = ((), (), s32[]{:S(2)}) async-start(), calls=%async_computation.8 | async-start | bytes 5013504 | tf_op jit(solution)/shard_map/reduce_scatter | solution.py:509
  155.2 23.3 %collective-permute-start.5 = (bf16[2048,256]{1,0:T(8,128)(2,1)S(1)}, bf16[2048,256]{1,0:T(8,128)(2,1)S(1)}, u32[]{:S(2)}, u32[]{:S(2)}) collective-permute-start(bf16[2048,256]{1,0:T(8,128)(2,1)S(1)} %pad_maximum_fusion.9), channel_id=1, source_target_pairs={{0,1},{1,0},{2,3},{3,2},{4,5},{5,4},{6,7},{7,6},{8,9},{9,8},{10,11... | collective-permute-start | bytes 3145736 | tf_op jit(solution)/shard_map/ppermute | solution.py:455
  156.5 23.0 %collective-permute-start.7 = (bf16[2048,256]{1,0:T(8,128)(2,1)S(1)}, bf16[2048,256]{1,0:T(8,128)(2,1)S(1)}, u32[]{:S(2)}, u32[]{:S(2)}) collective-permute-start(bf16[2048,256]{1,0:T(8,128)(2,1)S(1)} %pad_maximum_fusion.10), channel_id=1, source_target_pairs={{0,2},{1,3},{2,0},{3,1},{4,6},{5,7},{6,4},{7,5},{8,10},{9,11},{10,... | collective-permute-start | bytes 3145736 | tf_op jit(solution)/shard_map/ppermute | solution.py:455
  157.3 44.7 %collective-permute-start.17 = (bf16[2048,256]{1,0:T(8,128)(2,1)S(1)}, bf16[2048,256]{1,0:T(8,128)(2,1)S(1)}, u32[]{:S(2)}, u32[]{:S(2)}) collective-permute-start(bf16[2048,256]{1,0:T(8,128)(2,1)S(1)} %fusion.29), channel_id=1, source_target_pairs={{0,2},{1,3},{2,0},{3,1},{4,6},{5,7},{6,4},{7,5},{8,10},{9,11},{10,... | collective-permute-start | bytes 3145736 | tf_op jit(solution)/shard_map/ppermute | solution.py:455
  158.5 44.7 %collective-permute-start.16 = (bf16[2048,256]{1,0:T(8,128)(2,1)S(1)}, bf16[2048,256]{1,0:T(8,128)(2,1)S(1)}, u32[]{:S(2)}, u32[]{:S(2)}) collective-permute-start(bf16[2048,256]{1,0:T(8,128)(2,1)S(1)} %fusion.29), channel_id=1, source_target_pairs={{0,1},{1,0},{2,3},{3,2},{4,5},{5,4},{6,7},{7,6},{8,9},{9,8},{10,11... | collective-permute-start | bytes 3145736 | tf_op jit(solution)/shard_map/ppermute | solution.py:455
  181.4 43.2 %collective-permute-start.9 = (bf16[2048,256]{1,0:T(8,128)(2,1)}, bf16[2048,256]{1,0:T(8,128)(2,1)}, u32[]{:S(2)}, u32[]{:S(2)}) collective-permute-start(bf16[2048,256]{1,0:T(8,128)(2,1)} %convert_element_type.156), channel_id=1, source_target_pairs={{0,2},{1,3},{2,0},{3,1},{4,6},{5,7},{6,4},{7,5},{8,10},{9,11},{10,... | collective-permute-start | bytes 3145736 | tf_op jit(solution)/shard_map/ppermute | solution.py:455
  181.7 44.3 %collective-permute-start.8 = (bf16[2048,256]{1,0:T(8,128)(2,1)}, bf16[2048,256]{1,0:T(8,128)(2,1)}, u32[]{:S(2)}, u32[]{:S(2)}) collective-permute-start(bf16[2048,256]{1,0:T(8,128)(2,1)} %convert_element_type.156), channel_id=1, source_target_pairs={{0,1},{1,0},{2,3},{3,2},{4,5},{5,4},{6,7},{7,6},{8,9},{9,8},{10,11... | collective-permute-start | bytes 3145736 | tf_op jit(solution)/shard_map/ppermute | solution.py:455
  202.9 76.3 %collective-permute-start.18 = (bf16[1024,256]{1,0:T(8,128)(2,1)}, bf16[1024,256]{1,0:T(8,128)(2,1)}, u32[]{:S(2)}, u32[]{:S(2)}) collective-permute-start(bf16[1024,256]{1,0:T(8,128)(2,1)} %slice.320), channel_id=1, source_target_pairs={{0,1},{1,0},{2,3},{3,2},{4,5},{5,4},{6,7},{7,6},{8,9},{9,8},{10,11... | collective-permute-start | bytes 1572872 | tf_op jit(solution)/shard_map/ppermute | solution.py:455
  204.4 74.8 %collective-permute-start.19 = (bf16[1024,256]{1,0:T(8,128)(2,1)}, bf16[1024,256]{1,0:T(8,128)(2,1)}, u32[]{:S(2)}, u32[]{:S(2)}) collective-permute-start(bf16[1024,256]{1,0:T(8,128)(2,1)} %slice.321), channel_id=1, source_target_pairs={{0,2},{1,3},{2,0},{3,1},{4,6},{5,7},{6,4},{7,5},{8,10},{9,11},{10,... | collective-permute-start | bytes 1572872 | tf_op jit(solution)/shard_map/ppermute | solution.py:455
  225.7 20.2 %collective-permute-start.10 = (bf16[1024,256]{1,0:T(8,128)(2,1)S(1)}, bf16[1024,256]{1,0:T(8,128)(2,1)S(1)}, u32[]{:S(2)}, u32[]{:S(2)}) collective-permute-start(bf16[1024,256]{1,0:T(8,128)(2,1)S(1)} %slice.308), channel_id=1, source_target_pairs={{0,1},{1,0},{2,3},{3,2},{4,5},{5,4},{6,7},{7,6},{8,9},{9,8},{10,11... | collective-permute-start | bytes 1572872 | tf_op jit(solution)/shard_map/ppermute | solution.py:455
  227.1 19.9 %collective-permute-start.11 = (bf16[1024,256]{1,0:T(8,128)(2,1)S(1)}, bf16[1024,256]{1,0:T(8,128)(2,1)S(1)}, u32[]{:S(2)}, u32[]{:S(2)}) collective-permute-start(bf16[1024,256]{1,0:T(8,128)(2,1)S(1)} %slice.309), channel_id=1, source_target_pairs={{0,2},{1,3},{2,0},{3,1},{4,6},{5,7},{6,4},{7,5},{8,10},{9,11},{10,... | collective-permute-start | bytes 1572872 | tf_op jit(solution)/shard_map/ppermute | solution.py:455
  321.1 341.7 %reduce-scatter.6.cloned.1.call-start = ((), (), s32[]{:S(2)}) async-start(), calls=%async_computation.7 | async-start | bytes 1179648 | tf_op jit(solution)/shard_map/reduce_scatter | solution.py:509
  342.6 22.5 %collective-permute-start.21 = (bf16[2048,256]{1,0:T(8,128)(2,1)S(1)}, bf16[2048,256]{1,0:T(8,128)(2,1)S(1)}, u32[]{:S(2)}, u32[]{:S(2)}) collective-permute-start(bf16[2048,256]{1,0:T(8,128)(2,1)S(1)} %pad_maximum_fusion.13), channel_id=1, source_target_pairs={{0,1},{1,0},{2,3},{3,2},{4,5},{5,4},{6,7},{7,6},{8,9},{9,8},{10,11... | collective-permute-start | bytes 3145736 | tf_op jit(solution)/shard_map/ppermute | solution.py:455
  343.2 22.0 %collective-permute-start.23 = (bf16[2048,256]{1,0:T(8,128)(2,1)S(1)}, bf16[2048,256]{1,0:T(8,128)(2,1)S(1)}, u32[]{:S(2)}, u32[]{:S(2)}) collective-permute-start(bf16[2048,256]{1,0:T(8,128)(2,1)S(1)} %pad_maximum_fusion.14), channel_id=1, source_target_pairs={{0,2},{1,3},{2,0},{3,1},{4,6},{5,7},{6,4},{7,5},{8,10},{9,11},{10,... | collective-permute-start | bytes 3145736 | tf_op jit(solution)/shard_map/ppermute | solution.py:455
  344.3 19.9 %collective-permute-start.24 = (f32[2048]{0:T(1024)S(1)}, f32[2048]{0:T(1024)S(1)}, u32[]{:S(2)}, u32[]{:S(2)}) collective-permute-start(f32[2048]{0:T(1024)S(1)} %get-tuple-element.104), channel_id=1, source_target_pairs={{0,1},{1,0},{2,3},{3,2},{4,5},{5,4},{6,7},{7,6},{8,9},{9,8},{10,11... | collective-permute-start | bytes 24584 | tf_op jit(solution)/shard_map/ppermute | solution.py:455
  345.4 18.9 %collective-permute-start.25 = (f32[2048]{0:T(1024)S(1)}, f32[2048]{0:T(1024)S(1)}, u32[]{:S(2)}, u32[]{:S(2)}) collective-permute-start(f32[2048]{0:T(1024)S(1)} %get-tuple-element.104), channel_id=1, source_target_pairs={{0,2},{1,3},{2,0},{3,1},{4,6},{5,7},{6,4},{7,5},{8,10},{9,11},{10,... | collective-permute-start | bytes 24584 | tf_op jit(solution)/shard_map/ppermute | solution.py:455
  345.8 19.3 %collective-permute-start.26 = (f32[2048]{0:T(1024)S(1)}, f32[2048]{0:T(1024)S(1)}, u32[]{:S(2)}, u32[]{:S(2)}) collective-permute-start(f32[2048]{0:T(1024)S(1)} %get-tuple-element.104), channel_id=1, source_target_pairs={{0,3},{1,2},{2,1},{3,0},{4,7},{5,6},{6,5},{7,4},{8,11},{9,10},{10,... | collective-permute-start | bytes 24584 | tf_op jit(solution)/shard_map/ppermute | solution.py:455
  368.0 20.3 %collective-permute-start.28 = (bf16[2048,256]{1,0:T(8,128)(2,1)S(1)}, bf16[2048,256]{1,0:T(8,128)(2,1)S(1)}, u32[]{:S(2)}, u32[]{:S(2)}) collective-permute-start(bf16[2048,256]{1,0:T(8,128)(2,1)S(1)} %get-tuple-element.102), channel_id=1, source_target_pairs={{0,2},{1,3},{2,0},{3,1},{4,6},{5,7},{6,4},{7,5},{8,10},{9,11},{10,... | collective-permute-start | bytes 3145736 | tf_op jit(solution)/shard_map/ppermute | solution.py:455
  368.5 20.0 %collective-permute-start.27 = (bf16[2048,256]{1,0:T(8,128)(2,1)S(1)}, bf16[2048,256]{1,0:T(8,128)(2,1)S(1)}, u32[]{:S(2)}, u32[]{:S(2)}) collective-permute-start(bf16[2048,256]{1,0:T(8,128)(2,1)S(1)} %get-tuple-element.102), channel_id=1, source_target_pairs={{0,1},{1,0},{2,3},{3,2},{4,5},{5,4},{6,7},{7,6},{8,9},{9,8},{10,11... | collective-permute-start | bytes 3145736 | tf_op jit(solution)/shard_map/ppermute | solution.py:455
  410.1 256.8 %reduce-scatter.4.cloned.1.call-start = ((), (), s32[]{:S(2)}) async-start(), calls=%async_computation.6 | async-start | bytes 3833856 | tf_op jit(solution)/shard_map/reduce_scatter | solution.py:509
  506.0 14.2 %collective-permute-start.12 = (bf16[1024,256]{1,0:T(8,128)(2,1)}, bf16[1024,256]{1,0:T(8,128)(2,1)}, u32[]{:S(2)}, u32[]{:S(2)}) collective-permute-start(bf16[1024,256]{1,0:T(8,128)(2,1)} %get-tuple-element.136), channel_id=1, source_target_pairs={{0,2},{1,3},{2,0},{3,1},{4,6},{5,7},{6,4},{7,5},{8,10},{9,11},{10,... | collective-permute-start | bytes 1572872 | tf_op jit(solution)/shard_map/ppermute | solution.py:455
  524.6 97.6 %collective-permute-start.13 = (bf16[2048,256]{1,0:T(8,128)(2,1)}, bf16[2048,256]{1,0:T(8,128)(2,1)}, u32[]{:S(2)}, u32[]{:S(2)}) collective-permute-start(bf16[2048,256]{1,0:T(8,128)(2,1)} %pad_maximum_fusion.11), channel_id=1, source_target_pairs={{0,1},{1,0},{2,3},{3,2},{4,5},{5,4},{6,7},{7,6},{8,9},{9,8},{10,11... | collective-permute-start | bytes 3145736 | tf_op jit(solution)/shard_map/ppermute | solution.py:455
  527.2 95.1 %collective-permute-start.15 = (bf16[2048,256]{1,0:T(8,128)(2,1)}, bf16[2048,256]{1,0:T(8,128)(2,1)}, u32[]{:S(2)}, u32[]{:S(2)}) collective-permute-start(bf16[2048,256]{1,0:T(8,128)(2,1)} %pad_maximum_fusion.12), channel_id=1, source_target_pairs={{0,2},{1,3},{2,0},{3,1},{4,6},{5,7},{6,4},{7,5},{8,10},{9,11},{10,... | collective-permute-start | bytes 3145736 | tf_op jit(solution)/shard_map/ppermute | solution.py:455
  530.3 92.0 %collective-permute-start.32 = (bf16[2048,256]{1,0:T(8,128)(2,1)}, bf16[2048,256]{1,0:T(8,128)(2,1)}, u32[]{:S(2)}, u32[]{:S(2)}) collective-permute-start(bf16[2048,256]{1,0:T(8,128)(2,1)} %pad_maximum_fusion.15), channel_id=1, source_target_pairs={{0,1},{1,0},{2,3},{3,2},{4,5},{5,4},{6,7},{7,6},{8,9},{9,8},{10,11... | collective-permute-start | bytes 3145736 | tf_op jit(solution)/shard_map/ppermute | solution.py:455
  531.6 90.7 %collective-permute-start.34 = (bf16[2048,256]{1,0:T(8,128)(2,1)}, bf16[2048,256]{1,0:T(8,128)(2,1)}, u32[]{:S(2)}, u32[]{:S(2)}) collective-permute-start(bf16[2048,256]{1,0:T(8,128)(2,1)} %pad_maximum_fusion.16), channel_id=1, source_target_pairs={{0,2},{1,3},{2,0},{3,1},{4,6},{5,7},{6,4},{7,5},{8,10},{9,11},{10,... | collective-permute-start | bytes 3145736 | tf_op jit(solution)/shard_map/ppermute | solution.py:455
  533.3 39.9 %collective-permute-start.35 = (f32[2,8,128]{2,1,0:T(8,128)S(1)}, f32[2,8,128]{2,1,0:T(8,128)S(1)}, u32[]{:S(2)}, u32[]{:S(2)}) collective-permute-start(f32[2,8,128]{2,1,0:T(8,128)S(1)} %bitcast.80), channel_id=1, source_target_pairs={{0,1},{1,0},{2,3},{3,2},{4,5},{5,4},{6,7},{7,6},{8,9},{9,8},{10,11... | collective-permute-start | bytes 24584 | tf_op jit(solution)/shard_map/ppermute | solution.py:455
  576.3 46.0 %collective-permute-start.37 = (f32[2,8,128]{2,1,0:T(8,128)S(1)}, f32[2,8,128]{2,1,0:T(8,128)S(1)}, u32[]{:S(2)}, u32[]{:S(2)}) collective-permute-start(f32[2,8,128]{2,1,0:T(8,128)S(1)} %bitcast.82), channel_id=1, source_target_pairs={{0,3},{1,2},{2,1},{3,0},{4,7},{5,6},{6,5},{7,4},{8,11},{9,10},{10,... | collective-permute-start | bytes 24584 | tf_op jit(solution)/shard_map/ppermute | solution.py:455
  (78 other events, 1601.0 us)
Sparse Core Ops, SparseCore 0:
  10.3 26.4 all-gather.5
  39.0 39.0 all-gather.3
  80.3 47.7 all-gather.7
  321.2 49.4 reduce-scatter.7
  410.2 33.1 reduce-scatter.5
  503.5 44.6 reduce-scatter.3

commit v2 on v1

--- a/solution.py
+++ b/solution.py
@@ -231,6 +231,9 @@
             pltpu.VMEM((nseq, heads, DK, DV), F32),
         ],
         compiler_params=pltpu.CompilerParams(dimension_semantics=("arbitrary", "arbitrary")),
+        cost_estimate=pl.CostEstimate(
+            flops=seqs * length * heads * 6_000_000, bytes_accessed=seqs * length * width * 8,
+            transcendentals=0),
         name="mixer_fwd",
     )(proj, conv, rates, gain)
 
@@ -431,6 +434,9 @@
             pltpu.VMEM((nseq, heads, DK, DV), F32),
         ],
         compiler_params=pltpu.CompilerParams(dimension_semantics=("arbitrary", "arbitrary")),
+        cost_estimate=pl.CostEstimate(
+            flops=seqs * length * heads * 10_000_000, bytes_accessed=seqs * length * width * 8,
+            transcendentals=0),
         name="mixer_bwd",
     )(proj, proj, dmixed, o, u, states, invs, conv, rates, gain)
     dconv = jnp.sum(dconv.reshape(CONV, 8, qkv), axis=1)
@@ -439,12 +445,217 @@
     return dproj, dots[:, :, 0, :], dconv, drate[0], drate[1], dgain
 
 
+ROWS = 512
+
+
+def piece_specs(blocks, width):
+    half = blocks // 2
+    here = pl.BlockSpec((ROWS, width), lambda i, *_: (i, 0))
+    top = pl.BlockSpec((ROWS, width), lambda i, *_: (jnp.minimum(i, half - 1), 0))
+    low = pl.BlockSpec((ROWS, width), lambda i, *_: (jnp.maximum(i - half, 0), 0))
+    return [here, here, here, top, low]
+
+
+def row_spec(width):
+    return pl.BlockSpec((ROWS, width), lambda i, *_: (i, 0))
+
+
+def whole_spec(shape):
+    return pl.BlockSpec(shape, lambda i, *_: (0,) * len(shape))
+
+
+def send_specs(tokens, width):
+    shapes = (
+        jax.ShapeDtypeStruct((tokens, width), F32),
+        jax.ShapeDtypeStruct((3, tokens, width), BF16),
+    )
+    return shapes, (row_spec(width), pl.BlockSpec((3, ROWS, width), lambda i, *_: (0, i, 0)))
+
+
+def block_cols(order_ref, b, width):
+    return pl.ds(pl.multiple_of(order_ref[b] * width, width), width)
+
+
+def read_pieces(refs, half):
+    own_ref, x_ref, y_ref, top_ref, low_ref = refs
+    far = jnp.where(pl.program_id(0) < half, top_ref[...], low_ref[...])
+    return own_ref[...], x_ref[...], y_ref[...], far
+
+
+def norm_into(refs, half, blocks_per_seq, lens_ref, order_ref, gain_ref, normed_ref, scale_ref):
+    i = pl.program_id(0)
+    pieces = [piece.astype(F32) for piece in read_pieces(refs, half)]
+    width = pieces[0].shape[1]
+    squares = pieces[0] * pieces[0]
+    for piece in pieces[1:]:
+        squares = squares + piece * piece
+    scale = lax.rsqrt(jnp.sum(squares, axis=1, keepdims=True) * (1.0 / (4 * width)) + NORM_EPS)
+    scale_ref[...] = scale
+    at = lax.rem(i, blocks_per_seq) * ROWS + iota2((ROWS, 1), 0)
+    masked = jnp.where(at < lens_ref[i // blocks_per_seq], scale, 0.0)
+    for b, piece in enumerate(pieces):
+        cols = block_cols(order_ref, b, width)
+        normed_ref[:, cols] = (piece * masked * gain_ref[:, cols]).astype(BF16)
+
+
+def send_blocks(order_ref, left, w_ref, cols, own_ref, send_ref):
+    width = own_ref.shape[1]
+    for b in range(4):
+        part = mm_nt(left, w_ref[block_cols(order_ref, b, width), cols])
+        if b == 0:
+            own_ref[...] = part
+        else:
+            send_ref[b - 1] = part.astype(BF16)
+
+
+def project_kernel(half, blocks_per_seq, lens_ref, order_ref, *refs):
+    gain_ref, w_ref, proj_ref, normed_ref, scale_ref = refs[5:]
+    norm_into(refs[:5], half, blocks_per_seq, lens_ref, order_ref, gain_ref, normed_ref, scale_ref)
+    proj_ref[...] = mm(normed_ref[...], w_ref[...])
+
+
+def norm_project(pieces, gain, weights, lens, order, length):
+    tokens, width = pieces[0].shape
+    blocks = tokens // ROWS
+    full, out = weights.shape
+    return pl.pallas_call(
+        functools.partial(project_kernel, blocks // 2, length // ROWS),
+        out_shape=(
+            jax.ShapeDtypeStruct((tokens, out), F32),
+            jax.ShapeDtypeStruct((tokens, full), BF16),
+            jax.ShapeDtypeStruct((tokens, 1), F32),
+        ),
+        grid_spec=pltpu.PrefetchScalarGridSpec(
+            num_scalar_prefetch=2,
+            grid=(blocks,),
+            in_specs=piece_specs(blocks, width) + [whole_spec((1, full)), whole_spec((full, out))],
+            out_specs=(row_spec(out), row_spec(full), row_spec(1)),
+        ),
+        cost_estimate=pl.CostEstimate(
+            flops=2 * tokens * full * out, bytes_accessed=tokens * (out * 4 + full * 4),
+            transcendentals=tokens),
+        name="norm_project",
+    )(lens, order, *pieces, gain, weights)
+
+
+def spread_kernel(order_ref, left_ref, w_ref, own_ref, send_ref):
+    send_blocks(order_ref, left_ref[...], w_ref, slice(None), own_ref, send_ref)
+
+
+def spread_product(left, weights, order):
+    tokens, inner = left.shape
+    full = weights.shape[0]
+    shapes, specs = send_specs(tokens, full // 4)
+    return pl.pallas_call(
+        spread_kernel,
+        out_shape=shapes,
+        grid_spec=pltpu.PrefetchScalarGridSpec(
+            num_scalar_prefetch=1,
+            grid=(tokens // ROWS,),
+            in_specs=[row_spec(inner), whole_spec((full, inner))],
+            out_specs=specs,
+        ),
+        cost_estimate=pl.CostEstimate(
+            flops=2 * tokens * full * inner, bytes_accessed=tokens * (full * 3 + inner * 2),
+            transcendentals=0),
+        name="spread_product",
+    )(order, left, weights)
+
+
+def feed_kernel(half, blocks_per_seq, lens_ref, order_ref, *refs):
+    (grad_ref, gain_ref, w_ref, normed_ref, scale_ref, act_ref, both_ref, dots_ref,
+     down_ref, down_send_ref, feed_ref, feed_send_ref) = refs[5:]
+    ff = act_ref.shape[1]
+    norm_into(refs[:5], half, blocks_per_seq, lens_ref, order_ref, gain_ref, normed_ref, scale_ref)
+    gate_up = mm(normed_ref[...], w_ref[:, : 2 * ff])
+    inner_grad = mm(grad_ref[...], w_ref[:, 2 * ff :])
+    gate_act = gate_up[:, :ff]
+    up_act = gate_up[:, ff:]
+    sig = sigm(gate_act)
+    silu = gate_act * sig
+    act_ref[...] = (silu * up_act).astype(BF16)
+    gate_grad = inner_grad * up_act * (sig * (1.0 + gate_act * (1.0 - sig)))
+    up_grad = inner_grad * silu
+    both_ref[:, :ff] = gate_grad.astype(BF16)
+    both_ref[:, ff:] = up_grad.astype(BF16)
+    dots = jnp.sum(gate_grad * gate_act + up_grad * up_act, axis=1, keepdims=True)
+    dots_ref[0] = jnp.broadcast_to(dots, (ROWS, 128)).T[0:8]
+    send_blocks(order_ref, both_ref[...], w_ref, slice(0, 2 * ff), down_ref, down_send_ref)
+    send_blocks(order_ref, act_ref[...], w_ref, slice(2 * ff, 3 * ff), feed_ref, feed_send_ref)
+
+
+def feed_forward(pieces, grad_full, gain, weights, lens, order, length):
+    tokens, width = pieces[0].shape
+    blocks = tokens // ROWS
+    full, out = weights.shape
+    ff = out // 3
+    shapes, specs = send_specs(tokens, width)
+    return pl.pallas_call(
+        functools.partial(feed_kernel, blocks // 2, length // ROWS),
+        out_shape=(
+            jax.ShapeDtypeStruct((tokens, full), BF16),
+            jax.ShapeDtypeStruct((tokens, 1), F32),
+            jax.ShapeDtypeStruct((tokens, ff), BF16),
+            jax.ShapeDtypeStruct((tokens, 2 * ff), BF16),
+            jax.ShapeDtypeStruct((blocks, 8, ROWS), F32),
+        ) + shapes + shapes,
+        grid_spec=pltpu.PrefetchScalarGridSpec(
+            num_scalar_prefetch=2,
+            grid=(blocks,),
+            in_specs=piece_specs(blocks, width)
+            + [row_spec(full), whole_spec((1, full)), whole_spec((full, out))],
+            out_specs=(row_spec(full), row_spec(1), row_spec(ff), row_spec(2 * ff),
+                       pl.BlockSpec((1, 8, ROWS), lambda i, *_: (i, 0, 0))) + specs + specs,
+        ),
+        cost_estimate=pl.CostEstimate(
+            flops=4 * tokens * full * out, bytes_accessed=tokens * full * 16,
+            transcendentals=tokens * ff),
+        name="feed_forward",
+    )(lens, order, *pieces, grad_full, gain, weights)
+
+
+def join_kernel(half, order_ref, *refs):
+    w_ref, full_ref, out_ref = refs[5:]
+    pieces = read_pieces(refs[:5], half)
+    width = pieces[0].shape[1]
+    for b, piece in enumerate(pieces):
+        full_ref[:, block_cols(order_ref, b, width)] = piece
+    out_ref[...] = mm(full_ref[...], w_ref[...])
+
+
+def join_product(pieces, weights, order):
+    tokens, width = pieces[0].shape
+    blocks = tokens // ROWS
+    full, out = weights.shape
+    return pl.pallas_call(
+        functools.partial(join_kernel, blocks // 2),
+        out_shape=(
+            jax.ShapeDtypeStruct((tokens, full), BF16),
+            jax.ShapeDtypeStruct((tokens, out), F32),
+        ),
+        grid_spec=pltpu.PrefetchScalarGridSpec(
+            num_scalar_prefetch=1,
+            grid=(blocks,),
+            in_specs=piece_specs(blocks, width) + [whole_spec((full, out))],
+            out_specs=(row_spec(full), row_spec(out)),
+        ),
+        cost_estimate=pl.CostEstimate(
+            flops=2 * tokens * full * out, bytes_accessed=tokens * (full * 4 + out * 4),
+            transcendentals=0),
+        name="join_product",
+    )(order, *pieces, weights)
+
+
 D = 1024
 PARTS = 1
 
 
 def contract_rows(left, right):
     return lax.dot_general(left, right, (((0,), (0,)), ((), ())), preferred_element_type=F32)
+
+
+def after(value, *others):
+    return lax.optimization_barrier((value,) + others)[0]
 
 
 def xor_perm(size, bit):
@@ -461,35 +672,33 @@
     from_y = send_col(values, 2)
     far_top = send_col(from_y[:half], 1)
     far_low = send_col(from_x[half:], 2)
-    return jnp.concatenate(
-        [values, from_x, from_y, jnp.concatenate([far_top, far_low], axis=0)], axis=1
-    )
-
-
-def sum_features(partial):
-    width = partial.shape[1] // 4
-    half = partial.shape[0] // 2
-    own, part_x, part_y, far = [partial[:, width * i : width * i + width] for i in range(4)]
-    far = far.astype(BF16)
-    via_x = send_col(far[:half], 1).astype(F32)
-    via_y = send_col(far[half:], 2).astype(F32)
+    return values, from_x, from_y, far_top, far_low
+
+
+def sum_features(own, send, *earlier):
+    half = own.shape[0] // 2
+    via_x = send_col(send[2, :half], 1).astype(F32)
+    via_y = send_col(send[2, half:], 2).astype(F32)
+    if earlier:
+        via_x = after(via_x, *earlier)
+        via_y = after(via_y, *earlier)
+    part_x = send[0].astype(F32)
+    part_y = send[1].astype(F32)
     to_y = jnp.concatenate([part_y[:half] + via_x, part_y[half:]], axis=0).astype(BF16)
     to_x = jnp.concatenate([part_x[:half], part_x[half:] + via_y], axis=0).astype(BF16)
     return own + send_col(to_x, 1).astype(F32) + send_col(to_y, 2).astype(F32)
 
 
+def sum_direct(own, send):
+    total = own
+    for bit in range(1, 4):
+        total = total + send_col(send[bit - 1], bit).astype(F32)
+    return total
+
+
 def sum_scalars(values):
-    total = values
-    for bit in range(1, 4):
-        total = total + send_col(values, bit)
-    return total
-
-
-def col_order(values, col):
-    rows = values.shape[0] // 4
-    return jnp.concatenate(
-        [lax.dynamic_slice_in_dim(values, (col ^ b) * rows, rows, 0) for b in range(4)], axis=0
-    )
+    values = values + send_col(values, 1)
+    return values + send_col(values, 2)
 
 
 def swap_cores(mine, dp):
@@ -499,17 +708,28 @@
     )
 
 
-def gather_weight(block, dp, col):
+def gather_weight(block, dp, *earlier):
     rows = block.shape[0] // 2
     half = lax.dynamic_slice_in_dim(block, dp * rows, rows, 0)
-    return col_order(lax.all_gather(half, ("row", "dp"), axis=0, tiled=True), col)
-
-
-def scatter_weight(grad, dp, col):
-    mine = lax.psum_scatter(
-        col_order(grad.astype(BF16), col), ("row", "dp"), scatter_dimension=0, tiled=True
-    )
+    if earlier:
+        half = after(half, *earlier)
+    return lax.all_gather(half, ("row", "dp"), axis=0, tiled=True)
+
+
+def scatter_weight(grad, dp):
+    mine = lax.psum_scatter(grad, ("row", "dp"), scatter_dimension=0, tiled=True)
     return swap_cores(mine, dp).astype(F32)
+
+
+def sum_small(values):
+    count = lax.axis_size("row")
+    if count != 4:
+        return lax.psum(values, ("dp", "row"))
+    size = values.shape[0]
+    total = jnp.pad(values, (0, -size % 1024)).reshape(-1, 128)
+    total = total + lax.ppermute(total, "dp", [(0, 1), (1, 0)])
+    others = [lax.ppermute(total, "row", xor_perm(count, bit)) for bit in range(1, count)]
+    return ((total + others[0]) + (others[1] + others[2])).reshape(-1)[:size]
 
 
 def on_device(
@@ -542,116 +762,121 @@
     tokens = per_part * length
     col = lax.axis_index("col")
     dp = lax.axis_index("dp")
+    order = (col ^ jnp.arange(4, dtype=jnp.int32)).astype(jnp.int32)
     row_block = query_proj.shape[0]
     vals = heads * DV
     qkv = heads * (2 * DK + DV)
-    ff_half = hidden_gate.shape[1]
+    ff = hidden_gate.shape[1]
+    ff_pad = -ff % 128
 
     in_block = jnp.concatenate(
         [query_proj, key_proj, value_proj, gate_proj, decay_proj, beta_proj,
          jnp.zeros((row_block, 128 - 2 * heads), BF16)], axis=1)
-    in_weights = gather_weight(in_block, dp, col)
-    out_weights = gather_weight(output_proj.T, dp, col)
-    ff_weights = gather_weight(
-        jnp.concatenate([hidden_gate, hidden_up, hidden_down.T], axis=1), dp, col)
-    up_weights = ff_weights[:, : 2 * ff_half]
-    down_weights = ff_weights[:, 2 * ff_half :]
+    in_weights = gather_weight(in_block, dp)
+    positions = lax.broadcasted_iota(jnp.int32, (seq_count, length), 1)
+    valid_all = (positions < seq_lengths[:, None]).astype(F32)
+    grad_all = out_grad.astype(F32) * valid_all[:, :, None]
+    ff_block = jnp.concatenate(
+        [jnp.pad(piece, ((0, 0), (0, ff_pad)))
+         for piece in (hidden_gate, hidden_up, hidden_down.T)], axis=1)
 
     conv = jnp.concatenate([query_conv, key_conv, value_conv], axis=1).astype(F32)
     rates = rate_rows(decay_log, step_bias)
     gain_row = output_gain.astype(F32)[None]
-    first_order = col_order(first_gain.astype(F32), col)[None]
-    second_order = col_order(second_gain.astype(F32), col)[None]
-    first_local = first_order[:, :col_width]
-    second_local = second_order[:, :col_width]
-    positions = lax.broadcasted_iota(jnp.int32, (seq_count, length), 1)
-    valid_all = (positions < seq_lengths[:, None]).astype(F32)
+    first_row = first_gain.astype(F32)[None]
+    second_row = second_gain.astype(F32)[None]
+    first_local = lax.dynamic_slice_in_dim(first_row, col * col_width, col_width, 1)
+    second_local = lax.dynamic_slice_in_dim(second_row, col * col_width, col_width, 1)
 
     state = []
     for part in range(parts):
         seqs = slice(part * per_part, (part + 1) * per_part)
-        valid = valid_all[seqs].reshape(tokens, 1)
-        local_low = inputs[seqs].reshape(tokens, col_width)
-        full = gather_features(local_low).astype(F32)
-        scale = lax.rsqrt(jnp.mean(full * full, axis=1, keepdims=True) + NORM_EPS)
-        normed = (full * scale * first_order * valid).astype(BF16)
-        grad_out = out_grad[seqs].reshape(tokens, col_width).astype(F32) * valid
-        state.append(dict(valid=valid, local=local_low.astype(F32), scale=scale, normed=normed,
-                          grad_out=grad_out))
+        local = inputs[seqs].reshape(tokens, col_width)
+        state.append(dict(
+            lens=seq_lengths[seqs], valid=valid_all[seqs].reshape(tokens, 1), local=local,
+            grad_out=grad_all[seqs].reshape(tokens, col_width), pieces=gather_features(local)))
+    out_weights = gather_weight(output_proj.T, dp, state[0]["pieces"][1])
     for st in state:
-        proj = jnp.dot(st["normed"], in_weights, preferred_element_type=F32)
+        proj, st["normed"], st["scale"] = norm_project(
+            st["pieces"], first_row, in_weights, st["lens"], order, length)
         st["proj"] = proj.reshape(per_part, length, -1)
+        if st is state[0]:
+            grad_low = grad_all.astype(BF16).reshape(seq_count * length, col_width)
+            grad_full = lax.all_gather(after(grad_low, st["scale"]), "col", axis=1, tiled=True)
+            ff_weights = gather_weight(ff_block, dp, st["scale"])
         mixed, *st["saved"] = mixer_fwd(st["proj"], conv, rates, gain_row, heads, per_part)
         st["mixed"] = mixed.reshape(tokens, vals)
-        attention = sum_features(mm_nt(st["mixed"], out_weights))
-        st["hidden"] = st["local"] + attention
-        st["grad_full"] = gather_features(st["grad_out"].astype(BF16))
+        attention = sum_features(*spread_product(st["mixed"], out_weights, order))
+        st["hidden"] = st["local"].astype(F32) + attention
+        st["pieces"] = gather_features(st["hidden"].astype(BF16))
     results = []
-    ff_grad = 0.0
+    gate_up_grad = 0.0
+    down_grad = 0.0
     second_gain_grad = 0.0
-    for st in state:
-        full = gather_features(st["hidden"].astype(BF16)).astype(F32)
-        scale = lax.rsqrt(jnp.mean(full * full, axis=1, keepdims=True) + NORM_EPS)
-        normed = (full * scale * second_order * st["valid"]).astype(BF16)
-        gate_up = jnp.dot(normed, up_weights, preferred_element_type=F32)
-        gate_act = gate_up[:, :ff_half]
-        up_act = gate_up[:, ff_half:]
-        sig = jax.nn.sigmoid(gate_act)
-        silu = gate_act * sig
-        act = (silu * up_act).astype(BF16)
-        inner_grad = jnp.dot(st["grad_full"], down_weights, preferred_element_type=F32)
-        gate_grad = (inner_grad * up_act * sig * (1.0 + gate_act * (1.0 - sig))).astype(BF16)
-        up_grad = (inner_grad * silu).astype(BF16)
-        both = jnp.concatenate([gate_grad, up_grad], axis=1)
-        dots = sum_scalars(jnp.sum(
-            gate_grad.astype(F32) * gate_act + up_grad.astype(F32) * up_act, axis=1))[:, None]
-        second_grad = sum_features(mm_nt(both, up_weights)) * st["valid"]
+    for part, st in enumerate(state):
+        st["grad_full"] = grad_full[part * tokens : (part + 1) * tokens]
+        (normed, scale, act, both, dots, second_own, second_send, feed_own, feed_send
+         ) = feed_forward(st["pieces"], st["grad_full"], second_row, ff_weights, st["lens"], order,
+                          length)
+        dots = sum_scalars(dots)[:, 0, :].reshape(tokens, 1)
+        second_grad = sum_features(second_own, second_send, dots) * st["valid"]
         hat = st["hidden"] * scale
         second_gain_grad = second_gain_grad + jnp.sum(second_grad * hat, axis=0)
         st["hidden_grad"] = st["grad_out"] + scale * (
             second_grad * second_local - hat * (dots * (1.0 / D)))
-        st["attn_grad"] = gather_features(st["hidden_grad"].astype(BF16))
-        feed = sum_features(mm_nt(act, down_weights))
-        results.append(((st["hidden"] + feed) * st["valid"]).astype(BF16))
-        ff_grad = ff_grad + jnp.concatenate(
-            [contract_rows(normed, both), contract_rows(st["grad_full"], act)], axis=1)
-    ff_grad = scatter_weight(ff_grad, dp, col)
+        st["pieces"] = gather_features(st["hidden_grad"].astype(BF16))
+        hidden, feed_own, feed_send = lax.optimization_barrier(
+            (st["hidden"], feed_own, feed_send, st["pieces"][4]))[:3]
+        feed = sum_direct(feed_own, feed_send)
+        results.append(((hidden + feed) * st["valid"]).astype(BF16))
+        gate_up_grad = gate_up_grad + contract_rows(normed, both)
+        down_grad = down_grad + contract_rows(st["grad_full"], act)
+    gate_up_low = gate_up_grad.astype(BF16)
+    down_low = down_grad.astype(BF16)
+    gate_up_grad = scatter_weight(gate_up_low, dp)
+    down_grad = scatter_weight(after(down_low, gate_up_low), dp)
     out_weight_grad = 0.0
     in_weight_grad = 0.0
     first_gain_grad = 0.0
-    input_grads = []
     small = 0.0
     for st in state:
-        mixed_grad = jnp.dot(st["attn_grad"], out_weights, preferred_element_type=F32)
+        own = after(st["pieces"][0], gate_up_low, down_low)
+        st["attn_grad"], mixed_grad = join_product(
+            (own,) + st["pieces"][1:], out_weights, order)
         out_weight_grad = out_weight_grad + contract_rows(st["attn_grad"], st["mixed"])
+        if st is state[-1]:
+            out_low = out_weight_grad.astype(BF16)
+            mixed_grad = after(mixed_grad, out_low)
         dproj, dots, *grads = mixer_bwd(
             st["proj"], mixed_grad.reshape(per_part, length, vals), st["saved"], conv, rates,
             gain_row, heads, per_part)
         small = small + jnp.concatenate([grad.reshape(-1) for grad in grads])
-        dproj = dproj.reshape(tokens, -1)
-        dots = sum_scalars(dots)
-        in_weight_grad = in_weight_grad + contract_rows(st["normed"], dproj)
-        st["dots"] = dots.reshape(tokens, 1)
-        first_grad = sum_features(mm_nt(dproj, in_weights)) * st["valid"]
-        hat = st["local"] * st["scale"]
+        st["dproj"] = dproj.reshape(tokens, -1)
+        st["dots"] = sum_scalars(dots)
+        in_weight_grad = in_weight_grad + contract_rows(
+            st["normed"], after(st["dproj"], *results))
+    in_low = in_weight_grad.astype(BF16)
+    in_weight_grad = scatter_weight(after(in_low, out_low), dp)
+    at = CONV * qkv + 2 * heads
+    gain_out = sum_scalars(small[at:].reshape(2, 128)).reshape(-1)
+    small_sums = sum_small(jnp.concatenate([small[:at], second_gain_grad, gain_out]))
+    input_grads = []
+    for st in state:
+        own, send = spread_product(after(st["dproj"], in_low, st["dots"]), in_weights, order)
+        first_grad = sum_features(own, send, small_sums) * st["valid"]
+        hat = st["local"].astype(F32) * st["scale"]
         first_gain_grad = first_gain_grad + jnp.sum(first_grad * hat, axis=0)
         input_grads.append(st["hidden_grad"] + st["scale"] * (
-            first_grad * first_local - hat * (st["dots"] * (1.0 / D))))
-    out_weight_grad = scatter_weight(out_weight_grad, dp, col)
-    in_weight_grad = scatter_weight(in_weight_grad, dp, col)
-    conv_size = CONV * qkv
-    small_sums = lax.psum(
-        jnp.concatenate([small[: conv_size + 2 * heads], second_gain_grad, first_gain_grad]),
-        ("dp", "row"))
-    conv_grad = small_sums[:conv_size].reshape(CONV, qkv)
-    gain_out_grad = lax.psum(small[conv_size + 2 * heads :], ("dp", "row", "col"))
-    at = conv_size + 2 * heads
+            first_grad * first_local - hat * (st["dots"].reshape(tokens, 1) * (1.0 / D))))
+    out_weight_grad = scatter_weight(out_low, dp)
+    first_gain_grad = sum_small(first_gain_grad)
+    conv_grad = small_sums[: CONV * qkv].reshape(CONV, qkv)
     gate_at = qkv + vals
     qk = heads * DK
     return (
         jnp.concatenate(results, axis=0).reshape(seq_count, length, col_width),
         jnp.concatenate(input_grads, axis=0).reshape(seq_count, length, col_width),
-        small_sums[at + col_width : at + 2 * col_width],
+        first_gain_grad,
         in_weight_grad[:, :qk],
         in_weight_grad[:, qk : 2 * qk],
         in_weight_grad[:, 2 * qk : qkv],
@@ -661,14 +886,14 @@
         conv_grad[:, :qk],
         conv_grad[:, qk : 2 * qk],
         conv_grad[:, 2 * qk :],
-        small_sums[conv_size : conv_size + heads],
-        small_sums[conv_size + heads : at],
-        gain_out_grad,
+        small_sums[CONV * qkv : CONV * qkv + heads],
+        small_sums[CONV * qkv + heads : at],
+        small_sums[at + col_width :],
         out_weight_grad.T,
         small_sums[at : at + col_width],
-        ff_grad[:, :ff_half],
-        ff_grad[:, ff_half : 2 * ff_half],
-        ff_grad[:, 2 * ff_half :].T,
+        gate_up_grad[:, :ff],
+        gate_up_grad[:, ff + ff_pad : 2 * ff + ff_pad],
+        down_grad[:, :ff].T,
     )
 
 

time: 693 us -> 526 us (0.76)
  matrix products: 122 us -> 32.6 us
  Pallas kernels: 110 us -> 185 us
  blocking collectives: 75 us -> 0 us
  waiting for transfers between devices: 226 us -> 166 us
  other arithmetic: 69.8 us -> 36.5 us
  starting transfers between devices: 29.3 us -> 54.1 us
    dot_general x8 -> x0, matrix products: 82.4 us -> none  [the longest x4 30.6 us: mm_nt(): lax.dot_general(a, b, (((1,), (1,)), ((), ())), preferred_element_type=F32)]
    psum x2 -> x0, blocking collectives: 75 us -> none  [the longest x1 45.8 us: on_device(): lax.psum(small[conv_size + 2 * heads:], ('dp', 'row', 'col'))]
    pallas_call x0 -> x5, Pallas kernels: none -> 74.8 us  [the longest x1 32.1 us: feed_forward(): pl.pallas_call(functools.partial(feed_kernel, blocks // 2, length // ROWS...]
    ppermute x38 -> x33, waiting for transfers between devices: 212 us -> 158 us  [send_col(): return lax.ppermute(values, 'col', xor_perm(4, bit))]
    reduce_sum x2 -> x0, other arithmetic: 24.6 us -> none  [on_device(): scale = lax.rsqrt(jnp.mean(full * full, axis=1, keepdims=True) + NORM_EPS)]
    ppermute x0 -> x8, starting transfers between devices: none -> 18.4 us  [the longest x2 13 us: sum_small(): total = total + lax.ppermute(total, 'dp', [(0, 1), (1, 0)])]
    concatenate x8 -> x1, other arithmetic: 18.8 us -> 0.87 us  [on_device(): jnp.concatenate([jnp.pad(piece, ((0, 0), (0, ff_pad))) for piece in (hidd...]
    all_gather x3 -> x4, waiting for transfers between devices: 13 us -> 1.6 us  [the longest x3 1.6 us: gather_weight(): return lax.all_gather(half, ('row', 'dp'), axis=0, tiled=True)]
  transfers between devices with their start and end apart: 47 -> 53, of which waited for: 23 -> 23; matrix products, arithmetic and copies ran while one was open for 27% -> 17% of each run, Pallas kernels for 16% -> 29%
where the time goes in v2:
time: 526 us; the launch traced here: 521 us
  Pallas kernels  185 us (35%)
  waiting for transfers between devices  166 us (32%)
  starting transfers between devices  54.1 us (10%)
  other arithmetic  36.5 us (7%)
  local copies, waits for them, and re-layouts  33.2 us (6%)
  matrix products  32.6 us (6%)
  between operations  15 us (3%)
    ppermute x33, waiting for transfers between devices, send_col(): return lax.ppermute(values, 'col', xor_perm(4, bit))  158 us
    pallas_call x1, Pallas kernels, mixer_bwd(): pl.pallas_call(functools.partial(bwd_kernel, heads, nseq), out_shape=(jax...  67.1 us
    pallas_call x1, Pallas kernels, mixer_fwd(): pl.pallas_call(functools.partial(fwd_kernel, heads, nseq), out_shape=(jax...  42.6 us
    dot_general x4, matrix products, contract_rows(): lax.dot_general(left, right, (((0,), (0,)), ((), ())), preferred_element_...  32.6 us
    pallas_call x1, Pallas kernels, feed_forward(): pl.pallas_call(functools.partial(feed_kernel, blocks // 2, length // ROWS...  32.1 us
    ppermute x33, starting transfers between devices, send_col(): return lax.ppermute(values, 'col', xor_perm(4, bit))  30.5 us
    pallas_call x2, Pallas kernels, spread_product(): pl.pallas_call(spread_kernel, out_shape=shapes, grid_spec=pltpu.PrefetchS...  19.1 us
    pallas_call x1, Pallas kernels, norm_project(): pl.pallas_call(functools.partial(project_kernel, blocks // 2, length // R...  15.7 us
  transfers between devices with their start and end apart: 53, of which 23 were waited for; matrix products, arithmetic and copies ran while one was open for 17% of the time, Pallas kernels for 29%

profile of v2, /device:TPU:1, one launch (start us, length us, event | category | flops | bytes accessed | tf_op | source)
XLA Modules:
  0.0 521.5 jit_solution(7867459517564161118)
XLA Ops:
  11.3 2.1 collective-permute-start
  15.4 20.9 %collective-permute-done.refs_1_ = bf16[2048,256]{1,0:T(8,128)(2,1)} collective-permute-done((bf16[2048,256]{1,0:T(8,128)(2,1)S(1)}, bf16[2048,256]{1,0:T(8,128)(2,1)}, u32[]{:S(2)}, u32[]{:S(2)}) %collective-permute-start) | collective-permute-done | bytes 1048608 | tf_op jit(solution)/shard_map/ppermute | solution.py:666
  42.3 2.0 convert_multiply_fusion.1
  44.3 6.5 %collective-permute-done.2.refs_3_ = bf16[1024,256]{1,0:T(8,128)(2,1)S(1)} collective-permute-done((bf16[1024,256]{1,0:T(8,128)(2,1)S(1)}, bf16[1024,256]{1,0:T(8,128)(2,1)S(1)}, u32[]{:S(2)}, u32[]{:S(2)}) %collective-permute-start.2) | collective-permute-done | bytes 524320 | tf_op jit(solution)/shard_map/ppermute | solution.py:666
  50.7 1.9 collective-permute-done.3.refs_4_
  54.3 15.7 %norm_project.1 = (f32[2048,1664]{1,0:T(8,128)}, bf16[2048,1024]{1,0:T(8,128)(2,1)}, f32[2048,1]{1,0:T(8,128)}) custom-call(s32[2]{0:T(128)} %lens_ref.3, s32[4]{0:T(128)} %iota_xor_fusion.order_ref, bf16[2048,256]{1,0:T(8,128)(2,1)} %bitcast.128, bf16[2048,256]{1,0:T(8,128)(2,1)} %collective-permute-done.refs_1_, ...), custom_call_target="tpu_custom_call" | custom-call | flops 6979321856 | bytes 22020096 | tf_op jit(solution)/shard_map/norm_project/pallas_call | solution.py:521
  74.1 42.6 %mixer_fwd.1 = (bf16[2,1024,512]{2,1,0:T(8,128)(2,1)}, f32[2,1024,512]{2,1,0:T(8,128)}, bf16[2,1024,512]{2,1,0:T(8,128)(2,1)}, bf16[2,8,2,128,256]{4,3,2,1,0:T(8,128)(2,1)}, bf16[2,8,2,128,128]{4,3,2,1,0:T(8,128)(2,1)}) custom-call(f32[2,1024,1664]{2,1,0:T(8,128)} %bitcast.148, f32[4,1024]{1,0:T(4,128)} %maximum_convert_fusion.conv_ref, ...), custom_call_target="tpu_custom_call" | custom-call | flops 24576000000 | bytes 27262976 | tf_op jit(solution)/shard_map/mixer_fwd/pallas_call | solution.py:206
  116.7 6.7 %spread_product.2 = (f32[2048,256]{1,0:T(8,128)}, bf16[3,2048,256]{2,1,0:T(8,128)(2,1)}) custom-call(s32[4]{0:T(128)} %iota_xor_fusion.order_ref, bf16[2048,512]{1,0:T(8,128)(2,1)} %bitcast.154, bf16[1024,512]{1,0:T(8,128)(2,1)} %all-gather.7.cloned.1.call-done.w_ref.refs_5_), custom_call_target="tpu_custom_call" | custom-call | flops 2147483648 | bytes 8388608 | tf_op jit(solution)/shard_map/spread_product/pallas_call | solution.py:549
  127.5 14.3 %collective-permute-done.6 = bf16[1024,256]{1,0:T(8,128)(2,1)S(1)} collective-permute-done((bf16[1024,256]{1,0:T(8,128)(2,1)S(1)}, bf16[1024,256]{1,0:T(8,128)(2,1)S(1)}, u32[]{:S(2)}, u32[]{:S(2)}) %collective-permute-start.6) | collective-permute-done | bytes 524320 | tf_op jit(solution)/shard_map/ppermute | solution.py:666
  145.4 22.3 %collective-permute-done.7 = bf16[2048,256]{1,0:T(8,128)(2,1)S(1)} collective-permute-done((bf16[2048,256]{1,0:T(8,128)(2,1)S(1)}, bf16[2048,256]{1,0:T(8,128)(2,1)S(1)}, u32[]{:S(2)}, u32[]{:S(2)}) %collective-permute-start.7) | collective-permute-done | bytes 1048608 | tf_op jit(solution)/shard_map/ppermute | solution.py:666
  170.7 20.8 %collective-permute-done.9.refs_2_ = bf16[2048,256]{1,0:T(8,128)(2,1)S(1)} collective-permute-done((bf16[2048,256]{1,0:T(8,128)(2,1)S(1)}, bf16[2048,256]{1,0:T(8,128)(2,1)S(1)}, u32[]{:S(2)}, u32[]{:S(2)}) %collective-permute-start.9) | collective-permute-done | bytes 1048608 | tf_op jit(solution)/shard_map/ppermute | solution.py:666
  194.0 9.5 %collective-permute-done.10.refs_3_ = bf16[1024,256]{1,0:T(8,128)(2,1)S(1)} collective-permute-done((bf16[1024,256]{1,0:T(8,128)(2,1)S(1)}, bf16[1024,256]{1,0:T(8,128)(2,1)S(1)}, u32[]{:S(2)}, u32[]{:S(2)}) %collective-permute-start.10) | collective-permute-done | bytes 524320 | tf_op jit(solution)/shard_map/ppermute | solution.py:666
  204.3 32.1 %feed_forward.1 = (bf16[2048,1024]{1,0:T(8,128)(2,1)}, f32[2048,1]{1,0:T(8,128)}, bf16[2048,768]{1,0:T(8,128)(2,1)}, bf16[2048,1536]{1,0:T(8,128)(2,1)}, f32[4,8...) custom-call(s32[2]{0:T(128)} %lens_ref.3, ...), custom_call_target="tpu_custom_call" | custom-call | flops 19327352832 | bytes 33554432 | tf_op jit(solution)/shard_map/feed_forward/pallas_call | solution.py:593
  237.3 3.0 slice_bitcast_fusion.10
  242.5 10.2 %convolution_convert_fusion = bf16[1024,1536]{1,0:T(8,128)(2,1)} fusion(bf16[2048,1024]{1,0:T(8,128)(2,1)S(1)} %copy-done.40, bf16[2048,1536]{1,0:T(8,128)(2,1)} %get-tuple-element.84), kind=kOutput, calls=%fused_computation | convolution fusion | flops 6444023808 | bytes 13631488 | tf_op jit(solution)/shard_map/dot_general | solution.py:654
  260.4 4.7 convolution_convert_fusion.2
  266.9 11.6 %collective-permute-done.17 = bf16[2048,256]{1,0:T(8,128)(2,1)} collective-permute-done((bf16[2048,256]{1,0:T(8,128)(2,1)}, bf16[2048,256]{1,0:T(8,128)(2,1)}, u32[]{:S(2)}, u32[]{:S(2)}) %collective-permute-start.17) | collective-permute-done | bytes 1048608 | tf_op jit(solution)/shard_map/ppermute | solution.py:666
  279.8 4.4 fusion.25
  286.2 17.2 %collective-permute-done.23.refs_2_ = bf16[2048,256]{1,0:T(8,128)(2,1)S(1)} collective-permute-done((bf16[2048,256]{1,0:T(8,128)(2,1)S(1)}, bf16[2048,256]{1,0:T(8,128)(2,1)S(1)}, u32[]{:S(2)}, u32[]{:S(2)}) %collective-permute-start.23) | collective-permute-done | bytes 1048608 | tf_op jit(solution)/shard_map/ppermute | solution.py:666
  305.4 11.5 %collective-permute-done.24.refs_3_ = bf16[1024,256]{1,0:T(8,128)(2,1)S(1)} collective-permute-done((bf16[1024,256]{1,0:T(8,128)(2,1)S(1)}, bf16[1024,256]{1,0:T(8,128)(2,1)S(1)}, u32[]{:S(2)}, u32[]{:S(2)}) %collective-permute-start.24) | collective-permute-done | bytes 524320 | tf_op jit(solution)/shard_map/ppermute | solution.py:666
  317.7 7.9 %join_product.1 = (bf16[2048,1024]{1,0:T(8,128)(2,1)}, f32[2048,512]{1,0:T(8,128)}) custom-call(s32[4]{0:T(128)} %iota_xor_fusion.order_ref, bf16[2048,256]{1,0:T(8,128)(2,1)} %copy-done.10, bf16[2048,256]{1,0:T(8,128)(2,1)} %copy-done.18, bf16[2048,256]{1,0:T(8,128)(2,1)} %copy-done.17, bf16[1024,256]{1,0:T(8,128)(2,1)} %copy-done.35, ...), custom_call_target="tpu_custom_call" | custom-call | flops 2147483648 | bytes 12582912 | tf_op jit(solution)/shard_map/join_product/pallas_call | solution.py:630
  325.5 6.2 %convolution_convert_fusion.3 = bf16[1024,512]{1,0:T(8,128)(2,1)} fusion(bf16[2048,1024]{1,0:T(8,128)(2,1)} %get-tuple-element.88, bf16[2048,512]{1,0:T(8,128)(2,1)} %bitcast.155), kind=kOutput, calls=%fused_computation.19 | convolution fusion | flops 2148007936 | bytes 7340032 | tf_op jit(solution)/shard_map/dot_general | solution.py:654
  332.6 3.6 slice_bitcast_fusion.2
  338.8 67.1 %mixer_bwd.1 = (bf16[2,1024,1664]{2,1,0:T(8,128)(2,1)}, f32[2,8,8,128]{3,2,1,0:T(8,128)}, f32[32,1024]{1,0:T(8,128)}, f32[16,128]{1,0:T(8,128)}, f32[8,256]{1,0:T(8,128)}) custom-call(f32[2,1024,1664]{2,1,0:T(8,128)} %bitcast.149, f32[2,1024,1664]{2,1,0:T(8,128)} %bitcast.150, f32[2,1024,512]{2,1,0:T(8,128)} %bitcast.153, ...), custom_call_target="tpu_custom_call" | custom-call | flops 40960000000 | bytes 27262976 | tf_op jit(solution)/shard_map/mixer_bwd/pallas_call | solution.py:402
  405.9 4.2 multiply_convert_fusion
  410.9 11.5 %convolution_convert_fusion.1 = bf16[1024,1664]{1,0:T(8,128)(2,1)} fusion(bf16[2048,1024]{1,0:T(8,128)(2,1)} %get-tuple-element.95, bf16[2048,1664]{1,0:T(8,128)(2,1)S(1)} %bitcast.152), kind=kOutput, calls=%fused_computation.1 | convolution fusion | flops 6981025792 | bytes 14417920 | tf_op jit(solution)/shard_map/dot_general | solution.py:654
  429.8 12.5 %spread_product.3 = (f32[2048,256]{1,0:T(8,128)}, bf16[3,2048,256]{2,1,0:T(8,128)(2,1)}) custom-call(s32[4]{0:T(128)} %iota_xor_fusion.order_ref, bf16[2048,1664]{1,0:T(8,128)(2,1)} %bitcast.151, bf16[1024,1664]{1,0:T(8,128)(2,1)} %all-gather.5.cloned.1.call-done.refs_6_.w_ref), custom_call_target="tpu_custom_call" | custom-call | flops 6979321856 | bytes 13107200 | tf_op jit(solution)/shard_map/spread_product/pallas_call | solution.py:549
  445.4 10.6 %collective-permute-start.30 = (f32[40,128]{1,0:T(8,128)S(1)}, f32[40,128]{1,0:T(8,128)S(1)}, u32[]{:S(2)}, u32[]{:S(2)}) collective-permute-start(f32[40,128]{1,0:T(8,128)S(1)} %pad_bitcast_fusion), channel_id=1, source_target_pairs={{0,16},{16,0},{1,17},{17,1},{2,18},{18,2},{3,19},{19,3},{4,20},{20... | collective-permute-start | bytes 61448 | tf_op jit(solution)/shard_map/ppermute | solution.py:730
  459.5 2.8 collective-permute-done.32
  475.2 15.0 %collective-permute-done.36 = bf16[2048,256]{1,0:T(8,128)(2,1)} collective-permute-done((bf16[2048,256]{1,0:T(8,128)(2,1)}, bf16[2048,256]{1,0:T(8,128)(2,1)}, u32[]{:S(2)}, u32[]{:S(2)}) %collective-permute-start.36) | collective-permute-done | bytes 1048608 | tf_op jit(solution)/shard_map/ppermute | solution.py:666
  491.6 3.7 fusion.5
  495.3 2.5 collective-permute-start.37
  (268 shorter events, 99.1 us)
Async XLA Ops:
  7.2 47.1 %all-gather.5.cloned.1.call-start = ((), (), s32[]{:S(2)}) async-start(), calls=%async_computation.4 | async-start | bytes 3833856 | tf_op jit(solution)/shard_map/all_gather | solution.py:716
  11.2 105.5 %all-gather.7.cloned.1.call-start = ((), (), s32[]{:S(2)}) async-start(), calls=%async_computation.5 | async-start | bytes 1179648 | tf_op jit(solution)/shard_map/all_gather | solution.py:716
  11.3 25.1 %collective-permute-start = (bf16[2048,256]{1,0:T(8,128)(2,1)S(1)}, bf16[2048,256]{1,0:T(8,128)(2,1)}, u32[]{:S(2)}, u32[]{:S(2)}) collective-permute-start(bf16[2048,256]{1,0:T(8,128)(2,1)S(1)} %bitcast.129), channel_id=1, source_target_pairs={{0,1},{1,0},{2,3},{3,2},{4,5},{5,4},{6,7},{7,6},{8,9},{9,8},{10,11... | collective-permute-start | bytes 3145736 | tf_op jit(solution)/shard_map/ppermute | solution.py:666
  13.4 24.2 %collective-permute-start.1 = (bf16[2048,256]{1,0:T(8,128)(2,1)S(1)}, bf16[2048,256]{1,0:T(8,128)(2,1)}, u32[]{:S(2)}, u32[]{:S(2)}) collective-permute-start(bf16[2048,256]{1,0:T(8,128)(2,1)S(1)} %bitcast.130), channel_id=1, source_target_pairs={{0,2},{1,3},{2,0},{3,1},{4,6},{5,7},{6,4},{7,5},{8,10},{9,11},{10,... | collective-permute-start | bytes 3145736 | tf_op jit(solution)/shard_map/ppermute | solution.py:666
  36.4 167.9 %all-gather.9.cloned.1.call-start = ((), (), s32[]{:S(2)}) async-start(), calls=%async_computation.6 | async-start | bytes 5242880 | tf_op jit(solution)/shard_map/all_gather | solution.py:805
  70.0 134.2 %all-gather.11.cloned.1.call-start = ((), (), s32[]{:S(2)}) async-start(), calls=%async_computation.7 | async-start | bytes 5308416 | tf_op jit(solution)/shard_map/all_gather | solution.py:716
  72.1 398.8 %reduce-scatter.11.cloned.1.call-start = ((), (), s32[]{:S(2)}) async-start(), calls=%async_computation.11 | async-start | bytes 1769472 | tf_op jit(solution)/shard_map/reduce_scatter | solution.py:720
  125.0 16.8 %collective-permute-start.6 = (bf16[1024,256]{1,0:T(8,128)(2,1)S(1)}, bf16[1024,256]{1,0:T(8,128)(2,1)S(1)}, u32[]{:S(2)}, u32[]{:S(2)}) collective-permute-start(bf16[1024,256]{1,0:T(8,128)(2,1)S(1)} %get-tuple-element.176), channel_id=1, source_target_pairs={{0,1},{1,0},{2,3},{3,2},{4,5},{5,4},{6,7},{7,6},{8,9},{9,8},{10,11... | collective-permute-start | bytes 1572872 | tf_op jit(solution)/shard_map/ppermute | solution.py:666
  126.2 15.8 %collective-permute-start.4 = (bf16[1024,256]{1,0:T(8,128)(2,1)S(1)}, bf16[1024,256]{1,0:T(8,128)(2,1)S(1)}, u32[]{:S(2)}, u32[]{:S(2)}) collective-permute-start(bf16[1024,256]{1,0:T(8,128)(2,1)S(1)} %get-tuple-element.177), channel_id=1, source_target_pairs={{0,2},{1,3},{2,0},{3,1},{4,6},{5,7},{6,4},{7,5},{8,10},{9,11},{10,... | collective-permute-start | bytes 1572872 | tf_op jit(solution)/shard_map/ppermute | solution.py:666
  143.6 24.1 %collective-permute-start.7 = (bf16[2048,256]{1,0:T(8,128)(2,1)S(1)}, bf16[2048,256]{1,0:T(8,128)(2,1)S(1)}, u32[]{:S(2)}, u32[]{:S(2)}) collective-permute-start(bf16[2048,256]{1,0:T(8,128)(2,1)S(1)} %pad_maximum_fusion.1), channel_id=1, source_target_pairs={{0,2},{1,3},{2,0},{3,1},{4,6},{5,7},{6,4},{7,5},{8,10},{9,11},{10,... | collective-permute-start | bytes 3145736 | tf_op jit(solution)/shard_map/ppermute | solution.py:666
  144.8 23.6 %collective-permute-start.5 = (bf16[2048,256]{1,0:T(8,128)(2,1)S(1)}, bf16[2048,256]{1,0:T(8,128)(2,1)S(1)}, u32[]{:S(2)}, u32[]{:S(2)}) collective-permute-start(bf16[2048,256]{1,0:T(8,128)(2,1)S(1)} %pad_maximum_fusion), channel_id=1, source_target_pairs={{0,1},{1,0},{2,3},{3,2},{4,5},{5,4},{6,7},{7,6},{8,9},{9,8},{10,11... | collective-permute-start | bytes 3145736 | tf_op jit(solution)/shard_map/ppermute | solution.py:666
  168.9 22.7 %collective-permute-start.9 = (bf16[2048,256]{1,0:T(8,128)(2,1)S(1)}, bf16[2048,256]{1,0:T(8,128)(2,1)S(1)}, u32[]{:S(2)}, u32[]{:S(2)}) collective-permute-start(bf16[2048,256]{1,0:T(8,128)(2,1)S(1)} %get-tuple-element.154.refs_0_), channel_id=1, source_target_pairs={{0,2},{1,3},{2,0},{3,1},{4,6},{5,7},{6,4},{7,5},{8,10},{9,11},{10,... | collective-permute-start | bytes 3145736 | tf_op jit(solution)/shard_map/ppermute | solution.py:666
  169.8 23.0 %collective-permute-start.8 = (bf16[2048,256]{1,0:T(8,128)(2,1)S(1)}, bf16[2048,256]{1,0:T(8,128)(2,1)S(1)}, u32[]{:S(2)}, u32[]{:S(2)}) collective-permute-start(bf16[2048,256]{1,0:T(8,128)(2,1)S(1)} %get-tuple-element.154.refs_0_), channel_id=1, source_target_pairs={{0,1},{1,0},{2,3},{3,2},{4,5},{5,4},{6,7},{7,6},{8,9},{9,8},{10,11... | collective-permute-start | bytes 3145736 | tf_op jit(solution)/shard_map/ppermute | solution.py:666
  240.4 12.3 %collective-permute-start.16 = (bf16[1024,256]{1,0:T(8,128)(2,1)}, bf16[1024,256]{1,0:T(8,128)(2,1)}, u32[]{:S(2)}, u32[]{:S(2)}) collective-permute-start(bf16[1024,256]{1,0:T(8,128)(2,1)} %get-tuple-element.170), channel_id=1, source_target_pairs={{0,1},{1,0},{2,3},{3,2},{4,5},{5,4},{6,7},{7,6},{8,9},{9,8},{10,11... | collective-permute-start | bytes 1572872 | tf_op jit(solution)/shard_map/ppermute | solution.py:666
  240.9 12.9 %collective-permute-start.12 = (bf16[1024,256]{1,0:T(8,128)(2,1)}, bf16[1024,256]{1,0:T(8,128)(2,1)}, u32[]{:S(2)}, u32[]{:S(2)}) collective-permute-start(bf16[1024,256]{1,0:T(8,128)(2,1)} %get-tuple-element.171), channel_id=1, source_target_pairs={{0,2},{1,3},{2,0},{3,1},{4,6},{5,7},{6,4},{7,5},{8,10},{9,11},{10,... | collective-permute-start | bytes 1572872 | tf_op jit(solution)/shard_map/ppermute | solution.py:666
  257.7 20.7 %collective-permute-start.17 = (bf16[2048,256]{1,0:T(8,128)(2,1)}, bf16[2048,256]{1,0:T(8,128)(2,1)}, u32[]{:S(2)}, u32[]{:S(2)}) collective-permute-start(bf16[2048,256]{1,0:T(8,128)(2,1)} %pad_maximum_fusion.3), channel_id=1, source_target_pairs={{0,2},{1,3},{2,0},{3,1},{4,6},{5,7},{6,4},{7,5},{8,10},{9,11},{10,... | collective-permute-start | bytes 3145736 | tf_op jit(solution)/shard_map/ppermute | solution.py:666
  259.4 20.4 %collective-permute-start.15 = (bf16[2048,256]{1,0:T(8,128)(2,1)}, bf16[2048,256]{1,0:T(8,128)(2,1)}, u32[]{:S(2)}, u32[]{:S(2)}) collective-permute-start(bf16[2048,256]{1,0:T(8,128)(2,1)} %pad_maximum_fusion.2), channel_id=1, source_target_pairs={{0,1},{1,0},{2,3},{3,2},{4,5},{5,4},{6,7},{7,6},{8,9},{9,8},{10,11... | collective-permute-start | bytes 3145736 | tf_op jit(solution)/shard_map/ppermute | solution.py:666
  265.2 233.8 %reduce-scatter.7.cloned.1.call-start = ((), (), s32[]{:S(2)}) async-start(), calls=%async_computation.9 | async-start | bytes 1179648 | tf_op jit(solution)/shard_map/reduce_scatter | solution.py:720
  284.2 19.2 %collective-permute-start.23 = (bf16[2048,256]{1,0:T(8,128)(2,1)S(1)}, bf16[2048,256]{1,0:T(8,128)(2,1)S(1)}, u32[]{:S(2)}, u32[]{:S(2)}) collective-permute-start(bf16[2048,256]{1,0:T(8,128)(2,1)S(1)} %get-tuple-element.86.refs_0_), channel_id=1, source_target_pairs={{0,2},{1,3},{2,0},{3,1},{4,6},{5,7},{6,4},{7,5},{8,10},{9,11},{10,... | collective-permute-start | bytes 3145736 | tf_op jit(solution)/shard_map/ppermute | solution.py:666
  285.2 19.4 %collective-permute-start.18 = (bf16[2048,256]{1,0:T(8,128)(2,1)S(1)}, bf16[2048,256]{1,0:T(8,128)(2,1)S(1)}, u32[]{:S(2)}, u32[]{:S(2)}) collective-permute-start(bf16[2048,256]{1,0:T(8,128)(2,1)S(1)} %get-tuple-element.86.refs_0_), channel_id=1, source_target_pairs={{0,1},{1,0},{2,3},{3,2},{4,5},{5,4},{6,7},{7,6},{8,9},{9,8},{10,11... | collective-permute-start | bytes 3145736 | tf_op jit(solution)/shard_map/ppermute | solution.py:666
  303.4 13.4 %collective-permute-start.24 = (bf16[1024,256]{1,0:T(8,128)(2,1)S(1)}, bf16[1024,256]{1,0:T(8,128)(2,1)S(1)}, u32[]{:S(2)}, u32[]{:S(2)}) collective-permute-start(bf16[1024,256]{1,0:T(8,128)(2,1)S(1)} %slice.327), channel_id=1, source_target_pairs={{0,1},{1,0},{2,3},{3,2},{4,5},{5,4},{6,7},{7,6},{8,9},{9,8},{10,11... | collective-permute-start | bytes 1572872 | tf_op jit(solution)/shard_map/ppermute | solution.py:666
  304.6 13.1 %collective-permute-start.19 = (bf16[1024,256]{1,0:T(8,128)(2,1)S(1)}, bf16[1024,256]{1,0:T(8,128)(2,1)}, u32[]{:S(2)}, u32[]{:S(2)}) collective-permute-start(bf16[1024,256]{1,0:T(8,128)(2,1)S(1)} %slice.326), channel_id=1, source_target_pairs={{0,2},{1,3},{2,0},{3,1},{4,6},{5,7},{6,4},{7,5},{8,10},{9,11},{10,... | collective-permute-start | bytes 1572872 | tf_op jit(solution)/shard_map/ppermute | solution.py:666
  331.8 172.0 %reduce-scatter.9.cloned.1.call-start = ((), (), s32[]{:S(2)}) async-start(), calls=%async_computation.10 | async-start | bytes 3538944 | tf_op jit(solution)/shard_map/reduce_scatter | solution.py:720
  332.5 173.1 %reduce-scatter.5.cloned.1.call-start = ((), (), s32[]{:S(2)}) async-start(), calls=%async_computation.8 | async-start | bytes 3833856 | tf_op jit(solution)/shard_map/reduce_scatter | solution.py:720
  336.2 69.7 %collective-permute-start.20 = (bf16[2048,256]{1,0:T(8,128)(2,1)}, bf16[2048,256]{1,0:T(8,128)(2,1)}, u32[]{:S(2)}, u32[]{:S(2)}) collective-permute-start(bf16[2048,256]{1,0:T(8,128)(2,1)} %get-tuple-element.165), channel_id=1, source_target_pairs={{0,1},{1,0},{2,3},{3,2},{4,5},{5,4},{6,7},{7,6},{8,9},{9,8},{10,11... | collective-permute-start | bytes 3145736 | tf_op jit(solution)/shard_map/ppermute | solution.py:666
  337.1 68.9 %collective-permute-start.22 = (bf16[2048,256]{1,0:T(8,128)(2,1)}, bf16[2048,256]{1,0:T(8,128)(2,1)}, u32[]{:S(2)}, u32[]{:S(2)}) collective-permute-start(bf16[2048,256]{1,0:T(8,128)(2,1)} %get-tuple-element.166), channel_id=1, source_target_pairs={{0,3},{1,2},{2,1},{3,0},{4,7},{5,6},{6,5},{7,4},{8,11},{9,10},{10,... | collective-permute-start | bytes 3145736 | tf_op jit(solution)/shard_map/ppermute | solution.py:666
  338.1 67.9 %collective-permute-start.21 = (bf16[2048,256]{1,0:T(8,128)(2,1)}, bf16[2048,256]{1,0:T(8,128)(2,1)}, u32[]{:S(2)}, u32[]{:S(2)}) collective-permute-start(bf16[2048,256]{1,0:T(8,128)(2,1)} %get-tuple-element.167), channel_id=1, source_target_pairs={{0,2},{1,3},{2,0},{3,1},{4,6},{5,7},{6,4},{7,5},{8,10},{9,11},{10,... | collective-permute-start | bytes 3145736 | tf_op jit(solution)/shard_map/ppermute | solution.py:666
  444.0 19.7 %collective-permute-start.35 = (bf16[1024,256]{1,0:T(8,128)(2,1)S(1)}, bf16[1024,256]{1,0:T(8,128)(2,1)S(1)}, u32[]{:S(2)}, u32[]{:S(2)}) collective-permute-start(bf16[1024,256]{1,0:T(8,128)(2,1)S(1)} %get-tuple-element.161), channel_id=1, source_target_pairs={{0,1},{1,0},{2,3},{3,2},{4,5},{5,4},{6,7},{7,6},{8,9},{9,8},{10,11... | collective-permute-start | bytes 1572872 | tf_op jit(solution)/shard_map/ppermute | solution.py:666
  444.6 19.2 %collective-permute-start.27 = (bf16[1024,256]{1,0:T(8,128)(2,1)S(1)}, bf16[1024,256]{1,0:T(8,128)(2,1)S(1)}, u32[]{:S(2)}, u32[]{:S(2)}) collective-permute-start(bf16[1024,256]{1,0:T(8,128)(2,1)S(1)} %get-tuple-element.162), channel_id=1, source_target_pairs={{0,2},{1,3},{2,0},{3,1},{4,6},{5,7},{6,4},{7,5},{8,10},{9,11},{10,... | collective-permute-start | bytes 1572872 | tf_op jit(solution)/shard_map/ppermute | solution.py:666
  466.5 23.8 %collective-permute-start.36 = (bf16[2048,256]{1,0:T(8,128)(2,1)}, bf16[2048,256]{1,0:T(8,128)(2,1)}, u32[]{:S(2)}, u32[]{:S(2)}) collective-permute-start(bf16[2048,256]{1,0:T(8,128)(2,1)} %pad_maximum_fusion.5), channel_id=1, source_target_pairs={{0,2},{1,3},{2,0},{3,1},{4,6},{5,7},{6,4},{7,5},{8,10},{9,11},{10,... | collective-permute-start | bytes 3145736 | tf_op jit(solution)/shard_map/ppermute | solution.py:666
  468.2 23.4 %collective-permute-start.34 = (bf16[2048,256]{1,0:T(8,128)(2,1)}, bf16[2048,256]{1,0:T(8,128)(2,1)}, u32[]{:S(2)}, u32[]{:S(2)}) collective-permute-start(bf16[2048,256]{1,0:T(8,128)(2,1)} %pad_maximum_fusion.4), channel_id=1, source_target_pairs={{0,1},{1,0},{2,3},{3,2},{4,5},{5,4},{6,7},{7,6},{8,9},{9,8},{10,11... | collective-permute-start | bytes 3145736 | tf_op jit(solution)/shard_map/ppermute | solution.py:666
  470.9 26.9 %collective-permute-start.44 = (bf16[128,768]{1,0:T(8,128)(2,1)}, bf16[128,768]{1,0:T(8,128)(2,1)S(1)}, u32[]{:S(2)}, u32[]{:S(2)}) collective-permute-start(bf16[128,768]{1,0:T(8,128)(2,1)} %reduce-scatter.11.cloned.1.call-done), channel_id=1, source_target_pairs={{0,16},{16,0},{1,17},{17,1},{2,18},{18,2},{3,19},{19,3},{4,20},{20... | collective-permute-start | bytes 589832 | tf_op jit(solution)/shard_map/ppermute | solution.py:705
  (62 other events, 463.3 us)
Sparse Core Ops, SparseCore 0:
  11.3 42.9 all-gather.4
  56.5 20.9 all-gather.6
  79.3 54.4 all-gather.8
  135.8 53.2 all-gather.10
  265.3 33.6 reduce-scatter.10
  331.9 33.6 reduce-scatter.6
  367.9 39.5 reduce-scatter.8
  422.5 47.2 reduce-scatter.4

commit v3 on v2

--- a/solution.py
+++ b/solution.py
@@ -17,11 +17,11 @@
 BF16 = jnp.bfloat16
 
 
-def mm(a, b):
+def mm1(a, b):
     return lax.dot_general(a, b, (((1,), (0,)), ((), ())), preferred_element_type=F32)
 
 
-def mm_nt(a, b):
+def nt1(a, b):
     return lax.dot_general(a, b, (((1,), (1,)), ((), ())), preferred_element_type=F32)
 
 
@@ -30,14 +30,32 @@
     return hi, (a - hi.astype(F32)).astype(BF16)
 
 
-def mm3(a, b):
+def mm(a, b):
     ah, al = halves(a)
     bh, bl = halves(b)
-    return mm(ah, bh) + (mm(ah, bl) + mm(al, bh))
+    return mm1(jnp.concatenate([ah, al, ah], axis=1), jnp.concatenate([bh, bh, bl], axis=0))
+
+
+def mm_nt(a, b):
+    ah, al = halves(a)
+    bh, bl = halves(b)
+    return nt1(jnp.concatenate([ah, al, ah], axis=1), jnp.concatenate([bh, bh, bl], axis=1))
+
+
+def mm_sum(a, b):
+    ah, al = halves(a)
+    bh, bl = halves(b)
+    return mm1(ah, bh) + (mm1(ah, bl) + mm1(al, bh))
+
+
+def mm_nt_sum(a, b):
+    ah, al = halves(a)
+    bh, bl = halves(b)
+    return nt1(ah, bh) + (nt1(ah, bl) + nt1(al, bh))
 
 
 def sigm(v):
-    return 1.0 / (1.0 + jnp.exp(-v))
+    return 0.5 * jnp.tanh(0.5 * v) + 0.5
 
 
 def iota2(shape, axis):
@@ -84,15 +102,15 @@
         zero32 = jnp.zeros((SUB, BLK), F32)
         off = jnp.where((row_i // 64 == col_i // 64) & (row_i // SUB > col_i // SUB), mat, 0.0)
         lhs = jnp.concatenate([off[32:64], off[96:128]], axis=0)
-        part = mm3(lhs, inv)
+        part = mm(lhs, inv)
         placed = jnp.concatenate([zero32, part[:32], zero32, part[32:]], axis=0)
         lhs = jnp.concatenate([inv[32:64], inv[96:128]], axis=0)
-        part = mm3(lhs, placed)
+        part = mm(lhs, placed)
         inv = inv - jnp.concatenate([zero32, part[:32], zero32, part[32:]], axis=0)
         off = jnp.where(col_i[64:] < 64, mat[64:], 0.0)
-        part = mm3(off, inv)
+        part = mm(off, inv)
         zero64 = jnp.zeros((64, BLK), F32)
-        part = mm3(inv[64:], jnp.concatenate([zero64, part], axis=0))
+        part = mm(inv[64:], jnp.concatenate([zero64, part], axis=0))
         inv = jnp.concatenate([inv[:64], inv[64:] - part], axis=0)
         out.append(inv)
     return out
@@ -110,7 +128,7 @@
     rest = log_decay - hi.astype(F32)
     mid = rest.astype(BF16)
     low = (rest - mid.astype(F32)).astype(BF16)
-    cum = mm(tri, hi) + (mm(tri, mid) + mm(tri, low))
+    cum = mm1(tri, hi) + (mm1(tri, mid) + mm1(tri, low))
     return log_decay, beta, cum
 
 
@@ -158,8 +176,8 @@
             cum_row = cum_t[h : h + 1, :]
             beta = beta_all[:, heads + h : heads + h + 1]
             ratio = jnp.exp(jnp.where(row_i >= col_i, cum - cum_row, -1e30))
-            kb = kn.astype(BF16)
-            kq = jnp.concatenate([kb, qn.astype(BF16)], axis=0)
+            kb = kn
+            kq = jnp.concatenate([kb, qn], axis=0)
             gram = mm_nt(kq, kb)
             a = jnp.where(row_i > col_i, gram[:BLK] * ratio * beta, 0.0)
             p = gram[BLK:] * ratio
@@ -172,12 +190,12 @@
     for item, inv in zip(items, invs):
         s, h, kq, a, p, kd, v, beta, ecum, elast = item
         state = state_ref[s, h]
-        low_state = state.astype(BF16)
+        low_state = state
         ks_qs = mm(kq, low_state)
         x = beta * (v - ecum * ks_qs[:BLK])
-        inv_low = inv.astype(BF16)
-        u = mm(inv_low, x.astype(BF16)).astype(BF16)
-        pk = jnp.concatenate([p, kd.T], axis=0).astype(BF16)
+        inv_low = inv
+        u = mm(inv_low, x)
+        pk = jnp.concatenate([p, kd.T], axis=0)
         pu = mm(pk, u)
         o = ecum * ks_qs[BLK:] + pu[:BLK]
         state_ref[s, h] = elast * state + pu[BLK:]
@@ -208,9 +226,9 @@
         out_shape=(
             jax.ShapeDtypeStruct((seqs, length, vals), BF16),
             jax.ShapeDtypeStruct((seqs, length, vals), F32),
-            jax.ShapeDtypeStruct((seqs, length, vals), BF16),
-            jax.ShapeDtypeStruct((seqs, blocks, heads, DK, DV), BF16),
-            jax.ShapeDtypeStruct((seqs, blocks, heads, BLK, BLK), BF16),
+            jax.ShapeDtypeStruct((seqs, length, vals), F32),
+            jax.ShapeDtypeStruct((seqs, blocks, heads, DK, DV), F32),
+            jax.ShapeDtypeStruct((seqs, blocks, heads, BLK, BLK), F32),
         ),
         grid=(seqs // nseq, blocks),
         in_specs=[
@@ -303,9 +321,9 @@
             elast = jnp.exp(last)
             ratio = jnp.exp(jnp.where(lower, cum - cum_row, -1e30))
             ktail = jnp.exp(last - cum)
-            kb = kn.astype(BF16)
-            qb = qn.astype(BF16)
-            gram = mm_nt(jnp.concatenate([kb, qb], axis=0), kb)
+            kb = kn
+            qb = qn
+            gram = mm_nt_sum(jnp.concatenate([kb, qb], axis=0), kb)
             sfac = jnp.where(strict, ratio * beta, 0.0)
             kgr = gram[:BLK]
             p = gram[BLK:] * ratio
@@ -324,36 +342,36 @@
             dots = dots + jnp.sum(dgate * g, axis=1, keepdims=True)
             dn = dm * gain * gsil
             do = ro * (dn - n * jnp.mean(dn * n, axis=1, keepdims=True))
-            dob = do.astype(BF16)
+            dob = do
             dstate = dstate_ref[s, h]
-            dstb = dstate.astype(BF16)
+            dstb = dstate
             u = u_ref[s, :, cols]
             sb = s_ref[s, 0, h]
             tinv = t_ref[s, 0, h]
             kd = kn * ktail
-            du = mm(jnp.concatenate([p.T, kd], axis=1).astype(BF16), jnp.concatenate([dob, dstb], axis=0))
-            dx = mm(tinv.astype(F32).T.astype(BF16), du.astype(BF16))
-            dxb = dx.astype(BF16)
+            du = mm_sum(jnp.concatenate([p.T, kd], axis=1), jnp.concatenate([dob, dstb], axis=0))
+            dx = mm_sum(tinv.astype(F32).T, du)
+            dxb = dx
             ddx = jnp.concatenate([dob, dxb], axis=0)
-            both = mm_nt(ddx, jnp.concatenate([sb, u], axis=0))
+            both = mm_nt_sum(ddx, jnp.concatenate([sb, u], axis=0))
             be = beta * ecum
             z = both[BLK:, :DK]
             dqi = ecum * both[:BLK, :DK]
             dki = -be * z
             dks = -be * dx
-            lhs = jnp.concatenate([qn.T, kn.T], axis=1).astype(BF16)
-            rhs = jnp.concatenate([(ecum * do).astype(BF16), dks.astype(BF16)], axis=0)
-            dstate_ref[s, h] = elast * dstate + mm(lhs, rhs)
-            dkd = mm_nt(u, dstb)
+            lhs = jnp.concatenate([qn.T, kn.T], axis=1)
+            rhs = jnp.concatenate([(ecum * do), dks], axis=0)
+            dstate_ref[s, h] = elast * dstate + mm_sum(lhs, rhs)
+            dkd = mm_nt_sum(u, dstb)
             dp = both[:BLK, DK:]
             da = -both[BLK:, DK:]
             dqk = dp * ratio
             dkg = da * sfac
             dlog = dp * p + dkg * kgr
-            pair = jnp.concatenate([dqk, dkg + dkg.T], axis=0).astype(BF16)
-            prod = mm(pair, kb)
+            pair = jnp.concatenate([dqk, dkg + dkg.T], axis=0)
+            prod = mm_sum(pair, kb)
             dqn = dqi + prod[:BLK]
-            dkn = dki + prod[BLK:] + mm(dqk.T.astype(BF16), qb) + dkd * ktail
+            dkn = dki + prod[BLK:] + mm_sum(dqk.T, qb) + dkd * ktail
             kz = jnp.sum(kn * z, axis=1, keepdims=True)
             dkdk = jnp.sum(dkd * kd, axis=1, keepdims=True)
             row_sum = jnp.sum(dlog, axis=1, keepdims=True)
@@ -371,7 +389,7 @@
             dact[2 * heads + h] = beta * dx
         tri = jnp.where(col_i >= row_i, 1.0, 0.0).astype(BF16)
         hi, lo = halves(dcum_all)
-        dlog_decay = mm(tri, hi) + mm(tri, lo)
+        dlog_decay = mm1(tri, hi) + mm1(tri, lo)
         dpre_a = dlog_decay * neg_rate * sigm(ab + bias)
         dpre_b = dbeta_all * beta_all * (1.0 - beta_all)
         dproj_ref[s, :, ab_at : ab_at + 128] = (dpre_a + dpre_b).astype(BF16)
@@ -391,13 +409,17 @@
         ds_ref[s, BLK : BLK + 8, :] = ds_ref[s, 0:8, :]
 
 
-def mixer_bwd(proj, dmixed, saved, conv, rates, gain, heads, nseq):
+def mixer_bwd(proj, dmixed, saved, conv, rates, gain, heads, nseq, seq):
     o, u, states, invs = saved
-    seqs, length, width = proj.shape
+    _, length, width = proj.shape
+    seqs = dmixed.shape[0]
+    first = seq // nseq
     blocks = length // BLK
     qkv = heads * (2 * DK + DV)
     vals = heads * DV
     tok = lambda i, c: (i, blocks - 1 - c, 0)
+    all_tok = lambda i, c: (i + first, blocks - 1 - c, 0)
+    all_blk = lambda i, c: (i + first, blocks - 1 - c, 0, 0, 0)
     whole = lambda i, c: (0, 0)
     dproj, dots, dconv, drate, dgain = pl.pallas_call(
         functools.partial(bwd_kernel, heads, nseq),
@@ -410,13 +432,14 @@
         ),
         grid=(seqs // nseq, blocks),
         in_specs=[
-            pl.BlockSpec((nseq, BLK, width), tok),
-            pl.BlockSpec((nseq, 8, qkv), lambda i, c: (i, jnp.maximum((blocks - 1 - c) * (BLK // 8) - 1, 0), 0)),
+            pl.BlockSpec((nseq, BLK, width), all_tok),
+            pl.BlockSpec((nseq, 8, qkv), lambda i, c: (
+                i + first, jnp.maximum((blocks - 1 - c) * (BLK // 8) - 1, 0), 0)),
             pl.BlockSpec((nseq, BLK, vals), tok),
-            pl.BlockSpec((nseq, BLK, vals), tok),
-            pl.BlockSpec((nseq, BLK, vals), tok),
-            pl.BlockSpec((nseq, 1, heads, DK, DV), lambda i, c: (i, blocks - 1 - c, 0, 0, 0)),
-            pl.BlockSpec((nseq, 1, heads, BLK, BLK), lambda i, c: (i, blocks - 1 - c, 0, 0, 0)),
+            pl.BlockSpec((nseq, BLK, vals), all_tok),
+            pl.BlockSpec((nseq, BLK, vals), all_tok),
+            pl.BlockSpec((nseq, 1, heads, DK, DV), all_blk),
+            pl.BlockSpec((nseq, 1, heads, BLK, BLK), all_blk),
             pl.BlockSpec((CONV, qkv), whole),
             pl.BlockSpec((2, 128), whole),
             pl.BlockSpec((1, DV), whole),
@@ -448,12 +471,18 @@
 ROWS = 512
 
 
-def piece_specs(blocks, width):
+def half_specs(blocks, width):
     half = blocks // 2
-    here = pl.BlockSpec((ROWS, width), lambda i, *_: (i, 0))
     top = pl.BlockSpec((ROWS, width), lambda i, *_: (jnp.minimum(i, half - 1), 0))
     low = pl.BlockSpec((ROWS, width), lambda i, *_: (jnp.maximum(i - half, 0), 0))
-    return [here, here, here, top, low]
+    return [top, low]
+
+
+def piece_specs(blocks, width, count):
+    here = [pl.BlockSpec((ROWS, width), lambda i, *_: (i, 0))]
+    if count == 5:
+        return here * 3 + half_specs(blocks, width)
+    return here + half_specs(blocks, width) * 3
 
 
 def row_spec(width):
@@ -477,9 +506,10 @@
 
 
 def read_pieces(refs, half):
-    own_ref, x_ref, y_ref, top_ref, low_ref = refs
-    far = jnp.where(pl.program_id(0) < half, top_ref[...], low_ref[...])
-    return own_ref[...], x_ref[...], y_ref[...], far
+    upper = pl.program_id(0) < half
+    first = 3 if len(refs) == 5 else 1
+    halves = [jnp.where(upper, refs[i][...], refs[i + 1][...]) for i in range(first, len(refs), 2)]
+    return [ref[...] for ref in refs[:first]] + halves
 
 
 def norm_into(refs, half, blocks_per_seq, lens_ref, order_ref, gain_ref, normed_ref, scale_ref):
@@ -501,7 +531,7 @@
 def send_blocks(order_ref, left, w_ref, cols, own_ref, send_ref):
     width = own_ref.shape[1]
     for b in range(4):
-        part = mm_nt(left, w_ref[block_cols(order_ref, b, width), cols])
+        part = nt1(left, w_ref[block_cols(order_ref, b, width), cols])
         if b == 0:
             own_ref[...] = part
         else:
@@ -511,7 +541,7 @@
 def project_kernel(half, blocks_per_seq, lens_ref, order_ref, *refs):
     gain_ref, w_ref, proj_ref, normed_ref, scale_ref = refs[5:]
     norm_into(refs[:5], half, blocks_per_seq, lens_ref, order_ref, gain_ref, normed_ref, scale_ref)
-    proj_ref[...] = mm(normed_ref[...], w_ref[...])
+    proj_ref[...] = mm1(normed_ref[...], w_ref[...])
 
 
 def norm_project(pieces, gain, weights, lens, order, length):
@@ -528,7 +558,7 @@
         grid_spec=pltpu.PrefetchScalarGridSpec(
             num_scalar_prefetch=2,
             grid=(blocks,),
-            in_specs=piece_specs(blocks, width) + [whole_spec((1, full)), whole_spec((full, out))],
+            in_specs=piece_specs(blocks, width, len(pieces)) + [whole_spec((1, full)), whole_spec((full, out))],
             out_specs=(row_spec(out), row_spec(full), row_spec(1)),
         ),
         cost_estimate=pl.CostEstimate(
@@ -562,13 +592,55 @@
     )(order, left, weights)
 
 
+def halves_blocks(half, order_ref, left, w_ref, cols, refs):
+    width = refs[0].shape[1]
+    parts = [nt1(left, w_ref[block_cols(order_ref, b, width), cols]) for b in range(4)]
+    refs[0][...] = parts[0]
+    upper = pl.program_id(0) < half
+
+    @pl.when(upper)
+    def _():
+        for b in range(1, 4):
+            refs[2 * b - 1][...] = parts[b].astype(BF16)
+
+    @pl.when(jnp.logical_not(upper))
+    def _():
+        for b in range(1, 4):
+            refs[2 * b][...] = parts[b].astype(BF16)
+
+
+def halves_kernel(half, order_ref, left_ref, w_ref, *refs):
+    halves_blocks(half, order_ref, left_ref[...], w_ref, slice(None), refs)
+
+
+def spread_halves(left, weights, order):
+    tokens, inner = left.shape
+    full = weights.shape[0]
+    blocks = tokens // ROWS
+    part = jax.ShapeDtypeStruct((tokens // 2, full // 4), BF16)
+    return pl.pallas_call(
+        functools.partial(halves_kernel, blocks // 2),
+        out_shape=(jax.ShapeDtypeStruct((tokens, full // 4), F32),) + (part,) * 6,
+        grid_spec=pltpu.PrefetchScalarGridSpec(
+            num_scalar_prefetch=1,
+            grid=(blocks,),
+            in_specs=[row_spec(inner), whole_spec((full, inner))],
+            out_specs=tuple(piece_specs(blocks, full // 4, 7)),
+        ),
+        cost_estimate=pl.CostEstimate(
+            flops=2 * tokens * full * inner, bytes_accessed=tokens * (full * 3 + inner * 2),
+            transcendentals=0),
+        name="spread_halves",
+    )(order, left, weights)
+
+
 def feed_kernel(half, blocks_per_seq, lens_ref, order_ref, *refs):
     (grad_ref, gain_ref, w_ref, normed_ref, scale_ref, act_ref, both_ref, dots_ref,
-     down_ref, down_send_ref, feed_ref, feed_send_ref) = refs[5:]
+     feed_ref, feed_send_ref) = refs[7:17]
     ff = act_ref.shape[1]
-    norm_into(refs[:5], half, blocks_per_seq, lens_ref, order_ref, gain_ref, normed_ref, scale_ref)
-    gate_up = mm(normed_ref[...], w_ref[:, : 2 * ff])
-    inner_grad = mm(grad_ref[...], w_ref[:, 2 * ff :])
+    norm_into(refs[:7], half, blocks_per_seq, lens_ref, order_ref, gain_ref, normed_ref, scale_ref)
+    gate_up = mm1(normed_ref[...], w_ref[:, : 2 * ff])
+    inner_grad = mm1(grad_ref[...], w_ref[:, 2 * ff :])
     gate_act = gate_up[:, :ff]
     up_act = gate_up[:, ff:]
     sig = sigm(gate_act)
@@ -580,7 +652,7 @@
     both_ref[:, ff:] = up_grad.astype(BF16)
     dots = jnp.sum(gate_grad * gate_act + up_grad * up_act, axis=1, keepdims=True)
     dots_ref[0] = jnp.broadcast_to(dots, (ROWS, 128)).T[0:8]
-    send_blocks(order_ref, both_ref[...], w_ref, slice(0, 2 * ff), down_ref, down_send_ref)
+    halves_blocks(half, order_ref, both_ref[...], w_ref, slice(0, 2 * ff), refs[17:])
     send_blocks(order_ref, act_ref[...], w_ref, slice(2 * ff, 3 * ff), feed_ref, feed_send_ref)
 
 
@@ -598,14 +670,17 @@
             jax.ShapeDtypeStruct((tokens, ff), BF16),
             jax.ShapeDtypeStruct((tokens, 2 * ff), BF16),
             jax.ShapeDtypeStruct((blocks, 8, ROWS), F32),
-        ) + shapes + shapes,
+        ) + shapes + (
+            jax.ShapeDtypeStruct((tokens, width), F32),
+        ) + (jax.ShapeDtypeStruct((tokens // 2, width), BF16),) * 6,
         grid_spec=pltpu.PrefetchScalarGridSpec(
             num_scalar_prefetch=2,
             grid=(blocks,),
-            in_specs=piece_specs(blocks, width)
+            in_specs=piece_specs(blocks, width, len(pieces))
             + [row_spec(full), whole_spec((1, full)), whole_spec((full, out))],
             out_specs=(row_spec(full), row_spec(1), row_spec(ff), row_spec(2 * ff),
-                       pl.BlockSpec((1, 8, ROWS), lambda i, *_: (i, 0, 0))) + specs + specs,
+                       pl.BlockSpec((1, 8, ROWS), lambda i, *_: (i, 0, 0))) + specs
+            + tuple(piece_specs(blocks, width, 7)),
         ),
         cost_estimate=pl.CostEstimate(
             flops=4 * tokens * full * out, bytes_accessed=tokens * full * 16,
@@ -615,12 +690,12 @@
 
 
 def join_kernel(half, order_ref, *refs):
-    w_ref, full_ref, out_ref = refs[5:]
-    pieces = read_pieces(refs[:5], half)
+    w_ref, full_ref, out_ref = refs[7:]
+    pieces = read_pieces(refs[:7], half)
     width = pieces[0].shape[1]
     for b, piece in enumerate(pieces):
         full_ref[:, block_cols(order_ref, b, width)] = piece
-    out_ref[...] = mm(full_ref[...], w_ref[...])
+    out_ref[...] = mm1(full_ref[...], w_ref[...])
 
 
 def join_product(pieces, weights, order):
@@ -636,7 +711,7 @@
         grid_spec=pltpu.PrefetchScalarGridSpec(
             num_scalar_prefetch=1,
             grid=(blocks,),
-            in_specs=piece_specs(blocks, width) + [whole_spec((full, out))],
+            in_specs=piece_specs(blocks, width, len(pieces)) + [whole_spec((full, out))],
             out_specs=(row_spec(full), row_spec(out)),
         ),
         cost_estimate=pl.CostEstimate(
@@ -696,9 +771,30 @@
     return total
 
 
+def gather_halves(values):
+    half = values.shape[0] // 2
+    top, low = values[:half], values[half:]
+    y_top = send_col(top, 2)
+    x_low = send_col(low, 1)
+    x_top = send_col(top, 1)
+    y_low = send_col(low, 2)
+    return values, x_top, x_low, y_top, y_low, send_col(y_top, 1), send_col(x_low, 2)
+
+
+def sum_halves(own, x_top, x_low, y_top, y_low, far_top, far_low):
+    via_x = send_col(far_top, 1).astype(F32)
+    via_y = send_col(far_low, 2).astype(F32)
+    x_top = send_col(x_top, 1)
+    y_low = send_col(y_low, 2)
+    x_low = send_col((x_low.astype(F32) + via_y).astype(BF16), 1)
+    y_top = send_col((y_top.astype(F32) + via_x).astype(BF16), 2)
+    top = x_top.astype(F32) + y_top.astype(F32)
+    low = x_low.astype(F32) + y_low.astype(F32)
+    return own + jnp.concatenate([top, low], axis=0)
+
+
 def sum_scalars(values):
-    values = values + send_col(values, 1)
-    return values + send_col(values, 2)
+    return (values + send_col(values, 1)) + (send_col(values, 2) + send_col(values, 3))
 
 
 def swap_cores(mine, dp):
@@ -806,27 +902,26 @@
             ff_weights = gather_weight(ff_block, dp, st["scale"])
         mixed, *st["saved"] = mixer_fwd(st["proj"], conv, rates, gain_row, heads, per_part)
         st["mixed"] = mixed.reshape(tokens, vals)
-        attention = sum_features(*spread_product(st["mixed"], out_weights, order))
+        attention = sum_halves(*spread_halves(st["mixed"], out_weights, order))
         st["hidden"] = st["local"].astype(F32) + attention
-        st["pieces"] = gather_features(st["hidden"].astype(BF16))
+        st["pieces"] = gather_halves(st["hidden"].astype(BF16))
     results = []
     gate_up_grad = 0.0
     down_grad = 0.0
     second_gain_grad = 0.0
     for part, st in enumerate(state):
         st["grad_full"] = grad_full[part * tokens : (part + 1) * tokens]
-        (normed, scale, act, both, dots, second_own, second_send, feed_own, feed_send
-         ) = feed_forward(st["pieces"], st["grad_full"], second_row, ff_weights, st["lens"], order,
+        normed, scale, act, both, dots, feed_own, feed_send, *sends = feed_forward(st["pieces"], st["grad_full"], second_row, ff_weights, st["lens"], order,
                           length)
         dots = sum_scalars(dots)[:, 0, :].reshape(tokens, 1)
-        second_grad = sum_features(second_own, second_send, dots) * st["valid"]
+        second_grad = sum_halves(*sends) * st["valid"]
         hat = st["hidden"] * scale
         second_gain_grad = second_gain_grad + jnp.sum(second_grad * hat, axis=0)
         st["hidden_grad"] = st["grad_out"] + scale * (
             second_grad * second_local - hat * (dots * (1.0 / D)))
-        st["pieces"] = gather_features(st["hidden_grad"].astype(BF16))
+        st["pieces"] = gather_halves(st["hidden_grad"].astype(BF16))
         hidden, feed_own, feed_send = lax.optimization_barrier(
-            (st["hidden"], feed_own, feed_send, st["pieces"][4]))[:3]
+            (st["hidden"], feed_own, feed_send, st["pieces"][6]))[:3]
         feed = sum_direct(feed_own, feed_send)
         results.append(((hidden + feed) * st["valid"]).astype(BF16))
         gate_up_grad = gate_up_grad + contract_rows(normed, both)
@@ -849,7 +944,7 @@
             mixed_grad = after(mixed_grad, out_low)
         dproj, dots, *grads = mixer_bwd(
             st["proj"], mixed_grad.reshape(per_part, length, vals), st["saved"], conv, rates,
-            gain_row, heads, per_part)
+            gain_row, heads, per_part, 0)
         small = small + jnp.concatenate([grad.reshape(-1) for grad in grads])
         st["dproj"] = dproj.reshape(tokens, -1)
         st["dots"] = sum_scalars(dots)

time: 526 us -> 529 us (level)
  waiting for transfers between devices: 166 us -> 140 us
  starting transfers between devices: 54.1 us -> 66.6 us
  Pallas kernels: 185 us -> 194 us
    ppermute x33 -> x44, waiting for transfers between devices: 158 us -> 133 us  [send_col(): return lax.ppermute(values, 'col', xor_perm(4, bit))]
    ppermute x33 -> x44, starting transfers between devices: 30.5 us -> 42.6 us  [send_col(): return lax.ppermute(values, 'col', xor_perm(4, bit))]
    pallas_call x0 -> x1, Pallas kernels: none -> 7.44 us  [spread_halves(): pl.pallas_call(functools.partial(halves_kernel, blocks // 2), out_shape=(...]
    pallas_call x2 -> x1, Pallas kernels: 19.1 us -> 12.5 us  [spread_product(): pl.pallas_call(spread_kernel, out_shape=shapes, grid_spec=pltpu.PrefetchS...]
    convert_element_type x2 -> x6, other arithmetic: 4.88 us -> 10.2 us  [the longest x2 3.34 us: sum_halves(): y_top = send_col((y_top.astype(F32) + via_x).astype(BF16), 2)]
    unnamed x96 -> x88, local copies, waits for them, and re-layouts: 12.6 us -> 13.3 us
  transfers between devices with their start and end apart: 53 -> 64, of which waited for: 23 -> 24; matrix products, arithmetic and copies ran while one was open for 17% -> 18% of each run, Pallas kernels for 29% -> 31%
where the time goes in v3:
time: 529 us; the launch traced here: 520 us
  Pallas kernels  194 us (37%)
  waiting for transfers between devices  140 us (26%)
  starting transfers between devices  66.6 us (13%)
  other arithmetic  37.9 us (7%)
  matrix products  36.2 us (7%)
  local copies, waits for them, and re-layouts  30.2 us (6%)
  between operations  15.3 us (3%)
    ppermute x44, waiting for transfers between devices, send_col(): return lax.ppermute(values, 'col', xor_perm(4, bit))  133 us
    pallas_call x1, Pallas kernels, mixer_bwd(): pl.pallas_call(functools.partial(bwd_kernel, heads, nseq), out_shape=(jax...  68.2 us
    pallas_call x1, Pallas kernels, mixer_fwd(): pl.pallas_call(functools.partial(fwd_kernel, heads, nseq), out_shape=(jax...  47.4 us
    ppermute x44, starting transfers between devices, send_col(): return lax.ppermute(values, 'col', xor_perm(4, bit))  42.6 us
    dot_general x4, matrix products, contract_rows(): lax.dot_general(left, right, (((0,), (0,)), ((), ())), preferred_element_...  36.2 us
    pallas_call x1, Pallas kernels, feed_forward(): pl.pallas_call(functools.partial(feed_kernel, blocks // 2, length // ROWS...  34.1 us
    pallas_call x1, Pallas kernels, norm_project(): pl.pallas_call(functools.partial(project_kernel, blocks // 2, length // R...  15.7 us
    ppermute x2, starting transfers between devices, sum_small(): total = total + lax.ppermute(total, 'dp', [(0, 1), (1, 0)])  14.1 us
  transfers between devices with their start and end apart: 64, of which 24 were waited for; matrix products, arithmetic and copies ran while one was open for 18% of the time, Pallas kernels for 31%

profile of v3, /device:TPU:1, one launch (start us, length us, event | category | flops | bytes accessed | tf_op | source)
XLA Modules:
  0.0 520.5 jit_solution(14684856342098815423)
XLA Ops:
  15.4 20.9 %collective-permute-done.refs_1_ = bf16[2048,256]{1,0:T(8,128)(2,1)} collective-permute-done((bf16[2048,256]{1,0:T(8,128)(2,1)S(1)}, bf16[2048,256]{1,0:T(8,128)(2,1)}, u32[]{:S(2)}, u32[]{:S(2)}) %collective-permute-start) | collective-permute-done | bytes 1048608 | tf_op jit(solution)/shard_map/ppermute | solution.py:741
  44.3 6.4 %collective-permute-done.2.refs_3_ = bf16[1024,256]{1,0:T(8,128)(2,1)S(1)} collective-permute-done((bf16[1024,256]{1,0:T(8,128)(2,1)S(1)}, bf16[1024,256]{1,0:T(8,128)(2,1)S(1)}, u32[]{:S(2)}, u32[]{:S(2)}) %collective-permute-start.2) | collective-permute-done | bytes 524320 | tf_op jit(solution)/shard_map/ppermute | solution.py:741
  54.3 15.7 %norm_project.1 = (f32[2048,1664]{1,0:T(8,128)}, bf16[2048,1024]{1,0:T(8,128)(2,1)}, f32[2048,1]{1,0:T(8,128)}) custom-call(s32[2]{0:T(128)} %lens_ref.3, s32[4]{0:T(128)} %iota_xor_fusion.order_ref, bf16[2048,256]{1,0:T(8,128)(2,1)} %bitcast.97, bf16[2048,256]{1,0:T(8,128)(2,1)} %collective-permute-done.refs_1_, ...), custom_call_target="tpu_custom_call" | custom-call | flops 6979321856 | bytes 22020096 | tf_op jit(solution)/shard_map/norm_project/pallas_call | solution.py:551
  73.9 47.4 %mixer_fwd.1 = (bf16[2,1024,512]{2,1,0:T(8,128)(2,1)}, f32[2,1024,512]{2,1,0:T(8,128)}, f32[2,1024,512]{2,1,0:T(8,128)}, f32[2,8,2,128,256]{4,3,2,1,0:T(8,128)}, f32[2,8,2,128,128]{4,3,2,1,0:T(8,128)}) custom-call(f32[2,1024,1664]{2,1,0:T(8,128)} %bitcast.121, f32[4,1024]{1,0:T(4,128)} %maximum_convert_fusion.conv_ref, f32[2,128]{1,0:T(2,128)} %pad_maximum_fusion.4.rate_ref, ...), custom_call_target="tpu_custom_call" | custom-call | flops 24576000000 | bytes 27262976 | tf_op jit(solution)/shard_map/mixer_fwd/pallas_call | solution.py:224
  121.3 7.4 %spread_halves.1 = (f32[2048,256]{1,0:T(8,128)}, bf16[1024,256]{1,0:T(8,128)(2,1)}, bf16[1024,256]{1,0:T(8,128)(2,1)}, bf16[1024,256]{1,0:T(8,128)(2,1)}, bf16[1...) custom-call(s32[4]{0:T(128)} %iota_xor_fusion.order_ref, bf16[2048,512]{1,0:T(8,128)(2,1)} %bitcast.127, ...), custom_call_target="tpu_custom_call" | custom-call | flops 2147483648 | bytes 8388608 | tf_op jit(solution)/shard_map/spread_halves/pallas_call | solution.py:621
  131.5 9.8 %collective-permute-done.5 = bf16[1024,256]{1,0:T(8,128)(2,1)S(1)} collective-permute-done((bf16[1024,256]{1,0:T(8,128)(2,1)}, bf16[1024,256]{1,0:T(8,128)(2,1)S(1)}, u32[]{:S(2)}, u32[]{:S(2)}) %collective-permute-start.5) | collective-permute-done | bytes 524320 | tf_op jit(solution)/shard_map/ppermute | solution.py:741
  147.3 5.3 %collective-permute-done.4 = bf16[1024,256]{1,0:T(8,128)(2,1)S(1)} collective-permute-done((bf16[1024,256]{1,0:T(8,128)(2,1)}, bf16[1024,256]{1,0:T(8,128)(2,1)S(1)}, u32[]{:S(2)}, u32[]{:S(2)}) %collective-permute-start.4) | collective-permute-done | bytes 524320 | tf_op jit(solution)/shard_map/ppermute | solution.py:741
  152.7 10.9 %collective-permute-done.9 = bf16[1024,256]{1,0:T(8,128)(2,1)S(1)} collective-permute-done((bf16[1024,256]{1,0:T(8,128)(2,1)}, bf16[1024,256]{1,0:T(8,128)(2,1)S(1)}, u32[]{:S(2)}, u32[]{:S(2)}) %collective-permute-start.9) | collective-permute-done | bytes 524320 | tf_op jit(solution)/shard_map/ppermute | solution.py:741
  166.4 3.6 collective-permute-start.11
  171.5 8.3 %collective-permute-done.11.refs_2_ = bf16[1024,256]{1,0:T(8,128)(2,1)} collective-permute-done((bf16[1024,256]{1,0:T(8,128)(2,1)}, bf16[1024,256]{1,0:T(8,128)(2,1)}, u32[]{:S(2)}, u32[]{:S(2)}) %collective-permute-start.11) | collective-permute-done | bytes 524320 | tf_op jit(solution)/shard_map/ppermute | solution.py:741
  183.0 8.9 %collective-permute-done.13.refs_4_ = bf16[1024,256]{1,0:T(8,128)(2,1)} collective-permute-done((bf16[1024,256]{1,0:T(8,128)(2,1)}, bf16[1024,256]{1,0:T(8,128)(2,1)}, u32[]{:S(2)}, u32[]{:S(2)}) %collective-permute-start.13) | collective-permute-done | bytes 524320 | tf_op jit(solution)/shard_map/ppermute | solution.py:741
  191.9 11.2 %collective-permute-done.15.refs_6_ = bf16[1024,256]{1,0:T(8,128)(2,1)} collective-permute-done((bf16[1024,256]{1,0:T(8,128)(2,1)}, bf16[1024,256]{1,0:T(8,128)(2,1)}, u32[]{:S(2)}, u32[]{:S(2)}) %collective-permute-start.15) | collective-permute-done | bytes 524320 | tf_op jit(solution)/shard_map/ppermute | solution.py:741
  203.2 34.1 %feed_forward.1 = (bf16[2048,1024]{1,0:T(8,128)(2,1)}, f32[2048,1]{1,0:T(8,128)}, bf16[2048,768]{1,0:T(8,128)(2,1)}, bf16[2048,1536]{1,0:T(8,128)(2,1)}, f32[4,8...) custom-call(s32[2]{0:T(128)} %lens_ref.3, ...), custom_call_target="tpu_custom_call" | custom-call | flops 19327352832 | bytes 33554432 | tf_op jit(solution)/shard_map/feed_forward/pallas_call | solution.py:665
  241.6 11.5 %convolution_convert_fusion = bf16[1024,1536]{1,0:T(8,128)(2,1)} fusion(bf16[2048,1024]{1,0:T(8,128)(2,1)} %get-tuple-element.99, bf16[2048,1536]{1,0:T(8,128)(2,1)} %get-tuple-element.100), kind=kOutput, calls=%fused_computation | convolution fusion | flops 6444023808 | bytes 13631488 | tf_op jit(solution)/shard_map/dot_general | solution.py:729
  260.7 6.9 %convolution_convert_fusion.2 = bf16[1024,768]{1,0:T(8,128)(2,1)} fusion(bf16[2048,1024]{1,0:T(8,128)(2,1)} %all-gather.9.cloned.1.call-done.refs_7_, bf16[2048,768]{1,0:T(8,128)(2,1)S(1)} %copy-done.36), kind=kOutput, calls=%fused_computation.20 | convolution fusion | flops 3222011904 | bytes 8912896 | tf_op jit(solution)/shard_map/dot_general | solution.py:729
  270.1 5.9 %collective-permute-done.18 = bf16[1024,256]{1,0:T(8,128)(2,1)} collective-permute-done((bf16[1024,256]{1,0:T(8,128)(2,1)}, bf16[1024,256]{1,0:T(8,128)(2,1)}, u32[]{:S(2)}, u32[]{:S(2)}) %collective-permute-start.18) | collective-permute-done | bytes 524320 | tf_op jit(solution)/shard_map/ppermute | solution.py:741
  278.7 3.2 fusion.24
  285.9 5.5 %collective-permute-done.31.refs_3_ = bf16[1024,256]{1,0:T(8,128)(2,1)S(1)} collective-permute-done((bf16[1024,256]{1,0:T(8,128)(2,1)S(1)}, bf16[1024,256]{1,0:T(8,128)(2,1)S(1)}, u32[]{:S(2)}, u32[]{:S(2)}) %collective-permute-start.31) | collective-permute-done | bytes 524320 | tf_op jit(solution)/shard_map/ppermute | solution.py:741
  292.9 8.1 %collective-permute-done.30.refs_1_ = bf16[1024,256]{1,0:T(8,128)(2,1)S(1)} collective-permute-done((bf16[1024,256]{1,0:T(8,128)(2,1)S(1)}, bf16[1024,256]{1,0:T(8,128)(2,1)S(1)}, u32[]{:S(2)}, u32[]{:S(2)}) %collective-permute-start.30) | collective-permute-done | bytes 524320 | tf_op jit(solution)/shard_map/ppermute | solution.py:741
  301.3 10.9 %collective-permute-done.33.refs_5_ = bf16[1024,256]{1,0:T(8,128)(2,1)S(1)} collective-permute-done((bf16[1024,256]{1,0:T(8,128)(2,1)S(1)}, bf16[1024,256]{1,0:T(8,128)(2,1)S(1)}, u32[]{:S(2)}, u32[]{:S(2)}) %collective-permute-start.33) | collective-permute-done | bytes 524320 | tf_op jit(solution)/shard_map/ppermute | solution.py:741
  313.1 8.6 %join_product.1 = (bf16[2048,1024]{1,0:T(8,128)(2,1)}, f32[2048,512]{1,0:T(8,128)}) custom-call(s32[4]{0:T(128)} %iota_xor_fusion.order_ref, bf16[2048,256]{1,0:T(8,128)(2,1)} %copy-done.7, bf16[1024,256]{1,0:T(8,128)(2,1)} %copy-done.29, bf16[1024,256]{1,0:T(8,128)(2,1)} %copy-done.28, bf16[1024,256]{1,0:T(8,128)(2,1)} %copy-done.27, ...), custom_call_target="tpu_custom_call" | custom-call | flops 2147483648 | bytes 12582912 | tf_op jit(solution)/shard_map/join_product/pallas_call | solution.py:705
  321.6 6.2 %convolution_convert_fusion.3 = bf16[1024,512]{1,0:T(8,128)(2,1)} fusion(bf16[2048,1024]{1,0:T(8,128)(2,1)} %get-tuple-element.104, bf16[2048,512]{1,0:T(8,128)(2,1)} %bitcast.128), kind=kOutput, calls=%fused_computation.21 | convolution fusion | flops 2148007936 | bytes 7340032 | tf_op jit(solution)/shard_map/dot_general | solution.py:729
  328.7 3.6 slice_bitcast_fusion.2
  334.9 68.2 %mixer_bwd.1 = (bf16[2,1024,1664]{2,1,0:T(8,128)(2,1)}, f32[2,8,8,128]{3,2,1,0:T(8,128)}, f32[32,1024]{1,0:T(8,128)}, f32[16,128]{1,0:T(8,128)}, f32[8,256]{1,0:T(8,128)}) custom-call(f32[2,1024,1664]{2,1,0:T(8,128)} %bitcast.122, f32[2,1024,1664]{2,1,0:T(8,128)} %bitcast.123, f32[2,1024,512]{2,1,0:T(8,128)} %bitcast.126, ...), custom_call_target="tpu_custom_call" | custom-call | flops 40960000000 | bytes 27262976 | tf_op jit(solution)/shard_map/mixer_bwd/pallas_call | solution.py:424
  403.2 4.2 multiply_convert_fusion
  408.0 11.6 %convolution_convert_fusion.1 = bf16[1024,1664]{1,0:T(8,128)(2,1)} fusion(bf16[2048,1024]{1,0:T(8,128)(2,1)} %get-tuple-element.111, bf16[2048,1664]{1,0:T(8,128)(2,1)S(1)} %bitcast.125), kind=kOutput, calls=%fused_computation.1 | convolution fusion | flops 6981025792 | bytes 14417920 | tf_op jit(solution)/shard_map/dot_general | solution.py:729
  428.7 12.5 %spread_product.1 = (f32[2048,256]{1,0:T(8,128)}, bf16[3,2048,256]{2,1,0:T(8,128)(2,1)}) custom-call(s32[4]{0:T(128)} %iota_xor_fusion.order_ref, bf16[2048,1664]{1,0:T(8,128)(2,1)} %bitcast.124, bf16[1024,1664]{1,0:T(8,128)(2,1)} %all-gather.5.cloned.1.call-done.refs_6_.w_ref), custom_call_target="tpu_custom_call" | custom-call | flops 6979321856 | bytes 13107200 | tf_op jit(solution)/shard_map/spread_product/pallas_call | solution.py:579
  444.8 11.6 %collective-permute-start.41 = (f32[40,128]{1,0:T(8,128)S(1)}, f32[40,128]{1,0:T(8,128)S(1)}, u32[]{:S(2)}, u32[]{:S(2)}) collective-permute-start(f32[40,128]{1,0:T(8,128)S(1)} %pad_bitcast_fusion), channel_id=1, source_target_pairs={{0,16},{16,0},{1,17},{17,1},{2,18},{18,2},{3,19},{19,3},{4,20},{20... | collective-permute-start | bytes 61448 | tf_op jit(solution)/shard_map/ppermute | solution.py:826
  457.4 2.6 collective-permute-start.42
  474.4 16.6 %collective-permute-done.47 = bf16[2048,256]{1,0:T(8,128)(2,1)} collective-permute-done((bf16[2048,256]{1,0:T(8,128)(2,1)}, bf16[2048,256]{1,0:T(8,128)(2,1)}, u32[]{:S(2)}, u32[]{:S(2)}) %collective-permute-start.47) | collective-permute-done | bytes 1048608 | tf_op jit(solution)/shard_map/ppermute | solution.py:741
  491.1 3.7 fusion.5
  494.8 2.4 collective-permute-start.48
  (275 shorter events, 111.4 us)
Async XLA Ops:
  7.2 47.1 %all-gather.5.cloned.1.call-start = ((), (), s32[]{:S(2)}) async-start(), calls=%async_computation.4 | async-start | bytes 3833856 | tf_op jit(solution)/shard_map/all_gather | solution.py:812
  11.2 110.1 %all-gather.7.cloned.1.call-start = ((), (), s32[]{:S(2)}) async-start(), calls=%async_computation.5 | async-start | bytes 1179648 | tf_op jit(solution)/shard_map/all_gather | solution.py:812
  11.3 25.1 %collective-permute-start = (bf16[2048,256]{1,0:T(8,128)(2,1)S(1)}, bf16[2048,256]{1,0:T(8,128)(2,1)}, u32[]{:S(2)}, u32[]{:S(2)}) collective-permute-start(bf16[2048,256]{1,0:T(8,128)(2,1)S(1)} %bitcast.98), channel_id=1, source_target_pairs={{0,1},{1,0},{2,3},{3,2},{4,5},{5,4},{6,7},{7,6},{8,9},{9,8},{10,11... | collective-permute-start | bytes 3145736 | tf_op jit(solution)/shard_map/ppermute | solution.py:741
  13.4 24.2 %collective-permute-start.1 = (bf16[2048,256]{1,0:T(8,128)(2,1)S(1)}, bf16[2048,256]{1,0:T(8,128)(2,1)}, u32[]{:S(2)}, u32[]{:S(2)}) collective-permute-start(bf16[2048,256]{1,0:T(8,128)(2,1)S(1)} %bitcast.99), channel_id=1, source_target_pairs={{0,2},{1,3},{2,0},{3,1},{4,6},{5,7},{6,4},{7,5},{8,10},{9,11},{10,... | collective-permute-start | bytes 3145736 | tf_op jit(solution)/shard_map/ppermute | solution.py:741
  36.4 166.8 %all-gather.9.cloned.1.call-start = ((), (), s32[]{:S(2)}) async-start(), calls=%async_computation.6 | async-start | bytes 5242880 | tf_op jit(solution)/shard_map/all_gather | solution.py:901
  70.0 133.2 %all-gather.11.cloned.1.call-start = ((), (), s32[]{:S(2)}) async-start(), calls=%async_computation.7 | async-start | bytes 5308416 | tf_op jit(solution)/shard_map/all_gather | solution.py:812
  72.0 400.4 %reduce-scatter.11.cloned.1.call-start = ((), (), s32[]{:S(2)}) async-start(), calls=%async_computation.11 | async-start | bytes 1769472 | tf_op jit(solution)/shard_map/reduce_scatter | solution.py:816
  131.2 21.4 %collective-permute-start.4 = (bf16[1024,256]{1,0:T(8,128)(2,1)}, bf16[1024,256]{1,0:T(8,128)(2,1)S(1)}, u32[]{:S(2)}, u32[]{:S(2)}) collective-permute-start(bf16[1024,256]{1,0:T(8,128)(2,1)} %get-tuple-element.76), channel_id=1, source_target_pairs={{0,1},{1,0},{2,3},{3,2},{4,5},{5,4},{6,7},{7,6},{8,9},{9,8},{10,11... | collective-permute-start | bytes 1572872 | tf_op jit(solution)/shard_map/ppermute | solution.py:741
  143.8 19.8 %collective-permute-start.9 = (bf16[1024,256]{1,0:T(8,128)(2,1)}, bf16[1024,256]{1,0:T(8,128)(2,1)S(1)}, u32[]{:S(2)}, u32[]{:S(2)}) collective-permute-start(bf16[1024,256]{1,0:T(8,128)(2,1)} %get-tuple-element.81), channel_id=1, source_target_pairs={{0,2},{1,3},{2,0},{3,1},{4,6},{5,7},{6,4},{7,5},{8,10},{9,11},{10,... | collective-permute-start | bytes 1572872 | tf_op jit(solution)/shard_map/ppermute | solution.py:741
  145.2 18.6 %collective-permute-start.8 = (bf16[1024,256]{1,0:T(8,128)(2,1)S(1)}, bf16[1024,256]{1,0:T(8,128)(2,1)S(1)}, u32[]{:S(2)}, u32[]{:S(2)}) collective-permute-start(bf16[1024,256]{1,0:T(8,128)(2,1)S(1)} %add_convert_fusion.2), channel_id=1, source_target_pairs={{0,1},{1,0},{2,3},{3,2},{4,5},{5,4},{6,7},{7,6},{8,9},{9,8},{10,11... | collective-permute-start | bytes 1572872 | tf_op jit(solution)/shard_map/ppermute | solution.py:741
  171.3 20.6 %collective-permute-start.13 = (bf16[1024,256]{1,0:T(8,128)(2,1)}, bf16[1024,256]{1,0:T(8,128)(2,1)}, u32[]{:S(2)}, u32[]{:S(2)}) collective-permute-start(bf16[1024,256]{1,0:T(8,128)(2,1)} %get-tuple-element.194), channel_id=1, source_target_pairs={{0,2},{1,3},{2,0},{3,1},{4,6},{5,7},{6,4},{7,5},{8,10},{9,11},{10,... | collective-permute-start | bytes 1572872 | tf_op jit(solution)/shard_map/ppermute | solution.py:741
  171.5 20.5 %collective-permute-start.10 = (bf16[1024,256]{1,0:T(8,128)(2,1)}, bf16[1024,256]{1,0:T(8,128)(2,1)}, u32[]{:S(2)}, u32[]{:S(2)}) collective-permute-start(bf16[1024,256]{1,0:T(8,128)(2,1)} %get-tuple-element.195), channel_id=1, source_target_pairs={{0,1},{1,0},{2,3},{3,2},{4,5},{5,4},{6,7},{7,6},{8,9},{9,8},{10,11... | collective-permute-start | bytes 1572872 | tf_op jit(solution)/shard_map/ppermute | solution.py:741
  179.8 23.4 %collective-permute-start.15 = (bf16[1024,256]{1,0:T(8,128)(2,1)}, bf16[1024,256]{1,0:T(8,128)(2,1)}, u32[]{:S(2)}, u32[]{:S(2)}) collective-permute-start(bf16[1024,256]{1,0:T(8,128)(2,1)} %collective-permute-done.11.refs_2_), channel_id=1, source_target_pairs={{0,2},{1,3},{2,0},{3,1},{4,6},{5,7},{6,4},{7,5},{8,10},{9,11},{10,... | collective-permute-start | bytes 1572872 | tf_op jit(solution)/shard_map/ppermute | solution.py:741
  181.1 22.0 %collective-permute-start.14 = (bf16[1024,256]{1,0:T(8,128)(2,1)}, bf16[1024,256]{1,0:T(8,128)(2,1)}, u32[]{:S(2)}, u32[]{:S(2)}) collective-permute-start(bf16[1024,256]{1,0:T(8,128)(2,1)} %collective-permute-done.12.refs_3_), channel_id=1, source_target_pairs={{0,1},{1,0},{2,3},{3,2},{4,5},{5,4},{6,7},{7,6},{8,9},{9,8},{10,11... | collective-permute-start | bytes 1572872 | tf_op jit(solution)/shard_map/ppermute | solution.py:741
  237.3 21.5 %collective-permute-start.24 = (f32[4,8,512]{2,1,0:T(8,128)}, f32[4,8,512]{2,1,0:T(8,128)S(1)}, u32[]{:S(2)}, u32[]{:S(2)}) collective-permute-start(f32[4,8,512]{2,1,0:T(8,128)} %get-tuple-element.95), channel_id=1, source_target_pairs={{0,3},{1,2},{2,1},{3,0},{4,7},{5,6},{6,5},{7,4},{8,11},{9,10},{10,... | collective-permute-start | bytes 196616 | tf_op jit(solution)/shard_map/ppermute | solution.py:741
  238.7 21.5 %collective-permute-start.23 = (f32[4,8,512]{2,1,0:T(8,128)}, f32[4,8,512]{2,1,0:T(8,128)S(1)}, u32[]{:S(2)}, u32[]{:S(2)}) collective-permute-start(f32[4,8,512]{2,1,0:T(8,128)} %get-tuple-element.95), channel_id=1, source_target_pairs={{0,2},{1,3},{2,0},{3,1},{4,6},{5,7},{6,4},{7,5},{8,10},{9,11},{10,... | collective-permute-start | bytes 196616 | tf_op jit(solution)/shard_map/ppermute | solution.py:741
  238.8 30.4 %collective-permute-start.22 = (f32[4,8,512]{2,1,0:T(8,128)}, f32[4,8,512]{2,1,0:T(8,128)S(1)}, u32[]{:S(2)}, u32[]{:S(2)}) collective-permute-start(f32[4,8,512]{2,1,0:T(8,128)} %get-tuple-element.95), channel_id=1, source_target_pairs={{0,1},{1,0},{2,3},{3,2},{4,5},{5,4},{6,7},{7,6},{8,9},{9,8},{10,11... | collective-permute-start | bytes 196616 | tf_op jit(solution)/shard_map/ppermute | solution.py:741
  256.6 20.8 %collective-permute-start.21 = (bf16[1024,256]{1,0:T(8,128)(2,1)}, bf16[1024,256]{1,0:T(8,128)(2,1)}, u32[]{:S(2)}, u32[]{:S(2)}) collective-permute-start(bf16[1024,256]{1,0:T(8,128)(2,1)} %get-tuple-element.94), channel_id=1, source_target_pairs={{0,2},{1,3},{2,0},{3,1},{4,6},{5,7},{6,4},{7,5},{8,10},{9,11},{10,... | collective-permute-start | bytes 1572872 | tf_op jit(solution)/shard_map/ppermute | solution.py:741
  260.2 17.2 %collective-permute-start.20 = (bf16[1024,256]{1,0:T(8,128)(2,1)}, bf16[1024,256]{1,0:T(8,128)(2,1)}, u32[]{:S(2)}, u32[]{:S(2)}) collective-permute-start(bf16[1024,256]{1,0:T(8,128)(2,1)} %add_convert_fusion), channel_id=1, source_target_pairs={{0,1},{1,0},{2,3},{3,2},{4,5},{5,4},{6,7},{7,6},{8,9},{9,8},{10,11... | collective-permute-start | bytes 1572872 | tf_op jit(solution)/shard_map/ppermute | solution.py:741
  267.6 230.8 %reduce-scatter.7.cloned.1.call-start = ((), (), s32[]{:S(2)}) async-start(), calls=%async_computation.9 | async-start | bytes 1179648 | tf_op jit(solution)/shard_map/reduce_scatter | solution.py:816
  291.4 20.8 %collective-permute-start.33 = (bf16[1024,256]{1,0:T(8,128)(2,1)S(1)}, bf16[1024,256]{1,0:T(8,128)(2,1)S(1)}, u32[]{:S(2)}, u32[]{:S(2)}) collective-permute-start(bf16[1024,256]{1,0:T(8,128)(2,1)S(1)} %collective-permute-done.31.refs_3_), channel_id=1, source_target_pairs={{0,1},{1,0},{2,3},{3,2},{4,5},{5,4},{6,7},{7,6},{8,9},{9,8},{10,11... | collective-permute-start | bytes 1572872 | tf_op jit(solution)/shard_map/ppermute | solution.py:741
  292.2 20.9 %collective-permute-start.26 = (bf16[1024,256]{1,0:T(8,128)(2,1)S(1)}, bf16[1024,256]{1,0:T(8,128)(2,1)}, u32[]{:S(2)}, u32[]{:S(2)}) collective-permute-start(bf16[1024,256]{1,0:T(8,128)(2,1)S(1)} %collective-permute-done.25.refs_2_), channel_id=1, source_target_pairs={{0,2},{1,3},{2,0},{3,1},{4,6},{5,7},{6,4},{7,5},{8,10},{9,11},{10,... | collective-permute-start | bytes 1572872 | tf_op jit(solution)/shard_map/ppermute | solution.py:741
  327.9 175.3 %reduce-scatter.9.cloned.1.call-start = ((), (), s32[]{:S(2)}) async-start(), calls=%async_computation.10 | async-start | bytes 3538944 | tf_op jit(solution)/shard_map/reduce_scatter | solution.py:816
  328.6 176.4 %reduce-scatter.5.cloned.1.call-start = ((), (), s32[]{:S(2)}) async-start(), calls=%async_computation.8 | async-start | bytes 3833856 | tf_op jit(solution)/shard_map/reduce_scatter | solution.py:816
  332.3 70.9 %collective-permute-start.27 = (bf16[2048,256]{1,0:T(8,128)(2,1)}, bf16[2048,256]{1,0:T(8,128)(2,1)}, u32[]{:S(2)}, u32[]{:S(2)}) collective-permute-start(bf16[2048,256]{1,0:T(8,128)(2,1)} %get-tuple-element.179), channel_id=1, source_target_pairs={{0,1},{1,0},{2,3},{3,2},{4,5},{5,4},{6,7},{7,6},{8,9},{9,8},{10,11... | collective-permute-start | bytes 3145736 | tf_op jit(solution)/shard_map/ppermute | solution.py:741
  333.2 70.0 %collective-permute-start.29 = (bf16[2048,256]{1,0:T(8,128)(2,1)}, bf16[2048,256]{1,0:T(8,128)(2,1)}, u32[]{:S(2)}, u32[]{:S(2)}) collective-permute-start(bf16[2048,256]{1,0:T(8,128)(2,1)} %get-tuple-element.180), channel_id=1, source_target_pairs={{0,3},{1,2},{2,1},{3,0},{4,7},{5,6},{6,5},{7,4},{8,11},{9,10},{10,... | collective-permute-start | bytes 3145736 | tf_op jit(solution)/shard_map/ppermute | solution.py:741
  334.9 68.3 %collective-permute-start.28 = (bf16[2048,256]{1,0:T(8,128)(2,1)}, bf16[2048,256]{1,0:T(8,128)(2,1)}, u32[]{:S(2)}, u32[]{:S(2)}) collective-permute-start(bf16[2048,256]{1,0:T(8,128)(2,1)} %get-tuple-element.181), channel_id=1, source_target_pairs={{0,2},{1,3},{2,0},{3,1},{4,6},{5,7},{6,4},{7,5},{8,10},{9,11},{10,... | collective-permute-start | bytes 3145736 | tf_op jit(solution)/shard_map/ppermute | solution.py:741
  442.9 20.8 %collective-permute-start.46 = (bf16[1024,256]{1,0:T(8,128)(2,1)S(1)}, bf16[1024,256]{1,0:T(8,128)(2,1)S(1)}, u32[]{:S(2)}, u32[]{:S(2)}) collective-permute-start(bf16[1024,256]{1,0:T(8,128)(2,1)S(1)} %get-tuple-element.175), channel_id=1, source_target_pairs={{0,1},{1,0},{2,3},{3,2},{4,5},{5,4},{6,7},{7,6},{8,9},{9,8},{10,11... | collective-permute-start | bytes 1572872 | tf_op jit(solution)/shard_map/ppermute | solution.py:741
  443.4 20.4 %collective-permute-start.37 = (bf16[1024,256]{1,0:T(8,128)(2,1)S(1)}, bf16[1024,256]{1,0:T(8,128)(2,1)S(1)}, u32[]{:S(2)}, u32[]{:S(2)}) collective-permute-start(bf16[1024,256]{1,0:T(8,128)(2,1)S(1)} %get-tuple-element.176), channel_id=1, source_target_pairs={{0,2},{1,3},{2,0},{3,1},{4,6},{5,7},{6,4},{7,5},{8,10},{9,11},{10,... | collective-permute-start | bytes 1572872 | tf_op jit(solution)/shard_map/ppermute | solution.py:741
  466.5 24.5 %collective-permute-start.47 = (bf16[2048,256]{1,0:T(8,128)(2,1)}, bf16[2048,256]{1,0:T(8,128)(2,1)}, u32[]{:S(2)}, u32[]{:S(2)}) collective-permute-start(bf16[2048,256]{1,0:T(8,128)(2,1)} %pad_maximum_fusion.1), channel_id=1, source_target_pairs={{0,2},{1,3},{2,0},{3,1},{4,6},{5,7},{6,4},{7,5},{8,10},{9,11},{10,... | collective-permute-start | bytes 3145736 | tf_op jit(solution)/shard_map/ppermute | solution.py:741
  467.6 23.4 %collective-permute-start.45 = (bf16[2048,256]{1,0:T(8,128)(2,1)}, bf16[2048,256]{1,0:T(8,128)(2,1)}, u32[]{:S(2)}, u32[]{:S(2)}) collective-permute-start(bf16[2048,256]{1,0:T(8,128)(2,1)} %pad_maximum_fusion), channel_id=1, source_target_pairs={{0,1},{1,0},{2,3},{3,2},{4,5},{5,4},{6,7},{7,6},{8,9},{9,8},{10,11... | collective-permute-start | bytes 3145736 | tf_op jit(solution)/shard_map/ppermute | solution.py:741
  472.4 24.8 %collective-permute-start.55 = (bf16[128,768]{1,0:T(8,128)(2,1)}, bf16[128,768]{1,0:T(8,128)(2,1)S(1)}, u32[]{:S(2)}, u32[]{:S(2)}) collective-permute-start(bf16[128,768]{1,0:T(8,128)(2,1)} %reduce-scatter.11.cloned.1.call-done), channel_id=1, source_target_pairs={{0,16},{16,0},{1,17},{17,1},{2,18},{18,2},{3,19},{19,3},{4,20},{20... | collective-permute-start | bytes 589832 | tf_op jit(solution)/shard_map/ppermute | solution.py:801
  (69 other events, 630.2 us)
Sparse Core Ops, SparseCore 0:
  11.3 42.9 all-gather.4
  56.5 20.9 all-gather.6
  79.3 52.0 all-gather.8
  133.4 52.4 all-gather.10
  267.7 33.5 reduce-scatter.10
  328.0 33.6 reduce-scatter.6
  364.0 39.8 reduce-scatter.8
  419.8 47.3 reduce-scatter.4

commit v4 on v3

--- a/solution.py
+++ b/solution.py
@@ -262,7 +262,7 @@
 
 def bwd_kernel(heads, nseq, proj_ref, prev_ref, dmix_ref, o_ref, u_ref, s_ref, t_ref,
                conv_ref, rate_ref, gain_ref,
-               dproj_ref, dots_ref, dconv_ref, drate_ref, dgain_ref, xs_ref, ds_ref, dstate_ref):
+               dproj_ref, dots_ref, dotc_ref, dconv_ref, drate_ref, dgain_ref, xs_ref, ds_ref, dstate_ref):
     qkv = heads * (2 * DK + DV)
     gate_at = qkv
     ab_at = qkv + heads * DV
@@ -403,6 +403,7 @@
             dx_in = dx_in + ds_ref[s, 3 - i : 3 - i + BLK, :] * kernel[i : i + 1]
         dproj_ref[s, :, 0:qkv] = dx_in.astype(BF16)
         dots = dots + jnp.sum(dx_in * xs_ref[s, 8 : 8 + BLK, :], axis=1, keepdims=True)
+        dotc_ref[s] = dots
         dots_ref[s, 0] = jnp.broadcast_to(dots, (BLK, 128)).T[0:8]
         for i in range(CONV):
             dconv_ref[8 * i : 8 * i + 8, :] += colsum(dpre * xs_ref[s, 5 + i : 5 + i + BLK, :])
@@ -421,11 +422,12 @@
     all_tok = lambda i, c: (i + first, blocks - 1 - c, 0)
     all_blk = lambda i, c: (i + first, blocks - 1 - c, 0, 0, 0)
     whole = lambda i, c: (0, 0)
-    dproj, dots, dconv, drate, dgain = pl.pallas_call(
+    dproj, dots, dot_cols, dconv, drate, dgain = pl.pallas_call(
         functools.partial(bwd_kernel, heads, nseq),
         out_shape=(
             jax.ShapeDtypeStruct((seqs, length, width), BF16),
             jax.ShapeDtypeStruct((seqs, blocks, 8, 128), F32),
+            jax.ShapeDtypeStruct((seqs, length, 1), F32),
             jax.ShapeDtypeStruct((8 * CONV, qkv), F32),
             jax.ShapeDtypeStruct((16, 128), F32),
             jax.ShapeDtypeStruct((8, DV), F32),
@@ -447,6 +449,7 @@
         out_specs=(
             pl.BlockSpec((nseq, BLK, width), tok),
             pl.BlockSpec((nseq, 1, 8, 128), lambda i, c: (i, blocks - 1 - c, 0, 0)),
+            pl.BlockSpec((nseq, BLK, 1), tok),
             pl.BlockSpec((8 * CONV, qkv), whole),
             pl.BlockSpec((16, 128), whole),
             pl.BlockSpec((8, DV), whole),
@@ -465,7 +468,7 @@
     dconv = jnp.sum(dconv.reshape(CONV, 8, qkv), axis=1)
     drate = jnp.sum(drate.reshape(2, 8, 128), axis=1)[:, :heads]
     dgain = jnp.sum(dgain, axis=0)
-    return dproj, dots[:, :, 0, :], dconv, drate[0], drate[1], dgain
+    return dproj, dots[:, :, 0, :], dot_cols, dconv, drate[0], drate[1], dgain
 
 
 ROWS = 512
@@ -568,11 +571,22 @@
     )(lens, order, *pieces, gain, weights)
 
 
-def spread_kernel(order_ref, left_ref, w_ref, own_ref, send_ref):
-    send_blocks(order_ref, left_ref[...], w_ref, slice(None), own_ref, send_ref)
-
-
-def spread_product(left, weights, order):
+def spread_kernel(order_ref, left_ref, w_ref, normed_ref, gain_ref, dots_ref, own_ref, send_ref):
+    width = own_ref.shape[1]
+    left = left_ref[...]
+    dots = dots_ref[...] * (1.0 / gain_ref.shape[1])
+    for b in range(4):
+        at = block_cols(order_ref, b, width)
+        gain = gain_ref[:, at]
+        part = nt1(left, w_ref[at, :])
+        part = part - normed_ref[:, at].astype(F32) * (1.0 / (gain * gain)) * dots
+        if b == 0:
+            own_ref[...] = part
+        else:
+            send_ref[b - 1] = part.astype(BF16)
+
+
+def spread_product(left, weights, order, normed, gain, dots):
     tokens, inner = left.shape
     full = weights.shape[0]
     shapes, specs = send_specs(tokens, full // 4)
@@ -582,19 +596,26 @@
         grid_spec=pltpu.PrefetchScalarGridSpec(
             num_scalar_prefetch=1,
             grid=(tokens // ROWS,),
-            in_specs=[row_spec(inner), whole_spec((full, inner))],
+            in_specs=[row_spec(inner), whole_spec((full, inner)), row_spec(full),
+                      whole_spec((1, full)), row_spec(1)],
             out_specs=specs,
         ),
         cost_estimate=pl.CostEstimate(
             flops=2 * tokens * full * inner, bytes_accessed=tokens * (full * 3 + inner * 2),
             transcendentals=0),
         name="spread_product",
-    )(order, left, weights)
-
-
-def halves_blocks(half, order_ref, left, w_ref, cols, refs):
+    )(order, left, weights, normed, gain, dots)
+
+
+def halves_blocks(half, order_ref, left, w_ref, cols, refs, fix=None):
     width = refs[0].shape[1]
     parts = [nt1(left, w_ref[block_cols(order_ref, b, width), cols]) for b in range(4)]
+    if fix is not None:
+        normed_ref, gain_ref, dots = fix
+        for b in range(4):
+            at = block_cols(order_ref, b, width)
+            gain = gain_ref[:, at]
+            parts[b] = parts[b] - normed_ref[:, at].astype(F32) * (1.0 / (gain * gain)) * dots
     refs[0][...] = parts[0]
     upper = pl.program_id(0) < half
 
@@ -652,7 +673,8 @@
     both_ref[:, ff:] = up_grad.astype(BF16)
     dots = jnp.sum(gate_grad * gate_act + up_grad * up_act, axis=1, keepdims=True)
     dots_ref[0] = jnp.broadcast_to(dots, (ROWS, 128)).T[0:8]
-    halves_blocks(half, order_ref, both_ref[...], w_ref, slice(0, 2 * ff), refs[17:])
+    halves_blocks(half, order_ref, both_ref[...], w_ref, slice(0, 2 * ff), refs[17:],
+                  (normed_ref, gain_ref, dots * (1.0 / gain_ref.shape[1])))
     send_blocks(order_ref, act_ref[...], w_ref, slice(2 * ff, 3 * ff), feed_ref, feed_send_ref)
 
 
@@ -916,14 +938,14 @@
         dots = sum_scalars(dots)[:, 0, :].reshape(tokens, 1)
         second_grad = sum_halves(*sends) * st["valid"]
         hat = st["hidden"] * scale
-        second_gain_grad = second_gain_grad + jnp.sum(second_grad * hat, axis=0)
-        st["hidden_grad"] = st["grad_out"] + scale * (
-            second_grad * second_local - hat * (dots * (1.0 / D)))
+        st["hidden_grad"] = st["grad_out"] + scale * (second_grad * second_local)
         st["pieces"] = gather_halves(st["hidden_grad"].astype(BF16))
         hidden, feed_own, feed_send = lax.optimization_barrier(
             (st["hidden"], feed_own, feed_send, st["pieces"][6]))[:3]
         feed = sum_direct(feed_own, feed_send)
         results.append(((hidden + feed) * st["valid"]).astype(BF16))
+        second_gain_grad = second_gain_grad + jnp.sum(
+            (second_grad + hat * dots / (D * second_local)) * hat, axis=0)
         gate_up_grad = gate_up_grad + contract_rows(normed, both)
         down_grad = down_grad + contract_rows(st["grad_full"], act)
     gate_up_low = gate_up_grad.astype(BF16)
@@ -942,36 +964,39 @@
         if st is state[-1]:
             out_low = out_weight_grad.astype(BF16)
             mixed_grad = after(mixed_grad, out_low)
-        dproj, dots, *grads = mixer_bwd(
+        dproj, dots, dot_cols, *grads = mixer_bwd(
             st["proj"], mixed_grad.reshape(per_part, length, vals), st["saved"], conv, rates,
             gain_row, heads, per_part, 0)
         small = small + jnp.concatenate([grad.reshape(-1) for grad in grads])
         st["dproj"] = dproj.reshape(tokens, -1)
         st["dots"] = sum_scalars(dots)
+        st["dot_cols"] = dot_cols.reshape(tokens, 1)
         in_weight_grad = in_weight_grad + contract_rows(
             st["normed"], after(st["dproj"], *results))
     in_low = in_weight_grad.astype(BF16)
     in_weight_grad = scatter_weight(after(in_low, out_low), dp)
     at = CONV * qkv + 2 * heads
-    gain_out = sum_scalars(small[at:].reshape(2, 128)).reshape(-1)
-    small_sums = sum_small(jnp.concatenate([small[:at], second_gain_grad, gain_out]))
     input_grads = []
     for st in state:
-        own, send = spread_product(after(st["dproj"], in_low, st["dots"]), in_weights, order)
-        first_grad = sum_features(own, send, small_sums) * st["valid"]
+        own, send = spread_product(after(st["dproj"], in_low), in_weights, order, st["normed"],
+                                   first_row, st["dot_cols"])
+        first_grad = sum_features(own, send) * st["valid"]
         hat = st["local"].astype(F32) * st["scale"]
-        first_gain_grad = first_gain_grad + jnp.sum(first_grad * hat, axis=0)
-        input_grads.append(st["hidden_grad"] + st["scale"] * (
-            first_grad * first_local - hat * (st["dots"].reshape(tokens, 1) * (1.0 / D))))
+        total = st["dots"].reshape(tokens, 1)
+        first_gain_grad = first_gain_grad + jnp.sum(
+            (first_grad + hat * total / (D * first_local)) * hat, axis=0)
+        input_grads.append(st["hidden_grad"] + st["scale"] * (first_grad * first_local))
     out_weight_grad = scatter_weight(out_low, dp)
-    first_gain_grad = sum_small(first_gain_grad)
+    small_sums = sum_small(
+        jnp.concatenate([small[:at], second_gain_grad, small[at:], first_gain_grad]))
+    gain_out = sum_scalars(small_sums[at + col_width : at + col_width + DV].reshape(2, 128))
     conv_grad = small_sums[: CONV * qkv].reshape(CONV, qkv)
     gate_at = qkv + vals
     qk = heads * DK
     return (
         jnp.concatenate(results, axis=0).reshape(seq_count, length, col_width),
         jnp.concatenate(input_grads, axis=0).reshape(seq_count, length, col_width),
-        first_gain_grad,
+        small_sums[at + col_width + DV :],
         in_weight_grad[:, :qk],
         in_weight_grad[:, qk : 2 * qk],
         in_weight_grad[:, 2 * qk : qkv],
@@ -983,7 +1008,7 @@
         conv_grad[:, 2 * qk :],
         small_sums[CONV * qkv : CONV * qkv + heads],
         small_sums[CONV * qkv + heads : at],
-        small_sums[at + col_width :],
+        gain_out.reshape(-1),
         out_weight_grad.T,
         small_sums[at : at + col_width],
         gate_up_grad[:, :ff],

time: 529 us -> 526 us (level)
  waiting for transfers between devices: 140 us -> 133 us
    ppermute x2 -> x1, starting transfers between devices: 14.1 us -> 0.08 us  [sum_small(): total = total + lax.ppermute(total, 'dp', [(0, 1), (1, 0)])]
    ppermute x4, starting transfers between devices: 4.31 us -> 14.7 us  [swap_cores(): other = lax.ppermute(mine, 'dp', [(0, 1), (1, 0)])]
    reduce_sum x1 -> x2, other arithmetic: 3.7 us -> 9.07 us  [the longest x1 6.55 us: on_device(): jnp.sum((first_grad + hat * total / (D * first_local)) * hat, axis=0)]
    unnamed x88 -> x96, local copies, waits for them, and re-layouts: 13.3 us -> 14.7 us
  transfers between devices with their start and end apart: 64 -> 60, of which waited for: 24 -> 20; matrix products, arithmetic and copies ran while one was open for 18% -> 19% of each run, Pallas kernels for 31% -> 31%
where the time goes in v4:
time: 526 us; the launch traced here: 517 us
  Pallas kernels  196 us (37%)
  waiting for transfers between devices  133 us (25%)
  starting transfers between devices  61.9 us (12%)
  other arithmetic  43 us (8%)
  matrix products  36.5 us (7%)
  local copies, waits for them, and re-layouts  32.3 us (6%)
  between operations  15.2 us (3%)
    ppermute x44, waiting for transfers between devices, send_col(): return lax.ppermute(values, 'col', xor_perm(4, bit))  130 us
    pallas_call x1, Pallas kernels, mixer_bwd(): pl.pallas_call(functools.partial(bwd_kernel, heads, nseq), out_shape=(jax...  68.4 us
    pallas_call x1, Pallas kernels, mixer_fwd(): pl.pallas_call(functools.partial(fwd_kernel, heads, nseq), out_shape=(jax...  47.5 us
    ppermute x44, starting transfers between devices, send_col(): return lax.ppermute(values, 'col', xor_perm(4, bit))  44.2 us
    dot_general x4, matrix products, contract_rows(): lax.dot_general(left, right, (((0,), (0,)), ((), ())), preferred_element_...  36.5 us
    pallas_call x1, Pallas kernels, feed_forward(): pl.pallas_call(functools.partial(feed_kernel, blocks // 2, length // ROWS...  34.3 us
    pallas_call x1, Pallas kernels, norm_project(): pl.pallas_call(functools.partial(project_kernel, blocks // 2, length // R...  15.7 us
    ppermute x4, starting transfers between devices, swap_cores(): other = lax.ppermute(mine, 'dp', [(0, 1), (1, 0)])  14.7 us
  transfers between devices with their start and end apart: 60, of which 20 were waited for; matrix products, arithmetic and copies ran while one was open for 19% of the time, Pallas kernels for 31%

profile of v4, /device:TPU:1, one launch (start us, length us, event | category | flops | bytes accessed | tf_op | source)
XLA Modules:
  0.0 517.4 jit_solution(16827729596570379219)
XLA Ops:
  15.4 20.9 %collective-permute-done.refs_1_ = bf16[2048,256]{1,0:T(8,128)(2,1)} collective-permute-done((bf16[2048,256]{1,0:T(8,128)(2,1)S(1)}, bf16[2048,256]{1,0:T(8,128)(2,1)}, u32[]{:S(2)}, u32[]{:S(2)}) %collective-permute-start) | collective-permute-done | bytes 1048608 | tf_op jit(solution)/shard_map/ppermute | solution.py:763
  43.7 7.1 %collective-permute-done.2.refs_3_ = bf16[1024,256]{1,0:T(8,128)(2,1)S(1)} collective-permute-done((bf16[1024,256]{1,0:T(8,128)(2,1)S(1)}, bf16[1024,256]{1,0:T(8,128)(2,1)S(1)}, u32[]{:S(2)}, u32[]{:S(2)}) %collective-permute-start.2) | collective-permute-done | bytes 524320 | tf_op jit(solution)/shard_map/ppermute | solution.py:763
  54.3 15.7 %norm_project.1 = (f32[2048,1664]{1,0:T(8,128)}, bf16[2048,1024]{1,0:T(8,128)(2,1)}, f32[2048,1]{1,0:T(8,128)}) custom-call(s32[2]{0:T(128)} %lens_ref.3, s32[4]{0:T(128)} %iota_xor_fusion.order_ref, bf16[2048,256]{1,0:T(8,128)(2,1)} %bitcast.94, bf16[2048,256]{1,0:T(8,128)(2,1)} %collective-permute-done.refs_1_, ...), custom_call_target="tpu_custom_call" | custom-call | flops 6979321856 | bytes 22020096 | tf_op jit(solution)/shard_map/norm_project/pallas_call | solution.py:554
  74.4 47.5 %mixer_fwd.1 = (bf16[2,1024,512]{2,1,0:T(8,128)(2,1)}, f32[2,1024,512]{2,1,0:T(8,128)}, f32[2,1024,512]{2,1,0:T(8,128)}, f32[2,8,2,128,256]{4,3,2,1,0:T(8,128)}, f32[2,8,2,128,128]{4,3,2,1,0:T(8,128)}) custom-call(f32[2,1024,1664]{2,1,0:T(8,128)} %bitcast.117, f32[4,1024]{1,0:T(4,128)} %maximum_convert_fusion.conv_ref, f32[2,128]{1,0:T(2,128)} %pad_maximum_fusion.4.rate_ref, ...), custom_call_target="tpu_custom_call" | custom-call | flops 24576000000 | bytes 27262976 | tf_op jit(solution)/shard_map/mixer_fwd/pallas_call | solution.py:224
  121.9 7.4 %spread_halves.1 = (f32[2048,256]{1,0:T(8,128)}, bf16[1024,256]{1,0:T(8,128)(2,1)}, bf16[1024,256]{1,0:T(8,128)(2,1)}, bf16[1024,256]{1,0:T(8,128)(2,1)}, bf16[1...) custom-call(s32[4]{0:T(128)} %iota_xor_fusion.order_ref, bf16[2048,512]{1,0:T(8,128)(2,1)} %bitcast.123, ...), custom_call_target="tpu_custom_call" | custom-call | flops 2147483648 | bytes 8388608 | tf_op jit(solution)/shard_map/spread_halves/pallas_call | solution.py:642
  132.0 9.8 %collective-permute-done.5 = bf16[1024,256]{1,0:T(8,128)(2,1)S(1)} collective-permute-done((bf16[1024,256]{1,0:T(8,128)(2,1)}, bf16[1024,256]{1,0:T(8,128)(2,1)S(1)}, u32[]{:S(2)}, u32[]{:S(2)}) %collective-permute-start.5) | collective-permute-done | bytes 524320 | tf_op jit(solution)/shard_map/ppermute | solution.py:763
  147.9 5.2 %collective-permute-done.4 = bf16[1024,256]{1,0:T(8,128)(2,1)S(1)} collective-permute-done((bf16[1024,256]{1,0:T(8,128)(2,1)}, bf16[1024,256]{1,0:T(8,128)(2,1)S(1)}, u32[]{:S(2)}, u32[]{:S(2)}) %collective-permute-start.4) | collective-permute-done | bytes 524320 | tf_op jit(solution)/shard_map/ppermute | solution.py:763
  153.2 11.0 %collective-permute-done.9 = bf16[1024,256]{1,0:T(8,128)(2,1)S(1)} collective-permute-done((bf16[1024,256]{1,0:T(8,128)(2,1)}, bf16[1024,256]{1,0:T(8,128)(2,1)S(1)}, u32[]{:S(2)}, u32[]{:S(2)}) %collective-permute-start.9) | collective-permute-done | bytes 524320 | tf_op jit(solution)/shard_map/ppermute | solution.py:763
  167.4 3.7 collective-permute-start.11
  172.6 8.4 %collective-permute-done.11.refs_2_ = bf16[1024,256]{1,0:T(8,128)(2,1)} collective-permute-done((bf16[1024,256]{1,0:T(8,128)(2,1)}, bf16[1024,256]{1,0:T(8,128)(2,1)}, u32[]{:S(2)}, u32[]{:S(2)}) %collective-permute-start.11) | collective-permute-done | bytes 524320 | tf_op jit(solution)/shard_map/ppermute | solution.py:763
  184.2 8.9 %collective-permute-done.13.refs_4_ = bf16[1024,256]{1,0:T(8,128)(2,1)} collective-permute-done((bf16[1024,256]{1,0:T(8,128)(2,1)}, bf16[1024,256]{1,0:T(8,128)(2,1)}, u32[]{:S(2)}, u32[]{:S(2)}) %collective-permute-start.13) | collective-permute-done | bytes 524320 | tf_op jit(solution)/shard_map/ppermute | solution.py:763
  193.2 11.2 %collective-permute-done.15.refs_6_ = bf16[1024,256]{1,0:T(8,128)(2,1)} collective-permute-done((bf16[1024,256]{1,0:T(8,128)(2,1)}, bf16[1024,256]{1,0:T(8,128)(2,1)}, u32[]{:S(2)}, u32[]{:S(2)}) %collective-permute-start.15) | collective-permute-done | bytes 524320 | tf_op jit(solution)/shard_map/ppermute | solution.py:763
  204.4 34.3 %feed_forward.1 = (bf16[2048,1024]{1,0:T(8,128)(2,1)}, f32[2048,1]{1,0:T(8,128)}, bf16[2048,768]{1,0:T(8,128)(2,1)}, bf16[2048,1536]{1,0:T(8,128)(2,1)}, f32[4,8...) custom-call(s32[2]{0:T(128)} %lens_ref.3, ...), custom_call_target="tpu_custom_call" | custom-call | flops 19327352832 | bytes 33554432 | tf_op jit(solution)/shard_map/feed_forward/pallas_call | solution.py:687
  243.0 11.8 %convolution_convert_fusion = bf16[1024,1536]{1,0:T(8,128)(2,1)} fusion(bf16[2048,1024]{1,0:T(8,128)(2,1)} %get-tuple-element.97, bf16[2048,1536]{1,0:T(8,128)(2,1)} %get-tuple-element.98), kind=kOutput, calls=%fused_computation | convolution fusion | flops 6444023808 | bytes 13631488 | tf_op jit(solution)/shard_map/dot_general | solution.py:751
  262.0 6.9 %convolution_convert_fusion.2 = bf16[1024,768]{1,0:T(8,128)(2,1)} fusion(bf16[2048,1024]{1,0:T(8,128)(2,1)} %all-gather.9.cloned.1.call-done.refs_7_, bf16[2048,768]{1,0:T(8,128)(2,1)S(1)} %copy-done.40), kind=kOutput, calls=%fused_computation.20 | convolution fusion | flops 3222011904 | bytes 8912896 | tf_op jit(solution)/shard_map/dot_general | solution.py:751
  271.4 6.1 %collective-permute-done.18 = bf16[1024,256]{1,0:T(8,128)(2,1)} collective-permute-done((bf16[1024,256]{1,0:T(8,128)(2,1)}, bf16[1024,256]{1,0:T(8,128)(2,1)}, u32[]{:S(2)}, u32[]{:S(2)}) %collective-permute-start.18) | collective-permute-done | bytes 524320 | tf_op jit(solution)/shard_map/ppermute | solution.py:763
  280.2 2.5 multiply_reduce_fusion
  287.1 5.5 %collective-permute-done.28.refs_3_ = bf16[1024,256]{1,0:T(8,128)(2,1)S(1)} collective-permute-done((bf16[1024,256]{1,0:T(8,128)(2,1)S(1)}, bf16[1024,256]{1,0:T(8,128)(2,1)S(1)}, u32[]{:S(2)}, u32[]{:S(2)}) %collective-permute-start.28) | collective-permute-done | bytes 524320 | tf_op jit(solution)/shard_map/ppermute | solution.py:763
  294.1 8.2 %collective-permute-done.27.refs_1_ = bf16[1024,256]{1,0:T(8,128)(2,1)S(1)} collective-permute-done((bf16[1024,256]{1,0:T(8,128)(2,1)S(1)}, bf16[1024,256]{1,0:T(8,128)(2,1)S(1)}, u32[]{:S(2)}, u32[]{:S(2)}) %collective-permute-start.27) | collective-permute-done | bytes 524320 | tf_op jit(solution)/shard_map/ppermute | solution.py:763
  302.5 10.9 %collective-permute-done.30.refs_5_ = bf16[1024,256]{1,0:T(8,128)(2,1)S(1)} collective-permute-done((bf16[1024,256]{1,0:T(8,128)(2,1)S(1)}, bf16[1024,256]{1,0:T(8,128)(2,1)S(1)}, u32[]{:S(2)}, u32[]{:S(2)}) %collective-permute-start.30) | collective-permute-done | bytes 524320 | tf_op jit(solution)/shard_map/ppermute | solution.py:763
  314.3 8.6 %join_product.1 = (bf16[2048,1024]{1,0:T(8,128)(2,1)}, f32[2048,512]{1,0:T(8,128)}) custom-call(s32[4]{0:T(128)} %iota_xor_fusion.order_ref, bf16[2048,256]{1,0:T(8,128)(2,1)} %copy-done.4, bf16[1024,256]{1,0:T(8,128)(2,1)} %copy-done.33, bf16[1024,256]{1,0:T(8,128)(2,1)} %copy-done.32, bf16[1024,256]{1,0:T(8,128)(2,1)} %copy-done.31, ...), custom_call_target="tpu_custom_call" | custom-call | flops 2147483648 | bytes 12582912 | tf_op jit(solution)/shard_map/join_product/pallas_call | solution.py:727
  322.9 6.2 %convolution_convert_fusion.3 = bf16[1024,512]{1,0:T(8,128)(2,1)} fusion(bf16[2048,1024]{1,0:T(8,128)(2,1)} %get-tuple-element.102, bf16[2048,512]{1,0:T(8,128)(2,1)} %bitcast.124), kind=kOutput, calls=%fused_computation.21 | convolution fusion | flops 2148007936 | bytes 7340032 | tf_op jit(solution)/shard_map/dot_general | solution.py:751
  329.9 3.6 slice_bitcast_fusion.2
  336.2 68.4 %mixer_bwd.1 = (bf16[2,1024,1664]{2,1,0:T(8,128)(2,1)}, f32[2,8,8,128]{3,2,1,0:T(8,128)}, f32[2,1024,1]{2,1,0:T(8,128)}, f32[32,1024]{1,0:T(8,128)}, f32[16,128]{1,0:T(8,128)}, /*index=5*/f32[8,256]{1,0:T(8,128)}) custom-call(f32[2,1024,1664]{2,1,0:T(8,128)} %bitcast.118, f32[2,1024,1664]{2,1,0:T(8,128)} %bitcast.119, f32[2,1024,512]{2,1,0:T(8,128)} %bitcast.122, ...), custom_call_target="tpu_custom_call" | custom-call | flops 40960000000 | bytes 27262976 | tf_op jit(solution)/shard_map/mixer_bwd/pallas_call | solution.py:425
  404.6 4.6 multiply_convert_fusion
  409.8 11.6 %convolution_convert_fusion.1 = bf16[1024,1664]{1,0:T(8,128)(2,1)} fusion(bf16[2048,1024]{1,0:T(8,128)(2,1)} %get-tuple-element.109.normed_ref, bf16[2048,1664]{1,0:T(8,128)(2,1)S(1)} %bitcast.121), kind=kOutput, calls=%fused_computation.1 | convolution fusion | flops 6981025792 | bytes 14417920 | tf_op jit(solution)/shard_map/dot_general | solution.py:751
  421.4 13.9 %spread_product.1 = (f32[2048,256]{1,0:T(8,128)}, bf16[3,2048,256]{2,1,0:T(8,128)(2,1)}) custom-call(s32[4]{0:T(128)} %iota_xor_fusion.order_ref, bf16[2048,1664]{1,0:T(8,128)(2,1)} %bitcast.120, bf16[1024,1664]{1,0:T(8,128)(2,1)} %all-gather.5.cloned.1.call-done.refs_6_.w_ref, bf16[2048,1024]{1,0:T(8,128)(2,1)} %get-tuple-element.109.normed_ref, ...), custom_call_target="tpu_custom_call" | custom-call | flops 6979321856 | bytes 13107200 | tf_op jit(solution)/shard_map/spread_product/pallas_call | solution.py:593
  439.5 6.0 %collective-permute-done.33 = bf16[1024,256]{1,0:T(8,128)(2,1)S(1)} collective-permute-done((bf16[1024,256]{1,0:T(8,128)(2,1)S(1)}, bf16[1024,256]{1,0:T(8,128)(2,1)S(1)}, u32[]{:S(2)}, u32[]{:S(2)}) %collective-permute-start.33) | collective-permute-done | bytes 524320 | tf_op jit(solution)/shard_map/ppermute | solution.py:763
  460.1 6.9 %collective-permute-done.40 = f32[2,8,128]{2,1,0:T(8,128)S(1)} collective-permute-done((f32[2,8,128]{2,1,0:T(8,128)S(1)}, f32[2,8,128]{2,1,0:T(8,128)S(1)}, u32[]{:S(2)}, u32[]{:S(2)}) %collective-permute-start.40) | collective-permute-done | bytes 8224 | tf_op jit(solution)/shard_map/ppermute | solution.py:763
  469.1 11.0 %collective-permute-start.51 = (bf16[128,768]{1,0:T(8,128)(2,1)}, bf16[128,768]{1,0:T(8,128)(2,1)S(1)}, u32[]{:S(2)}, u32[]{:S(2)}) collective-permute-start(bf16[128,768]{1,0:T(8,128)(2,1)} %reduce-scatter.11.cloned.1.call-done), channel_id=1, source_target_pairs={{0,16},{16,0},{1,17},{17,1},{2,18},{18,2},{3,19},{19,3},{4,20},{20... | collective-permute-start | bytes 589832 | tf_op jit(solution)/shard_map/ppermute | solution.py:823
  480.1 6.6 %fusion.5 = (f32[256]{0:T(256)}, f32[2048,256]{1,0:T(8,128)}) fusion(f32[256]{0:T(256)} %get-tuple-element.162, f32[2048]{0:T(1024)} %add_bitcast_fusion, f32[2048]{0:T(1024)} %reduce.1, f32[2048]{0:T(1024)S(1)} %bitcast.103, bf16[2048,256]{1,0:T(8,128)(2,1)} %collective-permute-done.34, f32[2048,256]{1,0:T(8,128)} %get-tuple-element.113, ...), kind=kLoop, calls=%fused_computation.17 | loop fusion | flops 9436928 | bytes 11571200 | tf_op jit(solution)/shard_map/reduce_sum | solution.py:986
  489.4 2.6 collective-permute-start.42
  (270 shorter events, 109.3 us)
Async XLA Ops:
  7.2 47.1 %all-gather.5.cloned.1.call-start = ((), (), s32[]{:S(2)}) async-start(), calls=%async_computation.4 | async-start | bytes 3833856 | tf_op jit(solution)/shard_map/all_gather | solution.py:834
  11.2 110.7 %all-gather.7.cloned.1.call-start = ((), (), s32[]{:S(2)}) async-start(), calls=%async_computation.5 | async-start | bytes 1179648 | tf_op jit(solution)/shard_map/all_gather | solution.py:834
  11.3 25.1 %collective-permute-start = (bf16[2048,256]{1,0:T(8,128)(2,1)S(1)}, bf16[2048,256]{1,0:T(8,128)(2,1)}, u32[]{:S(2)}, u32[]{:S(2)}) collective-permute-start(bf16[2048,256]{1,0:T(8,128)(2,1)S(1)} %bitcast.95), channel_id=1, source_target_pairs={{0,1},{1,0},{2,3},{3,2},{4,5},{5,4},{6,7},{7,6},{8,9},{9,8},{10,11... | collective-permute-start | bytes 3145736 | tf_op jit(solution)/shard_map/ppermute | solution.py:763
  13.4 24.2 %collective-permute-start.1 = (bf16[2048,256]{1,0:T(8,128)(2,1)S(1)}, bf16[2048,256]{1,0:T(8,128)(2,1)}, u32[]{:S(2)}, u32[]{:S(2)}) collective-permute-start(bf16[2048,256]{1,0:T(8,128)(2,1)S(1)} %bitcast.96), channel_id=1, source_target_pairs={{0,2},{1,3},{2,0},{3,1},{4,6},{5,7},{6,4},{7,5},{8,10},{9,11},{10,... | collective-permute-start | bytes 3145736 | tf_op jit(solution)/shard_map/ppermute | solution.py:763
  36.4 168.0 %all-gather.9.cloned.1.call-start = ((), (), s32[]{:S(2)}) async-start(), calls=%async_computation.6 | async-start | bytes 5242880 | tf_op jit(solution)/shard_map/all_gather | solution.py:923
  70.0 134.4 %all-gather.11.cloned.1.call-start = ((), (), s32[]{:S(2)}) async-start(), calls=%async_computation.7 | async-start | bytes 5308416 | tf_op jit(solution)/shard_map/all_gather | solution.py:834
  72.6 396.5 %reduce-scatter.11.cloned.1.call-start = ((), (), s32[]{:S(2)}) async-start(), calls=%async_computation.11 | async-start | bytes 1769472 | tf_op jit(solution)/shard_map/reduce_scatter | solution.py:838
  131.7 21.4 %collective-permute-start.4 = (bf16[1024,256]{1,0:T(8,128)(2,1)}, bf16[1024,256]{1,0:T(8,128)(2,1)S(1)}, u32[]{:S(2)}, u32[]{:S(2)}) collective-permute-start(bf16[1024,256]{1,0:T(8,128)(2,1)} %get-tuple-element.75), channel_id=1, source_target_pairs={{0,1},{1,0},{2,3},{3,2},{4,5},{5,4},{6,7},{7,6},{8,9},{9,8},{10,11... | collective-permute-start | bytes 1572872 | tf_op jit(solution)/shard_map/ppermute | solution.py:763
  144.3 19.9 %collective-permute-start.9 = (bf16[1024,256]{1,0:T(8,128)(2,1)}, bf16[1024,256]{1,0:T(8,128)(2,1)S(1)}, u32[]{:S(2)}, u32[]{:S(2)}) collective-permute-start(bf16[1024,256]{1,0:T(8,128)(2,1)} %get-tuple-element.80), channel_id=1, source_target_pairs={{0,2},{1,3},{2,0},{3,1},{4,6},{5,7},{6,4},{7,5},{8,10},{9,11},{10,... | collective-permute-start | bytes 1572872 | tf_op jit(solution)/shard_map/ppermute | solution.py:763
  145.8 18.5 %collective-permute-start.8 = (bf16[1024,256]{1,0:T(8,128)(2,1)S(1)}, bf16[1024,256]{1,0:T(8,128)(2,1)S(1)}, u32[]{:S(2)}, u32[]{:S(2)}) collective-permute-start(bf16[1024,256]{1,0:T(8,128)(2,1)S(1)} %add_convert_fusion.2), channel_id=1, source_target_pairs={{0,1},{1,0},{2,3},{3,2},{4,5},{5,4},{6,7},{7,6},{8,9},{9,8},{10,11... | collective-permute-start | bytes 1572872 | tf_op jit(solution)/shard_map/ppermute | solution.py:763
  172.5 20.7 %collective-permute-start.13 = (bf16[1024,256]{1,0:T(8,128)(2,1)}, bf16[1024,256]{1,0:T(8,128)(2,1)}, u32[]{:S(2)}, u32[]{:S(2)}) collective-permute-start(bf16[1024,256]{1,0:T(8,128)(2,1)} %get-tuple-element.193), channel_id=1, source_target_pairs={{0,2},{1,3},{2,0},{3,1},{4,6},{5,7},{6,4},{7,5},{8,10},{9,11},{10,... | collective-permute-start | bytes 1572872 | tf_op jit(solution)/shard_map/ppermute | solution.py:763
  172.6 20.5 %collective-permute-start.10 = (bf16[1024,256]{1,0:T(8,128)(2,1)}, bf16[1024,256]{1,0:T(8,128)(2,1)}, u32[]{:S(2)}, u32[]{:S(2)}) collective-permute-start(bf16[1024,256]{1,0:T(8,128)(2,1)} %get-tuple-element.194), channel_id=1, source_target_pairs={{0,1},{1,0},{2,3},{3,2},{4,5},{5,4},{6,7},{7,6},{8,9},{9,8},{10,11... | collective-permute-start | bytes 1572872 | tf_op jit(solution)/shard_map/ppermute | solution.py:763
  181.0 23.4 %collective-permute-start.15 = (bf16[1024,256]{1,0:T(8,128)(2,1)}, bf16[1024,256]{1,0:T(8,128)(2,1)}, u32[]{:S(2)}, u32[]{:S(2)}) collective-permute-start(bf16[1024,256]{1,0:T(8,128)(2,1)} %collective-permute-done.11.refs_2_), channel_id=1, source_target_pairs={{0,2},{1,3},{2,0},{3,1},{4,6},{5,7},{6,4},{7,5},{8,10},{9,11},{10,... | collective-permute-start | bytes 1572872 | tf_op jit(solution)/shard_map/ppermute | solution.py:763
  182.4 22.0 %collective-permute-start.14 = (bf16[1024,256]{1,0:T(8,128)(2,1)}, bf16[1024,256]{1,0:T(8,128)(2,1)}, u32[]{:S(2)}, u32[]{:S(2)}) collective-permute-start(bf16[1024,256]{1,0:T(8,128)(2,1)} %collective-permute-done.12.refs_3_), channel_id=1, source_target_pairs={{0,1},{1,0},{2,3},{3,2},{4,5},{5,4},{6,7},{7,6},{8,9},{9,8},{10,11... | collective-permute-start | bytes 1572872 | tf_op jit(solution)/shard_map/ppermute | solution.py:763
  238.7 21.5 %collective-permute-start.37 = (f32[4,8,512]{2,1,0:T(8,128)}, f32[4,8,512]{2,1,0:T(8,128)S(1)}, u32[]{:S(2)}, u32[]{:S(2)}) collective-permute-start(f32[4,8,512]{2,1,0:T(8,128)} %get-tuple-element.117), channel_id=1, source_target_pairs={{0,3},{1,2},{2,1},{3,0},{4,7},{5,6},{6,5},{7,4},{8,11},{9,10},{10,... | collective-permute-start | bytes 196616 | tf_op jit(solution)/shard_map/ppermute | solution.py:763
  240.1 21.4 %collective-permute-start.36 = (f32[4,8,512]{2,1,0:T(8,128)}, f32[4,8,512]{2,1,0:T(8,128)S(1)}, u32[]{:S(2)}, u32[]{:S(2)}) collective-permute-start(f32[4,8,512]{2,1,0:T(8,128)} %get-tuple-element.117), channel_id=1, source_target_pairs={{0,2},{1,3},{2,0},{3,1},{4,6},{5,7},{6,4},{7,5},{8,10},{9,11},{10,... | collective-permute-start | bytes 196616 | tf_op jit(solution)/shard_map/ppermute | solution.py:763
  240.2 30.3 %collective-permute-start.35 = (f32[4,8,512]{2,1,0:T(8,128)}, f32[4,8,512]{2,1,0:T(8,128)S(1)}, u32[]{:S(2)}, u32[]{:S(2)}) collective-permute-start(f32[4,8,512]{2,1,0:T(8,128)} %get-tuple-element.117), channel_id=1, source_target_pairs={{0,1},{1,0},{2,3},{3,2},{4,5},{5,4},{6,7},{7,6},{8,9},{9,8},{10,11... | collective-permute-start | bytes 196616 | tf_op jit(solution)/shard_map/ppermute | solution.py:763
  258.0 20.8 %collective-permute-start.21 = (bf16[1024,256]{1,0:T(8,128)(2,1)}, bf16[1024,256]{1,0:T(8,128)(2,1)}, u32[]{:S(2)}, u32[]{:S(2)}) collective-permute-start(bf16[1024,256]{1,0:T(8,128)(2,1)} %get-tuple-element.93), channel_id=1, source_target_pairs={{0,2},{1,3},{2,0},{3,1},{4,6},{5,7},{6,4},{7,5},{8,10},{9,11},{10,... | collective-permute-start | bytes 1572872 | tf_op jit(solution)/shard_map/ppermute | solution.py:763
  260.2 17.3 %collective-permute-start.18 = (bf16[1024,256]{1,0:T(8,128)(2,1)}, bf16[1024,256]{1,0:T(8,128)(2,1)}, u32[]{:S(2)}, u32[]{:S(2)}) collective-permute-start(bf16[1024,256]{1,0:T(8,128)(2,1)} %add_convert_fusion.1), channel_id=1, source_target_pairs={{0,2},{1,3},{2,0},{3,1},{4,6},{5,7},{6,4},{7,5},{8,10},{9,11},{10,... | collective-permute-start | bytes 1572872 | tf_op jit(solution)/shard_map/ppermute | solution.py:763
  261.5 17.4 %collective-permute-start.20 = (bf16[1024,256]{1,0:T(8,128)(2,1)}, bf16[1024,256]{1,0:T(8,128)(2,1)}, u32[]{:S(2)}, u32[]{:S(2)}) collective-permute-start(bf16[1024,256]{1,0:T(8,128)(2,1)} %add_convert_fusion), channel_id=1, source_target_pairs={{0,1},{1,0},{2,3},{3,2},{4,5},{5,4},{6,7},{7,6},{8,9},{9,8},{10,11... | collective-permute-start | bytes 1572872 | tf_op jit(solution)/shard_map/ppermute | solution.py:763
  268.9 219.8 %reduce-scatter.7.cloned.1.call-start = ((), (), s32[]{:S(2)}) async-start(), calls=%async_computation.9 | async-start | bytes 1179648 | tf_op jit(solution)/shard_map/reduce_scatter | solution.py:838
  285.0 17.2 %collective-permute-start.27 = (bf16[1024,256]{1,0:T(8,128)(2,1)S(1)}, bf16[1024,256]{1,0:T(8,128)(2,1)S(1)}, u32[]{:S(2)}, u32[]{:S(2)}) collective-permute-start(bf16[1024,256]{1,0:T(8,128)(2,1)S(1)} %get-tuple-element.191), channel_id=1, source_target_pairs={{0,1},{1,0},{2,3},{3,2},{4,5},{5,4},{6,7},{7,6},{8,9},{9,8},{10,11... | collective-permute-start | bytes 1572872 | tf_op jit(solution)/shard_map/ppermute | solution.py:763
  292.6 20.9 %collective-permute-start.30 = (bf16[1024,256]{1,0:T(8,128)(2,1)S(1)}, bf16[1024,256]{1,0:T(8,128)(2,1)S(1)}, u32[]{:S(2)}, u32[]{:S(2)}) collective-permute-start(bf16[1024,256]{1,0:T(8,128)(2,1)S(1)} %collective-permute-done.28.refs_3_), channel_id=1, source_target_pairs={{0,1},{1,0},{2,3},{3,2},{4,5},{5,4},{6,7},{7,6},{8,9},{9,8},{10,11... | collective-permute-start | bytes 1572872 | tf_op jit(solution)/shard_map/ppermute | solution.py:763
  293.4 20.9 %collective-permute-start.23 = (bf16[1024,256]{1,0:T(8,128)(2,1)S(1)}, bf16[1024,256]{1,0:T(8,128)(2,1)}, u32[]{:S(2)}, u32[]{:S(2)}) collective-permute-start(bf16[1024,256]{1,0:T(8,128)(2,1)S(1)} %collective-permute-done.22.refs_2_), channel_id=1, source_target_pairs={{0,2},{1,3},{2,0},{3,1},{4,6},{5,7},{6,4},{7,5},{8,10},{9,11},{10,... | collective-permute-start | bytes 1572872 | tf_op jit(solution)/shard_map/ppermute | solution.py:763
  329.1 168.8 %reduce-scatter.9.cloned.1.call-start = ((), (), s32[]{:S(2)}) async-start(), calls=%async_computation.10 | async-start | bytes 3538944 | tf_op jit(solution)/shard_map/reduce_scatter | solution.py:838
  329.9 171.7 %reduce-scatter.5.cloned.1.call-start = ((), (), s32[]{:S(2)}) async-start(), calls=%async_computation.8 | async-start | bytes 3833856 | tf_op jit(solution)/shard_map/reduce_scatter | solution.py:838
  333.5 71.1 %collective-permute-start.24 = (bf16[2048,256]{1,0:T(8,128)(2,1)}, bf16[2048,256]{1,0:T(8,128)(2,1)S(1)}, u32[]{:S(2)}, u32[]{:S(2)}) collective-permute-start(bf16[2048,256]{1,0:T(8,128)(2,1)} %get-tuple-element.178), channel_id=1, source_target_pairs={{0,1},{1,0},{2,3},{3,2},{4,5},{5,4},{6,7},{7,6},{8,9},{9,8},{10,11... | collective-permute-start | bytes 3145736 | tf_op jit(solution)/shard_map/ppermute | solution.py:763
  334.6 70.0 %collective-permute-start.26 = (bf16[2048,256]{1,0:T(8,128)(2,1)}, bf16[2048,256]{1,0:T(8,128)(2,1)}, u32[]{:S(2)}, u32[]{:S(2)}) collective-permute-start(bf16[2048,256]{1,0:T(8,128)(2,1)} %get-tuple-element.179), channel_id=1, source_target_pairs={{0,3},{1,2},{2,1},{3,0},{4,7},{5,6},{6,5},{7,4},{8,11},{9,10},{10,... | collective-permute-start | bytes 3145736 | tf_op jit(solution)/shard_map/ppermute | solution.py:763
  336.1 68.6 %collective-permute-start.25 = (bf16[2048,256]{1,0:T(8,128)(2,1)}, bf16[2048,256]{1,0:T(8,128)(2,1)}, u32[]{:S(2)}, u32[]{:S(2)}) collective-permute-start(bf16[2048,256]{1,0:T(8,128)(2,1)} %get-tuple-element.180), channel_id=1, source_target_pairs={{0,2},{1,3},{2,0},{3,1},{4,6},{5,7},{6,4},{7,5},{8,10},{9,11},{10,... | collective-permute-start | bytes 3145736 | tf_op jit(solution)/shard_map/ppermute | solution.py:763
  449.1 30.9 %collective-permute-start.34 = (bf16[2048,256]{1,0:T(8,128)(2,1)}, bf16[2048,256]{1,0:T(8,128)(2,1)}, u32[]{:S(2)}, u32[]{:S(2)}) collective-permute-start(bf16[2048,256]{1,0:T(8,128)(2,1)} %pad_maximum_fusion.1), channel_id=1, source_target_pairs={{0,2},{1,3},{2,0},{3,1},{4,6},{5,7},{6,4},{7,5},{8,10},{9,11},{10,... | collective-permute-start | bytes 3145736 | tf_op jit(solution)/shard_map/ppermute | solution.py:763
  451.7 28.4 %collective-permute-start.32 = (bf16[2048,256]{1,0:T(8,128)(2,1)}, bf16[2048,256]{1,0:T(8,128)(2,1)}, u32[]{:S(2)}, u32[]{:S(2)}) collective-permute-start(bf16[2048,256]{1,0:T(8,128)(2,1)} %pad_maximum_fusion), channel_id=1, source_target_pairs={{0,1},{1,0},{2,3},{3,2},{4,5},{5,4},{6,7},{7,6},{8,9},{9,8},{10,11... | collective-permute-start | bytes 3145736 | tf_op jit(solution)/shard_map/ppermute | solution.py:763
  469.1 18.5 %collective-permute-start.51 = (bf16[128,768]{1,0:T(8,128)(2,1)}, bf16[128,768]{1,0:T(8,128)(2,1)S(1)}, u32[]{:S(2)}, u32[]{:S(2)}) collective-permute-start(bf16[128,768]{1,0:T(8,128)(2,1)} %reduce-scatter.11.cloned.1.call-done), channel_id=1, source_target_pairs={{0,16},{16,0},{1,17},{17,1},{2,18},{18,2},{3,19},{19,3},{4,20},{20... | collective-permute-start | bytes 589832 | tf_op jit(solution)/shard_map/ppermute | solution.py:823
  (69 other events, 828.9 us)
Sparse Core Ops, SparseCore 0:
  11.3 42.9 all-gather.4
  56.5 20.9 all-gather.6
  79.3 51.7 all-gather.8
  133.2 52.3 all-gather.10
  269.0 33.4 reduce-scatter.10
  329.2 33.6 reduce-scatter.6
  365.2 39.6 reduce-scatter.8
  421.5 46.1 reduce-scatter.4

commit v5 on v4

--- a/solution.py
+++ b/solution.py
@@ -987,9 +987,9 @@
             (first_grad + hat * total / (D * first_local)) * hat, axis=0)
         input_grads.append(st["hidden_grad"] + st["scale"] * (first_grad * first_local))
     out_weight_grad = scatter_weight(out_low, dp)
+    gain_out = sum_scalars(small[at:].reshape(2, 128)).reshape(-1)
     small_sums = sum_small(
-        jnp.concatenate([small[:at], second_gain_grad, small[at:], first_gain_grad]))
-    gain_out = sum_scalars(small_sums[at + col_width : at + col_width + DV].reshape(2, 128))
+        jnp.concatenate([small[:at], second_gain_grad, gain_out, first_gain_grad]))
     conv_grad = small_sums[: CONV * qkv].reshape(CONV, qkv)
     gate_at = qkv + vals
     qk = heads * DK
@@ -1008,7 +1008,7 @@
         conv_grad[:, 2 * qk :],
         small_sums[CONV * qkv : CONV * qkv + heads],
         small_sums[CONV * qkv + heads : at],
-        gain_out.reshape(-1),
+        small_sums[at + col_width : at + col_width + DV],
         out_weight_grad.T,
         small_sums[at : at + col_width],
         gate_up_grad[:, :ff],

time: 526 us -> 527 us (level)
  transfers between devices with their start and end apart: 60 -> 60, of which waited for: 20 -> 23; matrix products, arithmetic and copies ran while one was open for 19% -> 19% of each run, Pallas kernels for 31% -> 31%
where the time goes in v5:
time: 527 us; the launch traced here: 518 us
  Pallas kernels  196 us (37%)
  waiting for transfers between devices  135 us (26%)
  starting transfers between devices  60.8 us (12%)
  other arithmetic  42.4 us (8%)
  matrix products  36.5 us (7%)
  local copies, waits for them, and re-layouts  32.3 us (6%)
  between operations  15.2 us (3%)
    ppermute x44, waiting for transfers between devices, send_col(): return lax.ppermute(values, 'col', xor_perm(4, bit))  132 us
    pallas_call x1, Pallas kernels, mixer_bwd(): pl.pallas_call(functools.partial(bwd_kernel, heads, nseq), out_shape=(jax...  68.4 us
    pallas_call x1, Pallas kernels, mixer_fwd(): pl.pallas_call(functools.partial(fwd_kernel, heads, nseq), out_shape=(jax...  47.5 us
    ppermute x44, starting transfers between devices, send_col(): return lax.ppermute(values, 'col', xor_perm(4, bit))  44.2 us
    dot_general x4, matrix products, contract_rows(): lax.dot_general(left, right, (((0,), (0,)), ((), ())), preferred_element_...  36.5 us
    pallas_call x1, Pallas kernels, feed_forward(): pl.pallas_call(functools.partial(feed_kernel, blocks // 2, length // ROWS...  34.3 us
    pallas_call x1, Pallas kernels, norm_project(): pl.pallas_call(functools.partial(project_kernel, blocks // 2, length // R...  15.7 us
    unnamed x96, local copies, waits for them, and re-layouts  14.7 us
  transfers between devices with their start and end apart: 60, of which 23 were waited for; matrix products, arithmetic and copies ran while one was open for 19% of the time, Pallas kernels for 31%

profile of v5, /device:TPU:1, one launch (start us, length us, event | category | flops | bytes accessed | tf_op | source)
XLA Modules:
  0.0 517.7 jit_solution(10035712522531452931)
XLA Ops:
  15.4 20.9 %collective-permute-done.refs_1_ = bf16[2048,256]{1,0:T(8,128)(2,1)} collective-permute-done((bf16[2048,256]{1,0:T(8,128)(2,1)S(1)}, bf16[2048,256]{1,0:T(8,128)(2,1)}, u32[]{:S(2)}, u32[]{:S(2)}) %collective-permute-start) | collective-permute-done | bytes 1048608 | tf_op jit(solution)/shard_map/ppermute | solution.py:763
  43.7 7.1 %collective-permute-done.2.refs_3_ = bf16[1024,256]{1,0:T(8,128)(2,1)S(1)} collective-permute-done((bf16[1024,256]{1,0:T(8,128)(2,1)S(1)}, bf16[1024,256]{1,0:T(8,128)(2,1)S(1)}, u32[]{:S(2)}, u32[]{:S(2)}) %collective-permute-start.2) | collective-permute-done | bytes 524320 | tf_op jit(solution)/shard_map/ppermute | solution.py:763
  54.3 15.7 %norm_project.1 = (f32[2048,1664]{1,0:T(8,128)}, bf16[2048,1024]{1,0:T(8,128)(2,1)}, f32[2048,1]{1,0:T(8,128)}) custom-call(s32[2]{0:T(128)} %lens_ref.3, s32[4]{0:T(128)} %iota_xor_fusion.order_ref, bf16[2048,256]{1,0:T(8,128)(2,1)} %bitcast.92, bf16[2048,256]{1,0:T(8,128)(2,1)} %collective-permute-done.refs_1_, ...), custom_call_target="tpu_custom_call" | custom-call | flops 6979321856 | bytes 22020096 | tf_op jit(solution)/shard_map/norm_project/pallas_call | solution.py:554
  74.4 47.5 %mixer_fwd.1 = (bf16[2,1024,512]{2,1,0:T(8,128)(2,1)}, f32[2,1024,512]{2,1,0:T(8,128)}, f32[2,1024,512]{2,1,0:T(8,128)}, f32[2,8,2,128,256]{4,3,2,1,0:T(8,128)}, f32[2,8,2,128,128]{4,3,2,1,0:T(8,128)}) custom-call(f32[2,1024,1664]{2,1,0:T(8,128)} %bitcast.117, f32[4,1024]{1,0:T(4,128)} %maximum_convert_fusion.conv_ref, f32[2,128]{1,0:T(2,128)} %pad_maximum_fusion.4.rate_ref, ...), custom_call_target="tpu_custom_call" | custom-call | flops 24576000000 | bytes 27262976 | tf_op jit(solution)/shard_map/mixer_fwd/pallas_call | solution.py:224
  121.9 7.4 %spread_halves.1 = (f32[2048,256]{1,0:T(8,128)}, bf16[1024,256]{1,0:T(8,128)(2,1)}, bf16[1024,256]{1,0:T(8,128)(2,1)}, bf16[1024,256]{1,0:T(8,128)(2,1)}, bf16[1...) custom-call(s32[4]{0:T(128)} %iota_xor_fusion.order_ref, bf16[2048,512]{1,0:T(8,128)(2,1)} %bitcast.123, ...), custom_call_target="tpu_custom_call" | custom-call | flops 2147483648 | bytes 8388608 | tf_op jit(solution)/shard_map/spread_halves/pallas_call | solution.py:642
  132.0 9.8 %collective-permute-done.5 = bf16[1024,256]{1,0:T(8,128)(2,1)S(1)} collective-permute-done((bf16[1024,256]{1,0:T(8,128)(2,1)}, bf16[1024,256]{1,0:T(8,128)(2,1)S(1)}, u32[]{:S(2)}, u32[]{:S(2)}) %collective-permute-start.5) | collective-permute-done | bytes 524320 | tf_op jit(solution)/shard_map/ppermute | solution.py:763
  147.9 5.2 %collective-permute-done.4 = bf16[1024,256]{1,0:T(8,128)(2,1)S(1)} collective-permute-done((bf16[1024,256]{1,0:T(8,128)(2,1)}, bf16[1024,256]{1,0:T(8,128)(2,1)S(1)}, u32[]{:S(2)}, u32[]{:S(2)}) %collective-permute-start.4) | collective-permute-done | bytes 524320 | tf_op jit(solution)/shard_map/ppermute | solution.py:763
  153.2 11.0 %collective-permute-done.9 = bf16[1024,256]{1,0:T(8,128)(2,1)S(1)} collective-permute-done((bf16[1024,256]{1,0:T(8,128)(2,1)}, bf16[1024,256]{1,0:T(8,128)(2,1)S(1)}, u32[]{:S(2)}, u32[]{:S(2)}) %collective-permute-start.9) | collective-permute-done | bytes 524320 | tf_op jit(solution)/shard_map/ppermute | solution.py:763
  167.4 3.7 collective-permute-start.11
  172.6 8.4 %collective-permute-done.11.refs_2_ = bf16[1024,256]{1,0:T(8,128)(2,1)} collective-permute-done((bf16[1024,256]{1,0:T(8,128)(2,1)}, bf16[1024,256]{1,0:T(8,128)(2,1)}, u32[]{:S(2)}, u32[]{:S(2)}) %collective-permute-start.11) | collective-permute-done | bytes 524320 | tf_op jit(solution)/shard_map/ppermute | solution.py:763
  184.2 8.9 %collective-permute-done.13.refs_4_ = bf16[1024,256]{1,0:T(8,128)(2,1)} collective-permute-done((bf16[1024,256]{1,0:T(8,128)(2,1)}, bf16[1024,256]{1,0:T(8,128)(2,1)}, u32[]{:S(2)}, u32[]{:S(2)}) %collective-permute-start.13) | collective-permute-done | bytes 524320 | tf_op jit(solution)/shard_map/ppermute | solution.py:763
  193.2 11.2 %collective-permute-done.15.refs_6_ = bf16[1024,256]{1,0:T(8,128)(2,1)} collective-permute-done((bf16[1024,256]{1,0:T(8,128)(2,1)}, bf16[1024,256]{1,0:T(8,128)(2,1)}, u32[]{:S(2)}, u32[]{:S(2)}) %collective-permute-start.15) | collective-permute-done | bytes 524320 | tf_op jit(solution)/shard_map/ppermute | solution.py:763
  204.4 34.3 %feed_forward.1 = (bf16[2048,1024]{1,0:T(8,128)(2,1)}, f32[2048,1]{1,0:T(8,128)}, bf16[2048,768]{1,0:T(8,128)(2,1)}, bf16[2048,1536]{1,0:T(8,128)(2,1)}, f32[4,8...) custom-call(s32[2]{0:T(128)} %lens_ref.3, ...), custom_call_target="tpu_custom_call" | custom-call | flops 19327352832 | bytes 33554432 | tf_op jit(solution)/shard_map/feed_forward/pallas_call | solution.py:687
  243.0 11.8 %convolution_convert_fusion = bf16[1024,1536]{1,0:T(8,128)(2,1)} fusion(bf16[2048,1024]{1,0:T(8,128)(2,1)} %get-tuple-element.97, bf16[2048,1536]{1,0:T(8,128)(2,1)} %get-tuple-element.98), kind=kOutput, calls=%fused_computation | convolution fusion | flops 6444023808 | bytes 13631488 | tf_op jit(solution)/shard_map/dot_general | solution.py:751
  262.0 6.9 %convolution_convert_fusion.2 = bf16[1024,768]{1,0:T(8,128)(2,1)} fusion(bf16[2048,1024]{1,0:T(8,128)(2,1)} %all-gather.9.cloned.1.call-done.refs_7_, bf16[2048,768]{1,0:T(8,128)(2,1)S(1)} %copy-done.40), kind=kOutput, calls=%fused_computation.20 | convolution fusion | flops 3222011904 | bytes 8912896 | tf_op jit(solution)/shard_map/dot_general | solution.py:751
  271.4 6.1 %collective-permute-done.18 = bf16[1024,256]{1,0:T(8,128)(2,1)} collective-permute-done((bf16[1024,256]{1,0:T(8,128)(2,1)}, bf16[1024,256]{1,0:T(8,128)(2,1)}, u32[]{:S(2)}, u32[]{:S(2)}) %collective-permute-start.18) | collective-permute-done | bytes 524320 | tf_op jit(solution)/shard_map/ppermute | solution.py:763
  280.2 2.5 multiply_reduce_fusion
  287.1 5.5 %collective-permute-done.28.refs_3_ = bf16[1024,256]{1,0:T(8,128)(2,1)S(1)} collective-permute-done((bf16[1024,256]{1,0:T(8,128)(2,1)S(1)}, bf16[1024,256]{1,0:T(8,128)(2,1)S(1)}, u32[]{:S(2)}, u32[]{:S(2)}) %collective-permute-start.28) | collective-permute-done | bytes 524320 | tf_op jit(solution)/shard_map/ppermute | solution.py:763
  294.1 8.2 %collective-permute-done.27.refs_1_ = bf16[1024,256]{1,0:T(8,128)(2,1)S(1)} collective-permute-done((bf16[1024,256]{1,0:T(8,128)(2,1)S(1)}, bf16[1024,256]{1,0:T(8,128)(2,1)S(1)}, u32[]{:S(2)}, u32[]{:S(2)}) %collective-permute-start.27) | collective-permute-done | bytes 524320 | tf_op jit(solution)/shard_map/ppermute | solution.py:763
  302.5 10.9 %collective-permute-done.30.refs_5_ = bf16[1024,256]{1,0:T(8,128)(2,1)S(1)} collective-permute-done((bf16[1024,256]{1,0:T(8,128)(2,1)S(1)}, bf16[1024,256]{1,0:T(8,128)(2,1)S(1)}, u32[]{:S(2)}, u32[]{:S(2)}) %collective-permute-start.30) | collective-permute-done | bytes 524320 | tf_op jit(solution)/shard_map/ppermute | solution.py:763
  314.3 8.6 %join_product.1 = (bf16[2048,1024]{1,0:T(8,128)(2,1)}, f32[2048,512]{1,0:T(8,128)}) custom-call(s32[4]{0:T(128)} %iota_xor_fusion.order_ref, bf16[2048,256]{1,0:T(8,128)(2,1)} %copy-done.4, bf16[1024,256]{1,0:T(8,128)(2,1)} %copy-done.33, bf16[1024,256]{1,0:T(8,128)(2,1)} %copy-done.32, bf16[1024,256]{1,0:T(8,128)(2,1)} %copy-done.31, ...), custom_call_target="tpu_custom_call" | custom-call | flops 2147483648 | bytes 12582912 | tf_op jit(solution)/shard_map/join_product/pallas_call | solution.py:727
  322.9 6.2 %convolution_convert_fusion.3 = bf16[1024,512]{1,0:T(8,128)(2,1)} fusion(bf16[2048,1024]{1,0:T(8,128)(2,1)} %get-tuple-element.102, bf16[2048,512]{1,0:T(8,128)(2,1)} %bitcast.124), kind=kOutput, calls=%fused_computation.21 | convolution fusion | flops 2148007936 | bytes 7340032 | tf_op jit(solution)/shard_map/dot_general | solution.py:751
  329.9 3.6 slice_bitcast_fusion.2
  336.2 68.4 %mixer_bwd.1 = (bf16[2,1024,1664]{2,1,0:T(8,128)(2,1)}, f32[2,8,8,128]{3,2,1,0:T(8,128)}, f32[2,1024,1]{2,1,0:T(8,128)}, f32[32,1024]{1,0:T(8,128)}, f32[16,128]{1,0:T(8,128)}, /*index=5*/f32[8,256]{1,0:T(8,128)}) custom-call(f32[2,1024,1664]{2,1,0:T(8,128)} %bitcast.118, f32[2,1024,1664]{2,1,0:T(8,128)} %bitcast.119, f32[2,1024,512]{2,1,0:T(8,128)} %bitcast.122, ...), custom_call_target="tpu_custom_call" | custom-call | flops 40960000000 | bytes 27262976 | tf_op jit(solution)/shard_map/mixer_bwd/pallas_call | solution.py:425
  404.6 4.6 multiply_convert_fusion
  409.8 11.6 %convolution_convert_fusion.1 = bf16[1024,1664]{1,0:T(8,128)(2,1)} fusion(bf16[2048,1024]{1,0:T(8,128)(2,1)} %get-tuple-element.109.normed_ref, bf16[2048,1664]{1,0:T(8,128)(2,1)S(1)} %bitcast.121), kind=kOutput, calls=%fused_computation.1 | convolution fusion | flops 6981025792 | bytes 14417920 | tf_op jit(solution)/shard_map/dot_general | solution.py:751
  421.4 13.9 %spread_product.1 = (f32[2048,256]{1,0:T(8,128)}, bf16[3,2048,256]{2,1,0:T(8,128)(2,1)}) custom-call(s32[4]{0:T(128)} %iota_xor_fusion.order_ref, bf16[2048,1664]{1,0:T(8,128)(2,1)} %bitcast.120, bf16[1024,1664]{1,0:T(8,128)(2,1)} %all-gather.5.cloned.1.call-done.refs_6_.w_ref, bf16[2048,1024]{1,0:T(8,128)(2,1)} %get-tuple-element.109.normed_ref, ...), custom_call_target="tpu_custom_call" | custom-call | flops 6979321856 | bytes 13107200 | tf_op jit(solution)/shard_map/spread_product/pallas_call | solution.py:593
  439.5 6.0 %collective-permute-done.33 = bf16[1024,256]{1,0:T(8,128)(2,1)S(1)} collective-permute-done((bf16[1024,256]{1,0:T(8,128)(2,1)S(1)}, bf16[1024,256]{1,0:T(8,128)(2,1)S(1)}, u32[]{:S(2)}, u32[]{:S(2)}) %collective-permute-start.33) | collective-permute-done | bytes 524320 | tf_op jit(solution)/shard_map/ppermute | solution.py:763
  459.6 8.6 %collective-permute-done.39 = f32[2,128]{1,0:T(2,128)S(1)} collective-permute-done((f32[2,128]{1,0:T(2,128)S(1)}, f32[2,128]{1,0:T(2,128)S(1)}, u32[]{:S(2)}, u32[]{:S(2)}) %collective-permute-start.39) | collective-permute-done | bytes 1056 | tf_op jit(solution)/shard_map/ppermute | solution.py:763
  473.5 12.0 %collective-permute-start.51 = (bf16[128,768]{1,0:T(8,128)(2,1)}, bf16[128,768]{1,0:T(8,128)(2,1)S(1)}, u32[]{:S(2)}, u32[]{:S(2)}) collective-permute-start(bf16[128,768]{1,0:T(8,128)(2,1)} %reduce-scatter.11.cloned.1.call-done), channel_id=1, source_target_pairs={{0,16},{16,0},{1,17},{17,1},{2,18},{18,2},{3,19},{19,3},{4,20},{20... | collective-permute-start | bytes 589832 | tf_op jit(solution)/shard_map/ppermute | solution.py:823
  485.5 6.6 %fusion.5 = (f32[256]{0:T(256)}, f32[2048,256]{1,0:T(8,128)}) fusion(f32[256]{0:T(256)} %get-tuple-element.162, f32[2048]{0:T(1024)} %add_bitcast_fusion, f32[2048]{0:T(1024)} %reduce.1, f32[2048]{0:T(1024)S(1)} %bitcast.101, bf16[2048,256]{1,0:T(8,128)(2,1)} %collective-permute-done.34, f32[2048,256]{1,0:T(8,128)} %get-tuple-element.113, ...), kind=kLoop, calls=%fused_computation.17 | loop fusion | flops 9436928 | bytes 11571200 | tf_op jit(solution)/shard_map/reduce_sum | solution.py:986
  494.8 2.6 collective-permute-start.45
  (270 shorter events, 106.8 us)
Async XLA Ops:
  7.2 47.1 %all-gather.5.cloned.1.call-start = ((), (), s32[]{:S(2)}) async-start(), calls=%async_computation.4 | async-start | bytes 3833856 | tf_op jit(solution)/shard_map/all_gather | solution.py:834
  11.2 110.7 %all-gather.7.cloned.1.call-start = ((), (), s32[]{:S(2)}) async-start(), calls=%async_computation.5 | async-start | bytes 1179648 | tf_op jit(solution)/shard_map/all_gather | solution.py:834
  11.3 25.1 %collective-permute-start = (bf16[2048,256]{1,0:T(8,128)(2,1)S(1)}, bf16[2048,256]{1,0:T(8,128)(2,1)}, u32[]{:S(2)}, u32[]{:S(2)}) collective-permute-start(bf16[2048,256]{1,0:T(8,128)(2,1)S(1)} %bitcast.93), channel_id=1, source_target_pairs={{0,1},{1,0},{2,3},{3,2},{4,5},{5,4},{6,7},{7,6},{8,9},{9,8},{10,11... | collective-permute-start | bytes 3145736 | tf_op jit(solution)/shard_map/ppermute | solution.py:763
  13.4 24.2 %collective-permute-start.1 = (bf16[2048,256]{1,0:T(8,128)(2,1)S(1)}, bf16[2048,256]{1,0:T(8,128)(2,1)}, u32[]{:S(2)}, u32[]{:S(2)}) collective-permute-start(bf16[2048,256]{1,0:T(8,128)(2,1)S(1)} %bitcast.94), channel_id=1, source_target_pairs={{0,2},{1,3},{2,0},{3,1},{4,6},{5,7},{6,4},{7,5},{8,10},{9,11},{10,... | collective-permute-start | bytes 3145736 | tf_op jit(solution)/shard_map/ppermute | solution.py:763
  36.4 168.0 %all-gather.9.cloned.1.call-start = ((), (), s32[]{:S(2)}) async-start(), calls=%async_computation.6 | async-start | bytes 5242880 | tf_op jit(solution)/shard_map/all_gather | solution.py:923
  70.0 134.4 %all-gather.11.cloned.1.call-start = ((), (), s32[]{:S(2)}) async-start(), calls=%async_computation.7 | async-start | bytes 5308416 | tf_op jit(solution)/shard_map/all_gather | solution.py:834
  72.6 400.9 %reduce-scatter.11.cloned.1.call-start = ((), (), s32[]{:S(2)}) async-start(), calls=%async_computation.11 | async-start | bytes 1769472 | tf_op jit(solution)/shard_map/reduce_scatter | solution.py:838
  131.7 21.4 %collective-permute-start.4 = (bf16[1024,256]{1,0:T(8,128)(2,1)}, bf16[1024,256]{1,0:T(8,128)(2,1)S(1)}, u32[]{:S(2)}, u32[]{:S(2)}) collective-permute-start(bf16[1024,256]{1,0:T(8,128)(2,1)} %get-tuple-element.75), channel_id=1, source_target_pairs={{0,1},{1,0},{2,3},{3,2},{4,5},{5,4},{6,7},{7,6},{8,9},{9,8},{10,11... | collective-permute-start | bytes 1572872 | tf_op jit(solution)/shard_map/ppermute | solution.py:763
  144.3 19.9 %collective-permute-start.9 = (bf16[1024,256]{1,0:T(8,128)(2,1)}, bf16[1024,256]{1,0:T(8,128)(2,1)S(1)}, u32[]{:S(2)}, u32[]{:S(2)}) collective-permute-start(bf16[1024,256]{1,0:T(8,128)(2,1)} %get-tuple-element.80), channel_id=1, source_target_pairs={{0,2},{1,3},{2,0},{3,1},{4,6},{5,7},{6,4},{7,5},{8,10},{9,11},{10,... | collective-permute-start | bytes 1572872 | tf_op jit(solution)/shard_map/ppermute | solution.py:763
  145.8 18.5 %collective-permute-start.8 = (bf16[1024,256]{1,0:T(8,128)(2,1)S(1)}, bf16[1024,256]{1,0:T(8,128)(2,1)S(1)}, u32[]{:S(2)}, u32[]{:S(2)}) collective-permute-start(bf16[1024,256]{1,0:T(8,128)(2,1)S(1)} %add_convert_fusion.2), channel_id=1, source_target_pairs={{0,1},{1,0},{2,3},{3,2},{4,5},{5,4},{6,7},{7,6},{8,9},{9,8},{10,11... | collective-permute-start | bytes 1572872 | tf_op jit(solution)/shard_map/ppermute | solution.py:763
  172.5 20.7 %collective-permute-start.13 = (bf16[1024,256]{1,0:T(8,128)(2,1)}, bf16[1024,256]{1,0:T(8,128)(2,1)}, u32[]{:S(2)}, u32[]{:S(2)}) collective-permute-start(bf16[1024,256]{1,0:T(8,128)(2,1)} %get-tuple-element.193), channel_id=1, source_target_pairs={{0,2},{1,3},{2,0},{3,1},{4,6},{5,7},{6,4},{7,5},{8,10},{9,11},{10,... | collective-permute-start | bytes 1572872 | tf_op jit(solution)/shard_map/ppermute | solution.py:763
  172.6 20.5 %collective-permute-start.10 = (bf16[1024,256]{1,0:T(8,128)(2,1)}, bf16[1024,256]{1,0:T(8,128)(2,1)}, u32[]{:S(2)}, u32[]{:S(2)}) collective-permute-start(bf16[1024,256]{1,0:T(8,128)(2,1)} %get-tuple-element.194), channel_id=1, source_target_pairs={{0,1},{1,0},{2,3},{3,2},{4,5},{5,4},{6,7},{7,6},{8,9},{9,8},{10,11... | collective-permute-start | bytes 1572872 | tf_op jit(solution)/shard_map/ppermute | solution.py:763
  181.0 23.4 %collective-permute-start.15 = (bf16[1024,256]{1,0:T(8,128)(2,1)}, bf16[1024,256]{1,0:T(8,128)(2,1)}, u32[]{:S(2)}, u32[]{:S(2)}) collective-permute-start(bf16[1024,256]{1,0:T(8,128)(2,1)} %collective-permute-done.11.refs_2_), channel_id=1, source_target_pairs={{0,2},{1,3},{2,0},{3,1},{4,6},{5,7},{6,4},{7,5},{8,10},{9,11},{10,... | collective-permute-start | bytes 1572872 | tf_op jit(solution)/shard_map/ppermute | solution.py:763
  182.4 22.0 %collective-permute-start.14 = (bf16[1024,256]{1,0:T(8,128)(2,1)}, bf16[1024,256]{1,0:T(8,128)(2,1)}, u32[]{:S(2)}, u32[]{:S(2)}) collective-permute-start(bf16[1024,256]{1,0:T(8,128)(2,1)} %collective-permute-done.12.refs_3_), channel_id=1, source_target_pairs={{0,1},{1,0},{2,3},{3,2},{4,5},{5,4},{6,7},{7,6},{8,9},{9,8},{10,11... | collective-permute-start | bytes 1572872 | tf_op jit(solution)/shard_map/ppermute | solution.py:763
  238.7 21.5 %collective-permute-start.37 = (f32[4,8,512]{2,1,0:T(8,128)}, f32[4,8,512]{2,1,0:T(8,128)S(1)}, u32[]{:S(2)}, u32[]{:S(2)}) collective-permute-start(f32[4,8,512]{2,1,0:T(8,128)} %get-tuple-element.117), channel_id=1, source_target_pairs={{0,3},{1,2},{2,1},{3,0},{4,7},{5,6},{6,5},{7,4},{8,11},{9,10},{10,... | collective-permute-start | bytes 196616 | tf_op jit(solution)/shard_map/ppermute | solution.py:763
  240.1 21.4 %collective-permute-start.36 = (f32[4,8,512]{2,1,0:T(8,128)}, f32[4,8,512]{2,1,0:T(8,128)S(1)}, u32[]{:S(2)}, u32[]{:S(2)}) collective-permute-start(f32[4,8,512]{2,1,0:T(8,128)} %get-tuple-element.117), channel_id=1, source_target_pairs={{0,2},{1,3},{2,0},{3,1},{4,6},{5,7},{6,4},{7,5},{8,10},{9,11},{10,... | collective-permute-start | bytes 196616 | tf_op jit(solution)/shard_map/ppermute | solution.py:763
  240.2 30.3 %collective-permute-start.35 = (f32[4,8,512]{2,1,0:T(8,128)}, f32[4,8,512]{2,1,0:T(8,128)S(1)}, u32[]{:S(2)}, u32[]{:S(2)}) collective-permute-start(f32[4,8,512]{2,1,0:T(8,128)} %get-tuple-element.117), channel_id=1, source_target_pairs={{0,1},{1,0},{2,3},{3,2},{4,5},{5,4},{6,7},{7,6},{8,9},{9,8},{10,11... | collective-permute-start | bytes 196616 | tf_op jit(solution)/shard_map/ppermute | solution.py:763
  258.0 20.8 %collective-permute-start.21 = (bf16[1024,256]{1,0:T(8,128)(2,1)}, bf16[1024,256]{1,0:T(8,128)(2,1)}, u32[]{:S(2)}, u32[]{:S(2)}) collective-permute-start(bf16[1024,256]{1,0:T(8,128)(2,1)} %get-tuple-element.93), channel_id=1, source_target_pairs={{0,2},{1,3},{2,0},{3,1},{4,6},{5,7},{6,4},{7,5},{8,10},{9,11},{10,... | collective-permute-start | bytes 1572872 | tf_op jit(solution)/shard_map/ppermute | solution.py:763
  260.2 17.3 %collective-permute-start.18 = (bf16[1024,256]{1,0:T(8,128)(2,1)}, bf16[1024,256]{1,0:T(8,128)(2,1)}, u32[]{:S(2)}, u32[]{:S(2)}) collective-permute-start(bf16[1024,256]{1,0:T(8,128)(2,1)} %add_convert_fusion.1), channel_id=1, source_target_pairs={{0,2},{1,3},{2,0},{3,1},{4,6},{5,7},{6,4},{7,5},{8,10},{9,11},{10,... | collective-permute-start | bytes 1572872 | tf_op jit(solution)/shard_map/ppermute | solution.py:763
  261.5 17.4 %collective-permute-start.20 = (bf16[1024,256]{1,0:T(8,128)(2,1)}, bf16[1024,256]{1,0:T(8,128)(2,1)}, u32[]{:S(2)}, u32[]{:S(2)}) collective-permute-start(bf16[1024,256]{1,0:T(8,128)(2,1)} %add_convert_fusion), channel_id=1, source_target_pairs={{0,1},{1,0},{2,3},{3,2},{4,5},{5,4},{6,7},{7,6},{8,9},{9,8},{10,11... | collective-permute-start | bytes 1572872 | tf_op jit(solution)/shard_map/ppermute | solution.py:763
  268.9 225.3 %reduce-scatter.7.cloned.1.call-start = ((), (), s32[]{:S(2)}) async-start(), calls=%async_computation.9 | async-start | bytes 1179648 | tf_op jit(solution)/shard_map/reduce_scatter | solution.py:838
  285.0 17.2 %collective-permute-start.27 = (bf16[1024,256]{1,0:T(8,128)(2,1)S(1)}, bf16[1024,256]{1,0:T(8,128)(2,1)S(1)}, u32[]{:S(2)}, u32[]{:S(2)}) collective-permute-start(bf16[1024,256]{1,0:T(8,128)(2,1)S(1)} %get-tuple-element.191), channel_id=1, source_target_pairs={{0,1},{1,0},{2,3},{3,2},{4,5},{5,4},{6,7},{7,6},{8,9},{9,8},{10,11... | collective-permute-start | bytes 1572872 | tf_op jit(solution)/shard_map/ppermute | solution.py:763
  292.6 20.9 %collective-permute-start.30 = (bf16[1024,256]{1,0:T(8,128)(2,1)S(1)}, bf16[1024,256]{1,0:T(8,128)(2,1)S(1)}, u32[]{:S(2)}, u32[]{:S(2)}) collective-permute-start(bf16[1024,256]{1,0:T(8,128)(2,1)S(1)} %collective-permute-done.28.refs_3_), channel_id=1, source_target_pairs={{0,1},{1,0},{2,3},{3,2},{4,5},{5,4},{6,7},{7,6},{8,9},{9,8},{10,11... | collective-permute-start | bytes 1572872 | tf_op jit(solution)/shard_map/ppermute | solution.py:763
  293.4 20.9 %collective-permute-start.23 = (bf16[1024,256]{1,0:T(8,128)(2,1)S(1)}, bf16[1024,256]{1,0:T(8,128)(2,1)}, u32[]{:S(2)}, u32[]{:S(2)}) collective-permute-start(bf16[1024,256]{1,0:T(8,128)(2,1)S(1)} %collective-permute-done.22.refs_2_), channel_id=1, source_target_pairs={{0,2},{1,3},{2,0},{3,1},{4,6},{5,7},{6,4},{7,5},{8,10},{9,11},{10,... | collective-permute-start | bytes 1572872 | tf_op jit(solution)/shard_map/ppermute | solution.py:763
  329.1 171.6 %reduce-scatter.9.cloned.1.call-start = ((), (), s32[]{:S(2)}) async-start(), calls=%async_computation.10 | async-start | bytes 3538944 | tf_op jit(solution)/shard_map/reduce_scatter | solution.py:838
  329.9 173.0 %reduce-scatter.5.cloned.1.call-start = ((), (), s32[]{:S(2)}) async-start(), calls=%async_computation.8 | async-start | bytes 3833856 | tf_op jit(solution)/shard_map/reduce_scatter | solution.py:838
  333.5 71.1 %collective-permute-start.24 = (bf16[2048,256]{1,0:T(8,128)(2,1)}, bf16[2048,256]{1,0:T(8,128)(2,1)S(1)}, u32[]{:S(2)}, u32[]{:S(2)}) collective-permute-start(bf16[2048,256]{1,0:T(8,128)(2,1)} %get-tuple-element.178), channel_id=1, source_target_pairs={{0,1},{1,0},{2,3},{3,2},{4,5},{5,4},{6,7},{7,6},{8,9},{9,8},{10,11... | collective-permute-start | bytes 3145736 | tf_op jit(solution)/shard_map/ppermute | solution.py:763
  334.6 70.0 %collective-permute-start.26 = (bf16[2048,256]{1,0:T(8,128)(2,1)}, bf16[2048,256]{1,0:T(8,128)(2,1)}, u32[]{:S(2)}, u32[]{:S(2)}) collective-permute-start(bf16[2048,256]{1,0:T(8,128)(2,1)} %get-tuple-element.179), channel_id=1, source_target_pairs={{0,3},{1,2},{2,1},{3,0},{4,7},{5,6},{6,5},{7,4},{8,11},{9,10},{10,... | collective-permute-start | bytes 3145736 | tf_op jit(solution)/shard_map/ppermute | solution.py:763
  336.1 68.6 %collective-permute-start.25 = (bf16[2048,256]{1,0:T(8,128)(2,1)}, bf16[2048,256]{1,0:T(8,128)(2,1)}, u32[]{:S(2)}, u32[]{:S(2)}) collective-permute-start(bf16[2048,256]{1,0:T(8,128)(2,1)} %get-tuple-element.180), channel_id=1, source_target_pairs={{0,2},{1,3},{2,0},{3,1},{4,6},{5,7},{6,4},{7,5},{8,10},{9,11},{10,... | collective-permute-start | bytes 3145736 | tf_op jit(solution)/shard_map/ppermute | solution.py:763
  449.1 36.4 %collective-permute-start.34 = (bf16[2048,256]{1,0:T(8,128)(2,1)}, bf16[2048,256]{1,0:T(8,128)(2,1)}, u32[]{:S(2)}, u32[]{:S(2)}) collective-permute-start(bf16[2048,256]{1,0:T(8,128)(2,1)} %pad_maximum_fusion.1), channel_id=1, source_target_pairs={{0,2},{1,3},{2,0},{3,1},{4,6},{5,7},{6,4},{7,5},{8,10},{9,11},{10,... | collective-permute-start | bytes 3145736 | tf_op jit(solution)/shard_map/ppermute | solution.py:763
  451.7 33.8 %collective-permute-start.32 = (bf16[2048,256]{1,0:T(8,128)(2,1)}, bf16[2048,256]{1,0:T(8,128)(2,1)}, u32[]{:S(2)}, u32[]{:S(2)}) collective-permute-start(bf16[2048,256]{1,0:T(8,128)(2,1)} %pad_maximum_fusion), channel_id=1, source_target_pairs={{0,1},{1,0},{2,3},{3,2},{4,5},{5,4},{6,7},{7,6},{8,9},{9,8},{10,11... | collective-permute-start | bytes 3145736 | tf_op jit(solution)/shard_map/ppermute | solution.py:763
  473.5 19.5 %collective-permute-start.51 = (bf16[128,768]{1,0:T(8,128)(2,1)}, bf16[128,768]{1,0:T(8,128)(2,1)S(1)}, u32[]{:S(2)}, u32[]{:S(2)}) collective-permute-start(bf16[128,768]{1,0:T(8,128)(2,1)} %reduce-scatter.11.cloned.1.call-done), channel_id=1, source_target_pairs={{0,16},{16,0},{1,17},{17,1},{2,18},{18,2},{3,19},{19,3},{4,20},{20... | collective-permute-start | bytes 589832 | tf_op jit(solution)/shard_map/ppermute | solution.py:823
  (69 other events, 826.1 us)
Sparse Core Ops, SparseCore 0:
  11.3 42.9 all-gather.4
  56.5 20.9 all-gather.6
  79.3 51.7 all-gather.8
  133.2 52.3 all-gather.10
  269.0 33.4 reduce-scatter.10
  329.2 33.6 reduce-scatter.6
  365.2 39.6 reduce-scatter.8
  421.5 46.1 reduce-scatter.4
